TPU v7x, 32 devices: a whole 2x2x4 slice. The times are simulated.
32 devices in a mesh: frames: 8 (over z, x), rows: 4 (over y, core).
Axes of the slice: x: 2, y: 2, z: 4, core: 2. Of those that a mesh axis runs over, the one named last changes fastest.
Arguments:
- frames_in: bfloat16 [448, 197, 768], P(('frames', 'rows')), may hold values from -6 to 6
- cotangent: bfloat16 [448, 197, 768], P(('frames', 'rows')), may hold values from -6 to 6
- video_ids: int32 [448], P(('frames', 'rows')), may hold values from 0 to 511, as said below
- frame_device: int32 [448], P(('frames', 'rows')), may hold values from 0 to 7, as said below
- msg_weight: bfloat16 [768, 768], replicated, may hold values from -0.21875 to 0.21875
- msg_gain: float32 [768], replicated, may hold values from 0.5 to 1.5
- msg_qkv: bfloat16 [768, 2304], replicated, may hold values from -0.21875 to 0.21875
- msg_out: bfloat16 [768, 768], replicated, may hold values from -0.625 to 0.625
- attn_gain: float32 [768], replicated, may hold values from 0.5 to 1.5
- attn_qkv: bfloat16 [768, 2304], replicated, may hold values from -0.21875 to 0.21875
- attn_out: bfloat16 [768, 768], replicated, may hold values from -1.75 to 1.75
- mlp_gain: float32 [768], replicated, may hold values from 0.5 to 1.5
- up_weight: bfloat16 [768, 3072], replicated, may hold values from -0.21875 to 0.21875
- down_weight: bfloat16 [3072, 768], replicated, may hold values from -0.109375 to 0.109375
Outputs:
- output: bfloat16 [448, 197, 768], P(('frames', 'rows'))
- grad_in: bfloat16 [448, 197, 768], P(('frames', 'rows'))
- grad_msg_weight: float32 [768, 768], P('frames', 'rows')
- grad_msg_gain: float32 [768], P('frames')
- grad_msg_qkv: float32 [768, 2304], P('frames', 'rows')
- grad_msg_out: float32 [768, 768], P('frames', 'rows')
- grad_attn_gain: float32 [768], P('frames')
- grad_attn_qkv: float32 [768, 2304], P('frames', 'rows')
- grad_attn_out: float32 [768, 768], P('frames', 'rows')
- grad_mlp_gain: float32 [768], P('frames')
- grad_up_weight: float32 [768, 3072], P('frames', 'rows')
- grad_down_weight: float32 [3072, 768], P('frames', 'rows')
Inputs may be any that keep to these rules, and one draw needn't show every extreme that they name: `frame_device`: all frames of one video lie on devices with the same index along rows and name the same device. Of the 14 frames of one device at most 2 name the same device, and some device receives 2 from every device of its index along rows. `video_ids`: frames with one id form one video of at most 16 frames.
All inputs are finite; a program needn't handle non-finite values.
Results may differ from a plain program's by a relative error of at most 0.025.
Values may be sent and summed in bfloat16 or wider, within the bound.
No kernel may reach another device: no remote copies, remote signals or barrier semaphores. Data moves between devices by JAX's collectives and lax.ppermute only.
A program may use at most 256 MiB of HBM per device.

v0:
```python
import jax
import jax.numpy as jnp
from jax import lax
from jax.sharding import PartitionSpec as P

H = 12
HD = 64


EPS = 1e-05
FLOAT = jnp.float32
BFLOAT = jnp.bfloat16


def normalize(values):
    center = values - jnp.mean(values, axis=-1, keepdims=True)
    spread = jnp.mean(center * center, axis=-1, keepdims=True)
    scale_inv = lax.rsqrt(spread + EPS)
    return (center * scale_inv, scale_inv)


def norm_back(grad_out, gain_vec, normed, scale_inv):
    grad_normed = grad_out * gain_vec
    grad_gain = jnp.sum((grad_out * normed).reshape(-1, normed.shape[-1]), axis=0)
    grad_input = scale_inv * (
        grad_normed
        - jnp.mean(grad_normed, axis=-1, keepdims=True)
        - normed * jnp.mean(grad_normed * normed, axis=-1, keepdims=True)
    )
    return (grad_input, grad_gain)


def split_heads(proj, token, width):
    count = proj.shape[0]
    frame_len = proj.shape[1]
    key_rows = jnp.concatenate(
        [proj[..., width : 2 * width], token[:, None, :width]], axis=1
    ).reshape(count, frame_len + 1, H, HD)
    value_rows = jnp.concatenate([proj[..., 2 * width :], token[:, None, width:]], axis=1).reshape(
        count, frame_len + 1, H, HD
    )
    query_rows = proj[..., :width].reshape(count, frame_len, H, HD)
    return (query_rows, key_rows, value_rows)


def per_device(
    frames_in,
    cotangent,
    video_ids,
    frame_device,
    msg_weight,
    msg_gain,
    msg_qkv,
    msg_out,
    attn_gain,
    attn_qkv,
    attn_out,
    mlp_gain,
    up_weight,
    down_weight,
):
    local_frames, frame_len, width = frames_in.shape
    owners = lax.axis_size("frames")
    capacity = -(-local_frames // owners)
    slot_count = owners * capacity
    pair_count = local_frames // 2
    class_rows = frames_in[:, 0, :]
    frame_pos = jnp.arange(local_frames)
    earlier = (frame_device[:, None] == frame_device[None, :]) & (
        frame_pos[None, :] < frame_pos[:, None]
    )
    slot_index = frame_device * capacity + jnp.sum(earlier.astype(jnp.int32), axis=1)
    placing = jnp.arange(slot_count)[:, None] == slot_index[None, :]
    placing_bf = placing.astype(BFLOAT)
    message_start = jnp.dot(class_rows, msg_weight, preferred_element_type=FLOAT).astype(BFLOAT)
    outgoing = jnp.dot(placing_bf, message_start, preferred_element_type=FLOAT).astype(BFLOAT)
    outgoing_ids = jnp.sum(jnp.where(placing, video_ids[None, :] + 1, 0), axis=1) - 1
    arrived, arrived_ids = (
        lax.all_to_all(
            outgoing.reshape(owners, capacity, width),
            "frames",
            split_axis=0,
            concat_axis=0,
            tiled=True,
        ),
        lax.all_to_all(
            outgoing_ids.reshape(owners, capacity),
            "frames",
            split_axis=0,
            concat_axis=0,
            tiled=True,
        ),
    )
    arrived = arrived.reshape(slot_count, width)
    arrived_ids = arrived_ids.reshape(slot_count)
    msg_input = arrived.astype(FLOAT)
    msg_norm, msg_scale = normalize(msg_input)
    msg_hidden = (msg_norm * msg_gain).astype(BFLOAT)
    msg_proj = jnp.dot(msg_hidden, msg_qkv, preferred_element_type=FLOAT).astype(BFLOAT)
    msg_query = msg_proj[:, :width].reshape(slot_count, H, HD)
    msg_key = msg_proj[:, width : 2 * width].reshape(slot_count, H, HD)
    msg_value = msg_proj[:, 2 * width :].reshape(slot_count, H, HD)
    slot_pos = jnp.arange(slot_count)
    visible = (arrived_ids[:, None] == arrived_ids[None, :]) & (arrived_ids[:, None] >= 0) | (
        slot_pos[:, None] == slot_pos[None, :]
    )
    msg_scores = (
        jnp.einsum("ihd,jhd->hij", msg_query, msg_key, preferred_element_type=FLOAT) * 0.125
    )
    msg_scores = jnp.where(visible[None], msg_scores, -1e30)
    msg_prob = jax.nn.softmax(msg_scores, axis=-1)
    msg_prob_bf = msg_prob.astype(BFLOAT)
    msg_mixed = (
        jnp.einsum("hij,jhd->ihd", msg_prob_bf, msg_value, preferred_element_type=FLOAT)
        .astype(BFLOAT)
        .reshape(slot_count, width)
    )
    message = (msg_input + jnp.dot(msg_mixed, msg_out, preferred_element_type=FLOAT)).astype(BFLOAT)
    returned = lax.all_to_all(
        message.reshape(owners, capacity, width), "frames", split_axis=0, concat_axis=0, tiled=True
    ).reshape(slot_count, width)
    message_local = jnp.einsum(
        "sf,sd->fd", placing_bf, returned, preferred_element_type=FLOAT
    ).astype(BFLOAT)
    frames_f = frames_in.astype(FLOAT)
    first_norm, first_scale = normalize(frames_f)
    first_hidden = (first_norm * attn_gain).astype(BFLOAT)
    frame_proj = jnp.einsum(
        "frd,de->fre", first_hidden, attn_qkv, preferred_element_type=FLOAT
    ).astype(BFLOAT)
    token_norm, token_scale = normalize(message_local.astype(FLOAT))
    token_hidden = (token_norm * attn_gain).astype(BFLOAT)
    token_kv = jnp.dot(token_hidden, attn_qkv[:, width:], preferred_element_type=FLOAT).astype(
        BFLOAT
    )
    proj_blocks = frame_proj.reshape(pair_count, 2, frame_len, 3 * width)
    token_blocks = token_kv.reshape(pair_count, 2, 2 * width)

    def attend_forward(block):
        proj, token = block
        query_rows, key_rows, value_rows = split_heads(proj, token, width)
        scores = (
            jnp.einsum("fqhd,fkhd->fhqk", query_rows, key_rows, preferred_element_type=FLOAT)
            * 0.125
        )
        highest = jnp.max(scores, axis=-1, keepdims=True)
        expo = jnp.exp(scores - highest)
        totals = jnp.sum(expo, axis=-1, keepdims=True)
        log_total = highest + jnp.log(totals)
        probs_bf = (expo / totals).astype(BFLOAT)
        mixed = jnp.einsum(
            "fhqk,fkhd->fqhd", probs_bf, value_rows, preferred_element_type=FLOAT
        ).astype(BFLOAT)
        return (mixed.reshape(proj.shape[0], frame_len, width), log_total)

    mixed_blocks, lse_blocks = lax.map(attend_forward, (proj_blocks, token_blocks))
    mixed_heads = mixed_blocks.reshape(local_frames, frame_len, width)
    residual = frames_f + jnp.einsum(
        "frd,de->fre", mixed_heads, attn_out, preferred_element_type=FLOAT
    )
    second_norm, second_scale = normalize(residual)
    second_hidden = (second_norm * mlp_gain).astype(BFLOAT)
    up_part = jnp.einsum("frd,de->fre", second_hidden, up_weight, preferred_element_type=FLOAT)
    sigma = jax.nn.sigmoid(1.702 * up_part)
    activated = (up_part * sigma).astype(BFLOAT)
    output = (
        residual + jnp.einsum("fre,ed->frd", activated, down_weight, preferred_element_type=FLOAT)
    ).astype(BFLOAT)
    grad_down = jnp.einsum("fre,frd->ed", activated, cotangent, preferred_element_type=FLOAT)
    grad_act = jnp.einsum("frd,ed->fre", cotangent, down_weight, preferred_element_type=FLOAT)
    grad_up_part = (grad_act * (sigma + 1.702 * up_part * sigma * (1.0 - sigma))).astype(BFLOAT)
    grad_up = jnp.einsum("frd,fre->de", second_hidden, grad_up_part, preferred_element_type=FLOAT)
    grad_second = jnp.einsum("fre,de->frd", grad_up_part, up_weight, preferred_element_type=FLOAT)
    back_second, grad_mlp_gain = norm_back(grad_second, mlp_gain, second_norm, second_scale)
    grad_residual = cotangent.astype(FLOAT) + back_second
    grad_branch = grad_residual.astype(BFLOAT)
    grad_attn_out = jnp.einsum(
        "frd,fre->de", mixed_heads, grad_branch, preferred_element_type=FLOAT
    )
    grad_mixed = jnp.einsum(
        "fre,de->frd", grad_branch, attn_out, preferred_element_type=FLOAT
    ).astype(BFLOAT)
    grad_mix_blocks = grad_mixed.reshape(pair_count, 2, frame_len, width)

    def attend_backward(block):
        proj, token, log_total, grad_mix = block
        count = proj.shape[0]
        query_rows, key_rows, value_rows = split_heads(proj, token, width)
        scores = (
            jnp.einsum("fqhd,fkhd->fhqk", query_rows, key_rows, preferred_element_type=FLOAT)
            * 0.125
        )
        probs = jnp.exp(scores - log_total)
        probs_bf = probs.astype(BFLOAT)
        grad_heads = grad_mix.reshape(count, frame_len, H, HD)
        grad_probs = jnp.einsum(
            "fqhd,fkhd->fhqk", grad_heads, value_rows, preferred_element_type=FLOAT
        )
        grad_scores = (
            probs * (grad_probs - jnp.sum(probs * grad_probs, axis=-1, keepdims=True))
        ).astype(BFLOAT)
        grad_query = (
            jnp.einsum("fhqk,fkhd->fqhd", grad_scores, key_rows, preferred_element_type=FLOAT)
            * 0.125
        )
        grad_key = (
            jnp.einsum("fhqk,fqhd->fkhd", grad_scores, query_rows, preferred_element_type=FLOAT)
            * 0.125
        ).reshape(count, frame_len + 1, width)
        grad_value = jnp.einsum(
            "fhqk,fqhd->fkhd", probs_bf, grad_heads, preferred_element_type=FLOAT
        ).reshape(count, frame_len + 1, width)
        frame_grad = jnp.concatenate(
            [
                grad_query.reshape(count, frame_len, width),
                grad_key[:, :frame_len],
                grad_value[:, :frame_len],
            ],
            axis=-1,
        ).astype(BFLOAT)
        token_grad = jnp.concatenate(
            [grad_key[:, frame_len], grad_value[:, frame_len]], axis=-1
        ).astype(BFLOAT)
        return (frame_grad, token_grad)

    proj_grad_blocks, token_grad_blocks = lax.map(
        attend_backward, (proj_blocks, token_blocks, lse_blocks, grad_mix_blocks)
    )
    grad_proj = proj_grad_blocks.reshape(local_frames, frame_len, 3 * width)
    token_grad_bf = token_grad_blocks.reshape(local_frames, 2 * width)
    grad_qkv = jnp.einsum("frd,fre->de", first_hidden, grad_proj, preferred_element_type=FLOAT)
    grad_first = jnp.einsum("fre,de->frd", grad_proj, attn_qkv, preferred_element_type=FLOAT)
    back_first, grad_attn_gain = norm_back(grad_first, attn_gain, first_norm, first_scale)
    grad_frames = grad_residual + back_first
    grad_qkv = grad_qkv.at[:, width:].add(
        jnp.einsum("fd,fe->de", token_hidden, token_grad_bf, preferred_element_type=FLOAT)
    )
    grad_token = jnp.einsum(
        "fe,de->fd", token_grad_bf, attn_qkv[:, width:], preferred_element_type=FLOAT
    )
    back_token, token_gain_grad = norm_back(grad_token, attn_gain, token_norm, token_scale)
    grad_attn_gain = grad_attn_gain + token_gain_grad
    outgoing_grad = jnp.dot(
        placing_bf, back_token.astype(BFLOAT), preferred_element_type=FLOAT
    ).astype(BFLOAT)
    message_grad = lax.all_to_all(
        outgoing_grad.reshape(owners, capacity, width),
        "frames",
        split_axis=0,
        concat_axis=0,
        tiled=True,
    ).reshape(slot_count, width)
    grad_msg_out = jnp.einsum("id,ie->de", msg_mixed, message_grad, preferred_element_type=FLOAT)
    grad_msg_mixed = (
        jnp.einsum("ie,de->id", message_grad, msg_out, preferred_element_type=FLOAT)
        .astype(BFLOAT)
        .reshape(slot_count, H, HD)
    )
    msg_grad_prob = jnp.einsum(
        "ihd,jhd->hij", grad_msg_mixed, msg_value, preferred_element_type=FLOAT
    )
    msg_grad_scores = (
        msg_prob * (msg_grad_prob - jnp.sum(msg_prob * msg_grad_prob, axis=-1, keepdims=True))
    ).astype(BFLOAT)
    grad_msg_query = (
        jnp.einsum("hij,jhd->ihd", msg_grad_scores, msg_key, preferred_element_type=FLOAT) * 0.125
    )
    grad_msg_key = (
        jnp.einsum("hij,ihd->jhd", msg_grad_scores, msg_query, preferred_element_type=FLOAT) * 0.125
    )
    grad_msg_value = jnp.einsum(
        "hij,ihd->jhd", msg_prob_bf, grad_msg_mixed, preferred_element_type=FLOAT
    )
    grad_msg_proj = jnp.concatenate(
        [
            grad_msg_query.reshape(slot_count, width),
            grad_msg_key.reshape(slot_count, width),
            grad_msg_value.reshape(slot_count, width),
        ],
        axis=-1,
    ).astype(BFLOAT)
    grad_msg_qkv = jnp.einsum("id,ie->de", msg_hidden, grad_msg_proj, preferred_element_type=FLOAT)
    grad_msg_hidden = jnp.einsum("ie,de->id", grad_msg_proj, msg_qkv, preferred_element_type=FLOAT)
    back_msg, grad_msg_gain = norm_back(grad_msg_hidden, msg_gain, msg_norm, msg_scale)
    start_grad = (message_grad.astype(FLOAT) + back_msg).astype(BFLOAT)
    start_back = lax.all_to_all(
        start_grad.reshape(owners, capacity, width),
        "frames",
        split_axis=0,
        concat_axis=0,
        tiled=True,
    ).reshape(slot_count, width)
    start_local = jnp.einsum(
        "sf,sd->fd", placing_bf, start_back, preferred_element_type=FLOAT
    ).astype(BFLOAT)
    grad_msg_weight = jnp.einsum("fd,fe->de", class_rows, start_local, preferred_element_type=FLOAT)
    class_grad = jnp.einsum("fe,de->fd", start_local, msg_weight, preferred_element_type=FLOAT)
    grad_frames = grad_frames.at[:, 0, :].add(class_grad)
    partial_sums = (
        lax.psum_scatter(
            grad_msg_weight.astype(jnp.bfloat16), "rows", scatter_dimension=1, tiled=True
        ).astype(jnp.float32),
        lax.psum_scatter(
            grad_msg_qkv.astype(jnp.bfloat16), "rows", scatter_dimension=1, tiled=True
        ).astype(jnp.float32),
        lax.psum_scatter(
            grad_msg_out.astype(jnp.bfloat16), "rows", scatter_dimension=1, tiled=True
        ).astype(jnp.float32),
        lax.psum_scatter(
            grad_qkv.astype(jnp.bfloat16), "rows", scatter_dimension=1, tiled=True
        ).astype(jnp.float32),
        lax.psum_scatter(
            grad_attn_out.astype(jnp.bfloat16), "rows", scatter_dimension=1, tiled=True
        ).astype(jnp.float32),
        lax.psum_scatter(
            grad_up.astype(jnp.bfloat16), "rows", scatter_dimension=1, tiled=True
        ).astype(jnp.float32),
        lax.psum_scatter(
            grad_down.astype(jnp.bfloat16), "rows", scatter_dimension=1, tiled=True
        ).astype(jnp.float32),
    )
    gain_sums = lax.psum((grad_msg_gain, grad_attn_gain, grad_mlp_gain), "rows")
    summed = (
        lax.psum_scatter(partial_sums[0], "frames", scatter_dimension=0, tiled=True),
        lax.psum_scatter(partial_sums[1], "frames", scatter_dimension=0, tiled=True),
        lax.psum_scatter(partial_sums[2], "frames", scatter_dimension=0, tiled=True),
        lax.psum_scatter(partial_sums[3], "frames", scatter_dimension=0, tiled=True),
        lax.psum_scatter(partial_sums[4], "frames", scatter_dimension=0, tiled=True),
        lax.psum_scatter(partial_sums[5], "frames", scatter_dimension=0, tiled=True),
        lax.psum_scatter(partial_sums[6], "frames", scatter_dimension=0, tiled=True),
        lax.psum_scatter(gain_sums[0], "frames", scatter_dimension=0, tiled=True),
        lax.psum_scatter(gain_sums[1], "frames", scatter_dimension=0, tiled=True),
        lax.psum_scatter(gain_sums[2], "frames", scatter_dimension=0, tiled=True),
    )
    matrices = (summed[0], summed[1], summed[2], summed[3], summed[4], summed[5], summed[6])
    gains = (summed[7], summed[8], summed[9])
    return (
        output,
        grad_frames.astype(BFLOAT),
        matrices[0],
        gains[0],
        matrices[1],
        matrices[2],
        gains[1],
        matrices[3],
        matrices[4],
        gains[2],
        matrices[5],
        matrices[6],
    )


def solution(mesh):
    return jax.shard_map(
        per_device,
        mesh=mesh,
        in_specs=(
            P(("frames", "rows"), None, None),
            P(("frames", "rows"), None, None),
            P(("frames", "rows")),
            P(("frames", "rows")),
            P(),
            P(),
            P(),
            P(),
            P(),
            P(),
            P(),
            P(),
            P(),
            P(),
        ),
        out_specs=(
            P(("frames", "rows"), None, None),
            P(("frames", "rows"), None, None),
            P("frames", "rows"),
            P("frames"),
            P("frames", "rows"),
            P("frames", "rows"),
            P("frames"),
            P("frames", "rows"),
            P("frames", "rows"),
            P("frames"),
            P("frames", "rows"),
            P("frames", "rows"),
        ),
        check_vma=False,
    )
```

profile of v0, /device:TPU:0, one launch (start us, length us, event | category | flops | bytes accessed | tf_op | source)
XLA Modules:
  0.0 1411.3 jit_solution(15890021417594889096)
XLA Ops:
  9.8 7.3 all-to-all-start.1
  29.5 6.0 all-to-all-start
  68.2 16.5 %convolution_convert_fusion = bf16[14,197,2304]{2,1,0:T(8,128)(2,1)} fusion(bf16[768,2304]{1,0:T(8,128)(2,1)} %param.31, bf16[14,197,768]{2,1,0:T(8,128)(2,1)} %param.22, f32[768]{0:T(1024)S(1)} %copy-done.25, f32[14,197]{1,0:T(8,128)} %add_rsqrt_fusion.1, f32[14,197]{1,0:T(8,128)} %copy-done.20), kind=kOutput, calls=%fused_computation.61 | convolution fusion | flops 9777352704 | bytes 20509232 | tf_op jit(solution)/shard_map/frd,de->fre/dot_general | solution.py:128
  84.7 19.2 %copy.127 = bf16[7,2,197,2304]{2,3,1,0:T(8,128)(2,1)} copy(bf16[7,2,197,2304]{3,2,1,0:T(8,128)(2,1)} %bitcast.215) | data formatting | bytes 25417728 | tf_op jit(solution)/shard_map/while | solution.py:156
  111.7 139.2 %while.26 = (s32[]{:T(128)}, bf16[7,2,197,768]{2,3,1,0:T(8,128)(2,1)}, f32[7,2,12,197,1]{3,2,1,4,0:T(8,128)}, bf16[7,2,197,2304]{2,3,1,0:T(8,128)(2,1)}, bf16[7,2,1536]{2,1,0:T(2,128)(2,1)}, /*index=5*/s32[]{:T(128)}) while((s32[]{:T(128)}, bf16[7,2,197,768]{2,3,1,0:T(8,128)(2,1)}, f32[7,2,12,197,1]{3,2,1,4,0:T(8,128)}, ...), condition=%wide.region_13.14_spmd, body=%wide.region_10.13_spmd.sunk | while | flops 250809056 | bytes 37647232 | solution.py:156
  250.9 8.5 fusion.110
  264.1 27.3 %multiply_convert_fusion.4 = (bf16[14,197,3072]{2,1,0:T(8,128)(2,1)}, f32[14,197,3072]{2,1,0:T(8,128)}) fusion(bf16[768,3072]{1,0:T(8,128)(2,1)} %param.34, f32[14,197,768]{2,1,0:T(8,128)} %copy-done.8, f32[768]{0:T(1024)S(1)} %copy-done.38, f32[14,197]{1,0:T(8,128)S(1)} %add_rsqrt_fusion, f32[14,197]{1,0:T(8,128)S(1)} %broadcast_multiply_fusion.4), kind=kOutput, calls=%fused_computation.50 | convolution fusion | flops 13073184768 | bytes 64051760 | tf_op jit(solution)/shard_map/frd,de->fre/dot_general | solution.py:163
  291.4 32.5 %multiply_convert_fusion.3 = bf16[14,197,3072]{2,1,0:T(8,128)(2,1)} fusion(f32[14,197,3072]{2,1,0:T(8,128)} %get-tuple-element.270, bf16[14,197,768]{2,1,0:T(8,128)(2,1)} %param.23, bf16[3072,768]{1,0:T(8,128)(2,1)} %param.35), kind=kOutput, calls=%fused_computation.49 | convolution fusion | flops 13098602496 | bytes 59790336 | tf_op jit(solution)/shard_map/frd,ed->fre/dot_general | solution.py:170
  323.9 24.4 %multiply_reduce_fusion.2 = (f32[768]{0:T(1024)}, f32[14,197]{1,0:T(8,128)}, f32[14,197]{1,0:T(8,128)}, f32[14,197,768]{2,1,0:T(8,128)}) fusion(f32[14,197,768]{2,1,0:T(8,128)} %copy-done.8, f32[14,197]{1,0:T(8,128)} %copy-done.24, f32[14,197]{1,0:T(8,128)S(1)} %broadcast_multiply_fusion.4, f32[768]{0:T(1024)} %param.33, ...), kind=kOutput, calls=%fused_computation.71 | convolution fusion | flops 13030813696 | bytes 38659168 | tf_op jit(solution)/shard_map/fre,de->frd/dot_general | solution.py:173
  349.7 8.7 multiply_add_fusion
  365.0 5.9 bitcast_convert_fusion.2
  371.0 273.2 %while.27 = (s32[]{:T(128)}, bf16[7,2,197,2304]{2,3,1,0:T(8,128)(2,1)}, bf16[7,2,1536]{2,1,0:T(2,128)(2,1)}, bf16[7,2,197,2304]{2,3,1,0:T(8,128)(2,1)}, bf16[7,2...) while((s32[]{:T(128)}, ...), condition=%wide.region_20.21_spmd, body=%wide.region_18.20_spmd.sunk | while | flops 620987200 | bytes 75166272 | solution.py:226
  651.7 12.6 all_to_all.26
  693.9 10.6 all_to_all.27
  709.9 22.1 %convolution_bitcast_fusion = f32[768,2304]{1,0:T(8,128)S(1)} fusion(bf16[14,197,2304]{1,2,0:T(8,128)(2,1)} %bitcast.220, bf16[14,197,768]{2,1,0:T(8,128)(2,1)} %param.22, f32[768]{0:T(1024)S(1)} %copy-done.26, f32[14,197]{1,0:T(8,128)} %add_rsqrt_fusion.1, f32[14,197]{1,0:T(8,128)} %copy-done.20), kind=kOutput, calls=%fused_computation.80 | convolution fusion | flops 9770997760 | bytes 24048176 | tf_op jit(solution)/shard_map/frd,fre->de/dot_general | solution.py:231
  744.9 23.5 %bitcast_convert_fusion.1 = bf16[768,3072]{1,0:T(8,128)(2,1)} fusion(bf16[14,197,3072]{2,1,0:T(8,128)(2,1)} %multiply_convert_fusion.3, f32[14,197,768]{2,1,0:T(8,128)} %copy-done.8, f32[768]{0:T(1024)S(1)} %copy-done.39, f32[14,197]{1,0:T(8,128)} %copy-done.24, f32[14,197]{1,0:T(8,128)} %copy-done.22), kind=kOutput, calls=%fused_computation.63 | convolution fusion | flops 13024708608 | bytes 30161456 | tf_op jit(solution)/shard_map/frd,fre->de/dot_general | solution.py:172
  768.5 19.4 %bitcast_convert_fusion = bf16[3072,768]{0,1:T(8,128)(2,1)} fusion(bf16[14,197,3072]{2,1,0:T(8,128)(2,1)} %get-tuple-element.269, bf16[14,197,768]{2,1,0:T(8,128)(2,1)} %param.23), kind=kOutput, calls=%fused_computation.62 | convolution fusion | flops 13016236032 | bytes 25900032 | tf_op jit(solution)/shard_map/fre,frd->ed/dot_general | solution.py:169
  799.3 22.9 %reduce-scatter.27.cloned.1.call-done = bf16[768,576]{0,1:T(8,128)(2,1)} async-done(((bf16[768,2304]{0,1:T(8,128)(2,1)}), bf16[768,576]{0,1:T(8,128)(2,1)}) %reduce-scatter.27.cloned.1.call-update) | async-done | bytes 884752 | tf_op jit(solution)/shard_map/reduce_scatter | solution.py:303
  824.8 47.9 %reduce-scatter.35.cloned.1.call-done = bf16[768,768]{1,0:T(8,128)(2,1)} async-done(((bf16[768,3072]{1,0:T(8,128)(2,1)}), bf16[768,768]{1,0:T(8,128)(2,1)}) %reduce-scatter.35.cloned.1.call-update) | async-done | bytes 1179664 | tf_op jit(solution)/shard_map/reduce_scatter | solution.py:315
  877.5 24.9 %fusion.42 = (f32[768]{0:T(1024)}, f32[14,197]{1,0:T(8,128)S(1)}, f32[14,197]{1,0:T(8,128)}, f32[14,197,768]{2,1,0:T(8,128)}) fusion(bf16[14,197,768]{2,1,0:T(8,128)(2,1)} %param.22, f32[14,197]{1,0:T(8,128)} %add_rsqrt_fusion.1, f32[14,197]{1,0:T(8,128)S(1)} %copy-done.21, f32[768]{0:T(1024)} %param.30, bf16[14,197,2304]{1,2,0:T(8,128)(2,1)} %bitcast.221, ...), kind=kOutput, calls=%fused_computation.69 | convolution fusion | flops 9779462144 | bytes 29006944 | tf_op jit(solution)/shard_map/fre,de->frd/dot_general | solution.py:232
  903.0 20.0 %reduce-scatter.39.cloned.1.call-done = bf16[3072,192]{0,1:T(8,128)(2,1)} async-done(((bf16[3072,768]{0,1:T(8,128)(2,1)}), bf16[3072,192]{0,1:T(8,128)(2,1)}) %reduce-scatter.39.cloned.1.call-update) | async-done | bytes 1179664 | tf_op jit(solution)/shard_map/reduce_scatter | solution.py:318
  928.1 12.2 fusion.41
  940.4 21.6 %add_convert_fusion = bf16[14,197,768]{2,1,0:T(8,128)(2,1)} fusion(f32[14,197,768]{2,1,0:T(8,128)} %copy-done.8, bf16[14,197,3072]{2,1,0:T(8,128)(2,1)} %get-tuple-element.269, bf16[3072,768]{1,0:T(8,128)(2,1)} %param.35), kind=kOutput, calls=%fused_computation.74 | convolution fusion | flops 13018112000 | bytes 34372608 | tf_op jit(solution)/shard_map/fre,ed->frd/dot_general | solution.py:167
  962.0 37.1 %all-reduce.3 = (f32[768]{0:T(1024)}, f32[768]{0:T(1024)}, f32[768]{0:T(1024)S(1)}) all-reduce(f32[768]{0:T(1024)S(1)} %copy-done.32, f32[768]{0:T(1024)S(1)} %copy-done.33, f32[768]{0:T(1024)S(1)} %copy-done.40), channel_id=4, replica_groups=mesh['frames'=8,'rows'=4] {'frames'}, use_global_device_ids=true, to_apply=%region_32.33.clone | all-reduce | flops 2304 | bytes 18432
  1000.7 6.4 all-reduce.4
  1012.4 5.9 convert_element_type.214
  1018.3 36.8 %reduce-scatter.47.cloned.1.call-done = f32[96,192]{1,0:T(8,128)} async-done(((f32[768,192]{1,0:T(8,128)}), f32[96,192]{1,0:T(8,128)}) %reduce-scatter.47.cloned.1.call-update) | async-done | bytes 73744
  1055.1 65.5 %reduce-scatter.43.cloned.1.call-done = f32[96,192]{1,0:T(8,128)} async-done(((f32[768,192]{1,0:T(8,128)}), f32[96,192]{1,0:T(8,128)}) %reduce-scatter.43.cloned.1.call-update) | async-done | bytes 73744
  1120.7 69.9 %reduce-scatter.31.cloned.1.call-done = f32[96,576]{1,0:T(8,128)} async-done(((f32[768,576]{1,0:T(8,128)}), f32[96,576]{1,0:T(8,128)}) %reduce-scatter.31.cloned.1.call-update) | async-done | bytes 221200 | tf_op jit(solution)/shard_map/reduce_scatter | solution.py:327
  1190.5 70.0 %reduce-scatter.45.cloned.1.call-done = f32[96,576]{1,0:T(8,128)} async-done(((f32[768,576]{1,0:T(8,128)}), f32[96,576]{1,0:T(8,128)}) %reduce-scatter.45.cloned.1.call-update) | async-done | bytes 221200
  1260.5 72.1 %reduce-scatter.37.cloned.1.call-done = f32[96,768]{1,0:T(8,128)} async-done(((f32[768,768]{1,0:T(8,128)}), f32[96,768]{1,0:T(8,128)}) %reduce-scatter.37.cloned.1.call-update) | async-done | bytes 294928 | tf_op jit(solution)/shard_map/reduce_scatter | solution.py:329
  1332.6 72.0 %reduce-scatter.41.cloned.1.call-done = f32[384,192]{0,1:T(8,128)} async-done(((f32[3072,192]{0,1:T(8,128)}), f32[384,192]{0,1:T(8,128)}) %reduce-scatter.41.cloned.1.call-update) | async-done | bytes 294928 | tf_op jit(solution)/shard_map/reduce_scatter | solution.py:330
  (608 shorter events, 564.6 us)
Async XLA Ops:
  7.2 39.6 %copy-start = (bf16[768,2304]{1,0:T(8,128)(2,1)S(1)}, bf16[768,2304]{1,0:T(8,128)(2,1)}, u32[]{:S(2)}) copy-start(bf16[768,2304]{1,0:T(8,128)(2,1)} %param.28) | copy-start | bytes 10616836
  9.8 19.7 %all-to-all-start.1 = ((s32[8,1,2]{2,1,0:T(1,128)}), s32[8,1,2]{2,1,0:T(1,128)S(1)}, u32[]{:S(2)}, u32[]{:S(2)}) async-start(s32[8,1,2]{2,1,0:T(1,128)} %bitcast.30), calls=%async_computation.1 | async-start | bytes 8192 | tf_op jit(solution)/shard_map/all_to_all | solution.py:86
  18.7 28.1 %copy-start.17 = (f32[768]{0:T(1024)S(1)}, f32[768]{0:T(1024)}, u32[]{:S(2)}) copy-start(f32[768]{0:T(1024)} %param.27) | copy-start | bytes 9220
  24.4 43.7 %copy-start.25 = (f32[768]{0:T(1024)S(1)}, f32[768]{0:T(1024)}, u32[]{:S(2)}) copy-start(f32[768]{0:T(1024)} %param.30) | copy-start | bytes 9220
  29.5 12.7 all-to-all-start
  54.2 30.5 %copy-start.27 = (f32[12,16]{1,0:T(8,128)}, f32[12,16]{1,0:T(8,128)S(1)}, u32[]{:S(2)}) copy-start(f32[12,16]{1,0:T(8,128)S(1)} %get-tuple-element.263) | copy-start | bytes 2308
  64.0 39.9 %all-to-all-start.2 = ((bf16[8,2,768]{2,1,0:T(2,128)(2,1)}), bf16[8,2,768]{2,1,0:T(2,128)(2,1)}, u32[]{:S(2)}, u32[]{:S(2)}) async-start(bf16[8,2,768]{2,1,0:T(2,128)(2,1)} %reshape.492), calls=%async_computation.2 | async-start | bytes 49152 | tf_op jit(solution)/shard_map/all_to_all | solution.py:119
  67.9 720.0 %reduce-scatter.33.cloned.1.call-start = ((), (), s32[]{:S(2)}) async-start(), calls=%async_computation.23 | async-start | bytes 1474560 | tf_op jit(solution)/shard_map/reduce_scatter | solution.py:312
  259.4 90.3 %copy-start.22 = (f32[14,197]{1,0:T(8,128)}, f32[14,197]{1,0:T(8,128)S(1)}, u32[]{:S(2)}) copy-start(f32[14,197]{1,0:T(8,128)S(1)} %broadcast_multiply_fusion.4) | copy-start | bytes 33100
  264.1 27.3 %copy-start.24 = (f32[14,197]{1,0:T(8,128)}, f32[14,197]{1,0:T(8,128)S(1)}, u32[]{:S(2)}) copy-start(f32[14,197]{1,0:T(8,128)S(1)} %add_rsqrt_fusion) | copy-start | bytes 33100
  370.9 419.2 %reduce-scatter.29.cloned.1.call-start = ((), (), s32[]{:S(2)}) async-start(), calls=%async_computation.21 | async-start | bytes 1474560 | tf_op jit(solution)/shard_map/reduce_scatter | solution.py:306
  371.0 274.7 %copy-start.26 = (f32[768]{0:T(1024)S(1)}, f32[768]{0:T(1024)}, u32[]{:S(2)}) copy-start(f32[768]{0:T(1024)} %param.30) | copy-start | bytes 9220
  644.2 44.4 %copy-start.18 = (f32[768]{0:T(1024)S(1)}, f32[768]{0:T(1024)}, u32[]{:S(2)}) copy-start(f32[768]{0:T(1024)} %param.27) | copy-start | bytes 9220
  644.2 44.4 %copy-start.29 = (f32[16]{0:T(128)S(1)}, f32[16]{0:T(128)}, u32[]{:S(2)}) copy-start(f32[16]{0:T(128)} %copy-done.28) | copy-start | bytes 196
  644.2 44.4 %copy-start.31 = (f32[16]{0:T(128)S(1)}, f32[16]{0:T(128)}, u32[]{:S(2)}) copy-start(f32[16]{0:T(128)} %copy-done.30) | copy-start | bytes 196
  674.4 117.8 %reduce-scatter.25.cloned.1.call-start = ((), (), s32[]{:S(2)}) async-start(), calls=%async_computation.19 | async-start | bytes 1474560 | tf_op jit(solution)/shard_map/reduce_scatter | solution.py:300
  709.8 84.6 %reduce-scatter.49.cloned.1.call-start = ((), (), s32[]{:S(2)}) async-start(), calls=%async_computation.31 | async-start | bytes 4423680
  709.8 22.1 %copy-start.14 = (f32[14,768]{1,0:T(8,128)S(1)}, f32[14,768]{1,0:T(8,128)}, u32[]{:S(2)}) copy-start(f32[14,768]{1,0:T(8,128)} %copy-done.13) | copy-start | bytes 129028
  709.9 22.1 %copy-start.19 = (bf16[14,1536]{1,0:T(8,128)(2,1)S(1)}, bf16[14,1536]{1,0:T(8,128)(2,1)}, u32[]{:S(2)}) copy-start(bf16[14,1536]{1,0:T(8,128)(2,1)} %reshape.498) | copy-start | bytes 129028
  709.9 22.1 %copy-start.37 = (f32[14]{0:T(128)S(1)}, f32[14]{0:T(128)}, u32[]{:S(2)}) copy-start(f32[14]{0:T(128)} %copy-done.36) | copy-start | bytes 172
  709.9 22.1 %copy-start.42 = (f32[14]{0:T(128)S(1)}, f32[14]{0:T(128)}, u32[]{:S(2)}) copy-start(f32[14]{0:T(128)} %copy-done.41) | copy-start | bytes 172
  740.9 81.3 %reduce-scatter.27.cloned.1.call-start = ((), (), s32[]{:S(2)}) async-start(), calls=%async_computation.20 | async-start | bytes 4423680 | tf_op jit(solution)/shard_map/reduce_scatter | solution.py:303
  744.9 127.8 %reduce-scatter.35.cloned.1.call-start = ((), (), s32[]{:S(2)}) async-start(), calls=%async_computation.24 | async-start | bytes 5898240 | tf_op jit(solution)/shard_map/reduce_scatter | solution.py:315
  768.4 154.6 %reduce-scatter.39.cloned.1.call-start = ((), (), s32[]{:S(2)}) async-start(), calls=%async_computation.26 | async-start | bytes 5898240 | tf_op jit(solution)/shard_map/reduce_scatter | solution.py:318
  787.9 230.4 %reduce-scatter.51.cloned.1.call-start = ((), (), s32[]{:S(2)}) async-start(), calls=%async_computation.32 | async-start | bytes 884736
  790.0 265.1 %reduce-scatter.47.cloned.1.call-start = ((), (), s32[]{:S(2)}) async-start(), calls=%async_computation.30 | async-start | bytes 884736
  792.2 328.5 %reduce-scatter.43.cloned.1.call-start = ((), (), s32[]{:S(2)}) async-start(), calls=%async_computation.28 | async-start | bytes 884736
  794.3 396.2 %reduce-scatter.31.cloned.1.call-start = ((), (), s32[]{:S(2)}) async-start(), calls=%async_computation.22 | async-start | bytes 2211840 | tf_op jit(solution)/shard_map/reduce_scatter | solution.py:327
  799.3 78.3 %copy-start.21 = (f32[14,197]{1,0:T(8,128)S(1)}, f32[14,197]{1,0:T(8,128)}, u32[]{:S(2)}) copy-start(f32[14,197]{1,0:T(8,128)} %copy-done.20) | copy-start | bytes 33100
  799.3 461.2 %reduce-scatter.45.cloned.1.call-start = ((), (), s32[]{:S(2)}) async-start(), calls=%async_computation.29 | async-start | bytes 2211840
  824.7 507.8 %reduce-scatter.37.cloned.1.call-start = ((), (), s32[]{:S(2)}) async-start(), calls=%async_computation.25 | async-start | bytes 2654208 | tf_op jit(solution)/shard_map/reduce_scatter | solution.py:329
  875.6 528.9 %reduce-scatter.41.cloned.1.call-start = ((), (), s32[]{:S(2)}) async-start(), calls=%async_computation.27 | async-start | bytes 2654208 | tf_op jit(solution)/shard_map/reduce_scatter | solution.py:330
  (98 other events, 429.7 us)
Sparse Core Ops, SparseCore 0:
  371.1 27.0 reduce-scatter.32
  674.6 23.0 reduce-scatter.28
  709.9 23.0 reduce-scatter.24
  741.0 37.6 reduce-scatter.48
  781.7 40.4 reduce-scatter.26
  824.8 47.8 reduce-scatter.34
  875.2 47.8 reduce-scatter.38
  927.3 62.4 reduce-scatter.50
  993.7 61.4 reduce-scatter.46
  1059.2 61.3 reduce-scatter.42
  1124.7 65.7 reduce-scatter.30
  1194.8 65.6 reduce-scatter.44
  1264.5 67.9 reduce-scatter.36
  1336.5 67.9 reduce-scatter.40
where the time goes:
time: 1420 us; the launch traced here: 1410 us
  waiting for transfers between devices  482 us (34%)
  matrix products  412 us (29%)
  local copies, waits for them, and re-layouts  288 us (20%)
  other arithmetic  128 us (9%)
  blocking collectives  66.7 us (5%)
  starting transfers between devices  17.9 us (1%)
  between operations  15.3 us (1%)
    unnamed x19, waiting for transfers between devices  173 us
    reduce_scatter x1, waiting for transfers between devices, per_device(): lax.psum_scatter(partial_sums[5], 'frames', scatter_dimension=0, tiled=True)  72.1 us
    reduce_scatter x1, waiting for transfers between devices, per_device(): lax.psum_scatter(partial_sums[6], 'frames', scatter_dimension=0, tiled=True)  72 us
    reduce_scatter x1, waiting for transfers between devices, per_device(): lax.psum_scatter(partial_sums[3], 'frames', scatter_dimension=0, tiled=True)  69.9 us
    reduce_scatter x1, waiting for transfers between devices, per_device(): lax.psum_scatter(grad_up.astype(jnp.bfloat16), 'rows', scatter_dimension=...  47.9 us
    while x168, local copies, waits for them, and re-layouts  39.1 us
    unnamed x1, blocking collectives  37.1 us
    dot_general x7, matrix products, attend_backward(): jnp.einsum('fqhd,fkhd->fhqk', grad_heads, value_rows, preferred_element_t...  36.3 us
  transfers between devices with their start and end apart: 17, of which 10 were waited for; matrix products, arithmetic and copies ran while one was open for 37% of the time, Pallas kernels for 0%

commit v1 on v0

v1 whole, which is shorter than its diff:
```python
import functools

import jax
import jax.numpy as jnp
from jax import lax
from jax.experimental import pallas as pl
from jax.experimental.pallas import tpu as pltpu
from jax.sharding import PartitionSpec as P

H = 12
HD = 64
PAIR = 2 * HD
GROUP = 2
EPS = 1e-05
NEG = -1e30
FLOAT = jnp.float32
BFLOAT = jnp.bfloat16
VMEM_BYTES = 60 * 1024 * 1024


def params(**kw):
    return pltpu.CompilerParams(vmem_limit_bytes=VMEM_BYTES, **kw)


def padded_len(frame_len):
    return -(-(frame_len + 1) // 8) * 8


def whole(shape):
    return pl.BlockSpec(shape, lambda *_: (0,) * len(shape), pipeline_mode=pl.Buffered(1))


def rows_of(height, width):
    return pl.BlockSpec((height, width), lambda i: (i, 0))


def frames_of(pad, width):
    return pl.BlockSpec((GROUP, pad, width), lambda i: (i, 0, 0))


def normalize(values):
    center = values - jnp.mean(values, axis=-1, keepdims=True)
    spread = jnp.mean(center * center, axis=-1, keepdims=True)
    scale_inv = lax.rsqrt(spread + EPS)
    return (center * scale_inv, scale_inv)


def norm_back(grad_normed, normed, scale_inv):
    return scale_inv * (
        grad_normed
        - jnp.mean(grad_normed, axis=-1, keepdims=True)
        - normed * jnp.mean(grad_normed * normed, axis=-1, keepdims=True)
    )


def dot(a, b):
    return jnp.dot(a, b, preferred_element_type=FLOAT)


def dot_nt(a, b):
    return lax.dot_general(a, b, (((1,), (1,)), ((), ())), preferred_element_type=FLOAT)


def dot_tn(a, b):
    return lax.dot_general(a, b, (((0,), (0,)), ((), ())), preferred_element_type=FLOAT)


def load_rows(ref, frame_len):
    values = ref[...].astype(FLOAT)
    count, pad, width = values.shape
    row = lax.broadcasted_iota(jnp.int32, values.shape, 1)
    return jnp.where(row < frame_len, values, 0.0).reshape(count * pad, width)


def project_kernel(frame_len, x_ref, gain_ref, w_ref, hidden_ref, proj_ref):
    normed, _ = normalize(load_rows(x_ref, frame_len))
    hidden = (normed * gain_ref[...]).astype(BFLOAT)
    hidden_ref[...] = hidden
    width = hidden.shape[1]
    for part in range(3):
        cols = slice(part * width, (part + 1) * width)
        proj_ref[:, cols] = dot(hidden, w_ref[:, cols]).astype(BFLOAT)


def project(frames_in, gain, qkv):
    count, frame_len, width = frames_in.shape
    pad = padded_len(frame_len)
    block = GROUP * pad
    return pl.pallas_call(
        functools.partial(project_kernel, frame_len),
        grid=(count // GROUP,),
        in_specs=[frames_of(pad, width), whole((1, width)), whole(qkv.shape)],
        out_specs=[rows_of(block, width), rows_of(block, 3 * width)],
        out_shape=[
            jax.ShapeDtypeStruct((count * pad, width), BFLOAT),
            jax.ShapeDtypeStruct((count * pad, 3 * width), BFLOAT),
        ],
        compiler_params=params(),
        name="project",
    )(frames_in, gain, qkv)


def token_in(rows, token, frame_len):
    row = lax.broadcasted_iota(jnp.int32, rows.shape, 0)
    return jnp.where(row == frame_len, token, rows)


def attend_kernel(frame_len, x_ref, proj_ref, token_ref, out_w_ref, prob_ref, mixed_ref, res_ref):
    width = x_ref.shape[2]
    pad = x_ref.shape[1]
    pairs = width // PAIR

    def one_pair(j, carry):
        for f in range(GROUP):
            rows = pl.ds(f * pad, pad)
            at = [pl.ds(pl.multiple_of(part * width + j * PAIR, PAIR), PAIR) for part in range(3)]
            query = proj_ref[rows, at[0]]
            key = token_in(proj_ref[rows, at[1]], token_ref[f, :, at[0]], frame_len)
            value = token_in(proj_ref[rows, at[2]], token_ref[f, :, at[1]], frame_len)
            lane = lax.broadcasted_iota(jnp.int32, query.shape, 1)
            value_t = value.astype(FLOAT).T.astype(BFLOAT)
            outs = []
            for h in range(2):
                query_h = jnp.where((lane >= HD) == (h == 1), query, jnp.zeros_like(query))
                scores = dot_nt(key, query_h) * 0.125
                row = lax.broadcasted_iota(jnp.int32, scores.shape, 0)
                scores = jnp.where(row <= frame_len, scores, NEG)
                expo = jnp.exp(scores - jnp.max(scores, axis=0, keepdims=True))
                prob = (expo * (1.0 / jnp.sum(expo, axis=0, keepdims=True))).astype(BFLOAT)
                prob_ref[f, 2 * j + h] = prob
                outs.append(dot(value_t[h * HD : (h + 1) * HD], prob))
            mixed_ref[rows, at[0]] = jnp.concatenate(outs, axis=0).T.astype(BFLOAT)
        return carry

    lax.fori_loop(0, pairs, one_pair, 0)
    res_ref[...] = load_rows(x_ref, frame_len) + dot(mixed_ref[...], out_w_ref[...])


def attend(frames_in, proj, token_kv, out_w):
    count, frame_len, width = frames_in.shape
    pad = padded_len(frame_len)
    block = GROUP * pad
    heads = width // HD
    return pl.pallas_call(
        functools.partial(attend_kernel, frame_len),
        grid=(count // GROUP,),
        in_specs=[
            frames_of(pad, width),
            rows_of(block, 3 * width),
            frames_of(1, 2 * width),
            whole(out_w.shape),
        ],
        out_specs=[
            pl.BlockSpec((GROUP, heads, pad, pad), lambda i: (i, 0, 0, 0)),
            rows_of(block, width),
            rows_of(block, width),
        ],
        out_shape=[
            jax.ShapeDtypeStruct((count, heads, pad, pad), BFLOAT),
            jax.ShapeDtypeStruct((count * pad, width), BFLOAT),
            jax.ShapeDtypeStruct((count * pad, width), FLOAT),
        ],
        compiler_params=params(),
        name="attend",
    )(frames_in, proj, token_kv, out_w)


def mlp_kernel(
    frame_len,
    parts,
    res_ref,
    cot_ref,
    gain_ref,
    up_ref,
    down_ref,
    out_w_ref,
    output_ref,
    cot_rows_ref,
    second_ref,
    act_ref,
    grad_up_ref,
    branch_ref,
    grad_mixed_ref,
    gain_grad_ref,
):
    residual = res_ref[...]
    width = residual.shape[1]
    normed, scale_inv = normalize(residual)
    gain = gain_ref[...]
    second = (normed * gain).astype(BFLOAT)
    second_ref[...] = second
    cot = load_rows(cot_ref, frame_len)
    cot_bf = cot.astype(BFLOAT)
    cot_rows_ref[...] = cot_bf
    out = residual
    grad_second = jnp.zeros_like(residual)
    size = up_ref.shape[1] // parts
    for part in range(parts):
        cols = slice(part * size, (part + 1) * size)
        up_part = dot(second, up_ref[:, cols])
        sigma = 0.5 * jnp.tanh(0.851 * up_part) + 0.5
        gated = up_part * sigma
        act = gated.astype(BFLOAT)
        act_ref[:, cols] = act
        out = out + dot(act, down_ref[cols, :])
        grad_act = dot_nt(cot_bf, down_ref[cols, :])
        grad_up = (grad_act * (sigma + 1.702 * gated * (1.0 - sigma))).astype(BFLOAT)
        grad_up_ref[:, cols] = grad_up
        grad_second = grad_second + dot_nt(grad_up, up_ref[:, cols])
    output_ref[...] = out.astype(BFLOAT).reshape(output_ref.shape)
    gain_grad = jnp.sum(grad_second * normed, axis=0, keepdims=True)
    step = pl.program_id(0)
    gain_grad_ref[...] = jnp.where(step == 0, 0.0, gain_grad_ref[...]) + gain_grad
    branch = (cot + norm_back(grad_second * gain, normed, scale_inv)).astype(BFLOAT)
    branch_ref[...] = branch
    grad_mixed_ref[...] = dot_nt(branch, out_w_ref[...]).astype(BFLOAT)


def mlp(residual, cotangent, gain, up, down, out_w):
    count, frame_len, width = cotangent.shape
    pad = padded_len(frame_len)
    block = GROUP * pad
    rows = count * pad
    hidden = up.shape[1]
    shape = jax.ShapeDtypeStruct
    return pl.pallas_call(
        functools.partial(mlp_kernel, frame_len, 4),
        grid=(count // GROUP,),
        in_specs=[
            rows_of(block, width),
            frames_of(pad, width),
            whole((1, width)),
            whole(up.shape),
            whole(down.shape),
            whole(out_w.shape),
        ],
        out_specs=[
            frames_of(pad, width),
            rows_of(block, width),
            rows_of(block, width),
            rows_of(block, hidden),
            rows_of(block, hidden),
            rows_of(block, width),
            rows_of(block, width),
            pl.BlockSpec((1, width), lambda i: (0, 0)),
        ],
        out_shape=[
            shape((count, frame_len, width), BFLOAT),
            shape((rows, width), BFLOAT),
            shape((rows, width), BFLOAT),
            shape((rows, hidden), BFLOAT),
            shape((rows, hidden), BFLOAT),
            shape((rows, width), BFLOAT),
            shape((rows, width), BFLOAT),
            shape((1, width), FLOAT),
        ],
        compiler_params=params(),
        name="mlp",
    )(residual, cotangent, gain, up, down, out_w)


def weight_grad_kernel(left_ref, right_ref, out_ref):
    out_ref[...] = dot_tn(left_ref[...], right_ref[...]).astype(BFLOAT).reshape(out_ref.shape)


def weight_grad(left, right, tile, out_shape, out_block, out_index, name):
    rows = left.shape[0]
    return pl.pallas_call(
        weight_grad_kernel,
        grid=(right.shape[1] // tile,),
        in_specs=[whole(left.shape), pl.BlockSpec((rows, tile), lambda i: (0, i))],
        out_specs=pl.BlockSpec(out_block, out_index),
        out_shape=jax.ShapeDtypeStruct(out_shape, BFLOAT),
        compiler_params=params(),
        name=name,
    )(left, right)


def split_grad_kernel(left_ref, right_ref, out_ref, all_ref):
    step = pl.program_id(0)
    tile = right_ref.shape[1]
    all_ref[:, pl.ds(pl.multiple_of(step * tile, tile), tile)] = dot_tn(
        left_ref[...], right_ref[...]
    ).astype(BFLOAT)
    size = out_ref.shape[2]

    @pl.when(step == pl.num_programs(0) - 1)
    def _():
        for part in range(out_ref.shape[0]):
            out_ref[part] = all_ref[:, part * size : (part + 1) * size]


def split_grad(left, right, tile, parts, name):
    rows, width = left.shape
    columns = right.shape[1]
    shape = (parts, width, columns // parts)
    return pl.pallas_call(
        split_grad_kernel,
        grid=(columns // tile,),
        in_specs=[whole(left.shape), pl.BlockSpec((rows, tile), lambda i: (0, i))],
        out_specs=pl.BlockSpec(shape, lambda i: (0, 0, 0)),
        out_shape=jax.ShapeDtypeStruct(shape, BFLOAT),
        scratch_shapes=[pltpu.VMEM((width, columns), BFLOAT)],
        compiler_params=params(),
        name=name,
    )(left, right)


def attend_back_kernel(
    frame_len,
    proj_ref,
    token_ref,
    prob_ref,
    grad_mixed_ref,
    hidden_ref,
    token_hidden_ref,
    grad_proj_ref,
    full_hidden_ref,
    token_grad_ref,
):
    pad = prob_ref.shape[2]
    width = grad_mixed_ref.shape[1]
    for f in range(GROUP):
        rows = pl.ds(f * pad, pad)
        full_hidden_ref[rows, :] = token_in(hidden_ref[rows, :], token_hidden_ref[f], frame_len)

    def one_pair(j, carry):
        for f in range(GROUP):
            rows = pl.ds(f * pad, pad)
            at = [pl.ds(pl.multiple_of(part * width + j * PAIR, PAIR), PAIR) for part in range(3)]
            query = proj_ref[rows, at[0]]
            key = token_in(proj_ref[rows, at[1]], token_ref[f, :, at[0]], frame_len)
            value = token_in(proj_ref[rows, at[2]], token_ref[f, :, at[1]], frame_len)
            grad = grad_mixed_ref[rows, at[0]]
            lane = lax.broadcasted_iota(jnp.int32, query.shape, 1)
            key_t = key.astype(FLOAT).T.astype(BFLOAT)
            grad_query, grad_key, grad_value = [], [], []
            for h in range(2):
                prob = prob_ref[f, 2 * j + h]
                grad_h = jnp.where((lane >= HD) == (h == 1), grad, jnp.zeros_like(grad))
                grad_prob = dot_nt(value, grad_h)
                prob_f = prob.astype(FLOAT)
                part = prob_f * grad_prob
                scores = part - prob_f * jnp.sum(part, axis=0, keepdims=True)
                scores = scores.astype(BFLOAT)
                grad_value.append(dot(prob, grad))
                grad_key.append(dot(scores, query))
                grad_query.append(dot(key_t[h * HD : (h + 1) * HD], scores))
            grad_query = jnp.concatenate(grad_query, axis=0).T * 0.125
            grad_proj_ref[rows, at[0]] = grad_query.astype(BFLOAT)
            grad_key = jnp.where(lane >= HD, grad_key[1], grad_key[0]) * 0.125
            grad_proj_ref[rows, at[1]] = grad_key.astype(BFLOAT)
            grad_value = jnp.where(lane >= HD, grad_value[1], grad_value[0])
            grad_proj_ref[rows, at[2]] = grad_value.astype(BFLOAT)
        return carry

    lax.fori_loop(0, width // PAIR, one_pair, 0)
    for f in range(GROUP):
        row = f * pad + frame_len
        token_grad_ref[f] = grad_proj_ref[row : row + 1, width:]


def attend_back(proj, token_kv, prob, grad_mixed, hidden, token_hidden, frame_len):
    count, heads, pad, _ = prob.shape
    width = heads * HD
    block = GROUP * pad
    return pl.pallas_call(
        functools.partial(attend_back_kernel, frame_len),
        grid=(count // GROUP,),
        in_specs=[
            rows_of(block, 3 * width),
            frames_of(1, 2 * width),
            pl.BlockSpec((GROUP, heads, pad, pad), lambda i: (i, 0, 0, 0)),
            rows_of(block, width),
            rows_of(block, width),
            frames_of(1, width),
        ],
        out_specs=[rows_of(block, 3 * width), rows_of(block, width), frames_of(1, 2 * width)],
        out_shape=[
            jax.ShapeDtypeStruct((count * pad, 3 * width), BFLOAT),
            jax.ShapeDtypeStruct((count * pad, width), BFLOAT),
            jax.ShapeDtypeStruct((count, 1, 2 * width), BFLOAT),
        ],
        compiler_params=params(),
        name="attend_back",
    )(proj, token_kv, prob, grad_mixed, hidden, token_hidden)


def first_back_kernel(
    frame_len, x_ref, grad_proj_ref, branch_ref, class_ref, gain_ref, w_ref, grad_in_ref, gain_grad_ref
):
    normed, scale_inv = normalize(load_rows(x_ref, frame_len))
    grad = dot_nt(grad_proj_ref[...], w_ref[...])
    shape = (GROUP, grad.shape[0] // GROUP, grad.shape[1])
    step = pl.program_id(0)
    gain_grad = jnp.sum(grad * normed, axis=0, keepdims=True)
    gain_grad_ref[...] = jnp.where(step == 0, 0.0, gain_grad_ref[...]) + gain_grad
    total = branch_ref[...].astype(FLOAT) + norm_back(grad * gain_ref[...], normed, scale_inv)
    total = total.reshape(shape)
    row = lax.broadcasted_iota(jnp.int32, shape, 1)
    total = jnp.where(row == 0, total + class_ref[...], total)
    grad_in_ref[...] = total.astype(BFLOAT)


def first_back(frames_in, grad_proj, branch, class_grad, gain, qkv):
    count, frame_len, width = frames_in.shape
    pad = padded_len(frame_len)
    block = GROUP * pad
    return pl.pallas_call(
        functools.partial(first_back_kernel, frame_len),
        grid=(count // GROUP,),
        in_specs=[
            frames_of(pad, width),
            rows_of(block, 3 * width),
            rows_of(block, width),
            frames_of(1, width),
            whole((1, width)),
            whole(qkv.shape),
        ],
        out_specs=[frames_of(pad, width), pl.BlockSpec((1, width), lambda i: (0, 0))],
        out_shape=[
            jax.ShapeDtypeStruct((count, frame_len, width), BFLOAT),
            jax.ShapeDtypeStruct((1, width), FLOAT),
        ],
        compiler_params=params(),
        name="first_back",
    )(frames_in, grad_proj, branch, class_grad, gain, qkv)


def message_kernel(
    own,
    class_ref,
    id_row_ref,
    id_col_ref,
    weight_ref,
    gain_ref,
    qkv_ref,
    out_w_ref,
    attn_gain_ref,
    key_w_ref,
    value_w_ref,
    start_ref,
    hidden_ref,
    proj_ref,
    prob_ref,
    mixed_ref,
    message_ref,
    token_hidden_ref,
    token_kv_ref,
):
    width = weight_ref.shape[0]
    start = dot(class_ref[...], weight_ref[...]).astype(BFLOAT)
    start_ref[...] = start
    normed, _ = normalize(start.astype(FLOAT))
    hidden = (normed * gain_ref[...]).astype(BFLOAT)
    hidden_ref[...] = hidden
    proj_ref[...] = dot(hidden, qkv_ref[...]).astype(BFLOAT)
    visible = id_col_ref[...] == id_row_ref[...]

    def one_pair(j, carry):
        at = [pl.ds(pl.multiple_of(part * width + j * PAIR, PAIR), PAIR) for part in range(3)]
        query, key, value = (proj_ref[:, at[part]] for part in range(3))
        lane = lax.broadcasted_iota(jnp.int32, query.shape, 1)
        value_t = value.astype(FLOAT).T.astype(BFLOAT)
        outs = []
        for h in range(2):
            query_h = jnp.where((lane >= HD) == (h == 1), query, jnp.zeros_like(query))
            scores = jnp.where(visible, dot_nt(key, query_h) * 0.125, NEG)
            expo = jnp.exp(scores - jnp.max(scores, axis=0, keepdims=True))
            prob = (expo * (1.0 / jnp.sum(expo, axis=0, keepdims=True))).astype(BFLOAT)
            prob_ref[2 * j + h] = prob
            outs.append(dot(value_t[h * HD : (h + 1) * HD], prob))
        mixed_ref[:, at[0]] = jnp.concatenate(outs, axis=0).T.astype(BFLOAT)
        return carry

    lax.fori_loop(0, width // PAIR, one_pair, 0)
    message = start[:own].astype(FLOAT) + dot(mixed_ref[:own, :], out_w_ref[...])
    message = message.astype(BFLOAT)
    message_ref[...] = message
    normed, _ = normalize(message.astype(FLOAT))
    token_hidden = (normed * attn_gain_ref[...]).astype(BFLOAT)
    token_hidden_ref[...] = token_hidden
    token_kv_ref[:, :width] = dot(token_hidden, key_w_ref[...]).astype(BFLOAT)
    token_kv_ref[:, width:] = dot(token_hidden, value_w_ref[...]).astype(BFLOAT)


def message_forward(class_all, ids, own, weight, gain, qkv, out_w, attn_gain, attn_qkv):
    slots, width = class_all.shape
    heads = width // HD
    shape = jax.ShapeDtypeStruct
    part = lambda index: pl.BlockSpec((width, width), lambda i, index=index: (0, index))
    return pl.pallas_call(
        functools.partial(message_kernel, own),
        grid=(1,),
        in_specs=[
            whole((slots, width)),
            whole((1, slots)),
            whole((slots, 1)),
            whole(weight.shape),
            whole((1, width)),
            whole(qkv.shape),
            whole(out_w.shape),
            whole((1, width)),
            part(1),
            part(2),
        ],
        out_specs=[
            whole((slots, width)),
            whole((slots, width)),
            whole((slots, 3 * width)),
            whole((heads, slots, slots)),
            whole((slots, width)),
            whole((own, width)),
            whole((own, width)),
            whole((own, 2 * width)),
        ],
        out_shape=[
            shape((slots, width), BFLOAT),
            shape((slots, width), BFLOAT),
            shape((slots, 3 * width), BFLOAT),
            shape((heads, slots, slots), BFLOAT),
            shape((slots, width), BFLOAT),
            shape((own, width), BFLOAT),
            shape((own, width), BFLOAT),
            shape((own, 2 * width), BFLOAT),
        ],
        compiler_params=params(),
        name="message_forward",
    )(
        class_all,
        ids.reshape(1, slots),
        ids.reshape(slots, 1),
        weight,
        gain,
        qkv,
        out_w,
        attn_gain,
        attn_qkv,
        attn_qkv,
    )


def token_back_kernel(token_grad_ref, message_ref, gain_ref, key_w_ref, value_w_ref, grad_ref, gain_grad_ref):
    width = message_ref.shape[1]
    normed, scale_inv = normalize(message_ref[...].astype(FLOAT))
    grad = dot_nt(token_grad_ref[:, :width], key_w_ref[...])
    grad = grad + dot_nt(token_grad_ref[:, width:], value_w_ref[...])
    gain_grad_ref[...] = jnp.sum(grad * normed, axis=0, keepdims=True)
    grad_ref[...] = norm_back(grad * gain_ref[...], normed, scale_inv).astype(BFLOAT)


def token_back(token_grad, message, gain, attn_qkv):
    own, width = message.shape
    part = lambda index: pl.BlockSpec((width, width), lambda i, index=index: (0, index))
    return pl.pallas_call(
        token_back_kernel,
        grid=(1,),
        in_specs=[whole(token_grad.shape), whole(message.shape), whole((1, width)), part(1), part(2)],
        out_specs=[whole((own, width)), whole((1, width))],
        out_shape=[
            jax.ShapeDtypeStruct((own, width), BFLOAT),
            jax.ShapeDtypeStruct((1, width), FLOAT),
        ],
        compiler_params=params(),
        name="token_back",
    )(token_grad, message, gain, attn_qkv, attn_qkv)


def message_back_kernel(
    own,
    parts,
    block_ref,
    grad_ref,
    class_ref,
    start_ref,
    hidden_ref,
    proj_ref,
    prob_ref,
    mixed_ref,
    weight_ref,
    gain_ref,
    qkv_ref,
    out_w_ref,
    class_grad_ref,
    gain_grad_ref,
    sums_ref,
    grad_mixed_ref,
    grad_proj_ref,
):
    width = weight_ref.shape[0]
    grad = grad_ref[...]
    j = pl.program_id(0)

    @pl.when(j == 0)
    def _():
        grad_mixed_ref[...] = dot_nt(grad, out_w_ref[...]).astype(BFLOAT)

    def finish():
        grad_proj = grad_proj_ref[...]
        grad_hidden = dot_nt(grad_proj, qkv_ref[...])
        normed, scale_inv = normalize(start_ref[...].astype(FLOAT))
        gain_grad_ref[...] = jnp.sum(grad_hidden[:own] * normed[:own], axis=0, keepdims=True)
        back = norm_back(grad_hidden * gain_ref[...], normed, scale_inv)
        start_grad = (grad.astype(FLOAT) + back).astype(BFLOAT)
        class_grad_ref[...] = dot_nt(start_grad[:own], weight_ref[...])
        size = sums_ref.shape[1]
        row = lax.broadcasted_iota(jnp.int32, (size, width), 0)
        column = lax.broadcasted_iota(jnp.int32, (size, width), 1)
        pick = (column == row + block_ref[0] * size).astype(BFLOAT)
        offset = 0
        for left, right in (
            (hidden_ref[...], grad_proj),
            (class_ref[...], start_grad),
            (mixed_ref[...], grad),
        ):
            total = dot(dot_nt(pick, left).astype(BFLOAT), right).astype(BFLOAT)
            columns = total.shape[1] // parts
            for part in range(parts):
                sums_ref[part, :, offset : offset + columns] = total[
                    :, part * columns : (part + 1) * columns
                ]
            offset += columns

    at = [pl.ds(pl.multiple_of(part * width + j * PAIR, PAIR), PAIR) for part in range(3)]
    query, key, value = (proj_ref[:, at[part]] for part in range(3))
    grad_m = grad_mixed_ref[:, at[0]]
    lane = lax.broadcasted_iota(jnp.int32, query.shape, 1)
    key_t = key.astype(FLOAT).T.astype(BFLOAT)
    grad_query, grad_key, grad_value = [], [], []
    for h in range(2):
        prob = prob_ref[h]
        grad_h = jnp.where((lane >= HD) == (h == 1), grad_m, jnp.zeros_like(grad_m))
        grad_prob = dot_nt(value, grad_h)
        prob_f = prob.astype(FLOAT)
        part = prob_f * grad_prob
        scores = (part - prob_f * jnp.sum(part, axis=0, keepdims=True)).astype(BFLOAT)
        grad_value.append(dot(prob, grad_m))
        grad_key.append(dot(scores, query))
        grad_query.append(dot(key_t[h * HD : (h + 1) * HD], scores))
    grad_query = jnp.concatenate(grad_query, axis=0).T * 0.125
    grad_proj_ref[:, at[0]] = grad_query.astype(BFLOAT)
    grad_key = jnp.where(lane >= HD, grad_key[1], grad_key[0]) * 0.125
    grad_proj_ref[:, at[1]] = grad_key.astype(BFLOAT)
    grad_value = jnp.where(lane >= HD, grad_value[1], grad_value[0])
    grad_proj_ref[:, at[2]] = grad_value.astype(BFLOAT)

    @pl.when(j == pl.num_programs(0) - 1)
    def _():
        finish()


def message_back(block, parts, size, own, grad_all, class_all, saved, weight, gain, qkv, out_w):
    slots, width = class_all.shape
    start, hidden, proj, prob, mixed = saved
    shape = jax.ShapeDtypeStruct
    sums = (parts, size, 5 * width // parts)
    args = (grad_all, class_all, start, hidden, proj, prob, mixed, weight, gain, qkv, out_w)
    return pl.pallas_call(
        functools.partial(message_back_kernel, own, parts),
        grid=(width // PAIR,),
        in_specs=[pl.BlockSpec(memory_space=pltpu.SMEM)]
        + [pl.BlockSpec((2, slots, slots), lambda j: (j, 0, 0)) if a is prob else whole(a.shape) for a in args],
        out_specs=[whole((own, width)), whole((1, width)), whole(sums)],
        out_shape=[shape((own, width), FLOAT), shape((1, width), FLOAT), shape(sums, BFLOAT)],
        scratch_shapes=[pltpu.VMEM((slots, width), BFLOAT), pltpu.VMEM((slots, 3 * width), BFLOAT)],
        compiler_params=params(),
        name="message_back",
    )(block, *args)


def swap(values, axis, distance):
    return lax.ppermute(values, axis, [(i, i ^ distance) for i in range(lax.axis_size(axis))])


def gather_frames(values):
    owners = lax.axis_size("frames")
    if owners > 8:
        order = lax.axis_index("frames") ^ jnp.arange(owners)
        stacked = jnp.take(lax.all_gather(values, "frames"), order, axis=0)
    else:
        stacked = jnp.stack([values] + [swap(values, "frames", d) for d in range(1, owners)])
    return stacked.reshape(owners * values.shape[0], *values.shape[1:])


def pick(values, index, axis=0):
    return lax.dynamic_index_in_dim(values, index, axis, keepdims=False)


def add(*terms):
    total = terms[0].astype(FLOAT)
    for term in terms[1:]:
        total = total + term.astype(FLOAT)
    return total


def halve(values, axis, distance):
    bit = (lax.axis_index(axis) // distance) % 2
    got = swap(pick(values, 1 - bit, 1), axis, distance)
    return add(got, pick(values, bit, 1)).astype(BFLOAT)


def sum_over(values, axis, limit):
    size, distance = lax.axis_size(axis), 1
    block = values.shape[1:]
    while size > limit:
        values = halve(values.reshape(size // 2, 2, *block), axis, distance)
        size, distance = size // 2, 2 * distance
    index = lax.axis_index(axis) // distance
    terms = [pick(values, index)]
    for d in range(1, size):
        terms.append(swap(pick(values, index ^ d), axis, d * distance))
    return add(*terms)


def per_device(
    frames_in,
    cotangent,
    video_ids,
    frame_device,
    msg_weight,
    msg_gain,
    msg_qkv,
    msg_out,
    attn_gain,
    attn_qkv,
    attn_out,
    mlp_gain,
    up_weight,
    down_weight,
):
    count, frame_len, width = frames_in.shape
    owners, parts = lax.axis_size("frames"), lax.axis_size("rows")
    hidden_width = up_weight.shape[1]
    own = -(-count // 16) * 16
    msg_gain, attn_gain, mlp_gain = (g.reshape(1, width) for g in (msg_gain, attn_gain, mlp_gain))
    block_index = lax.axis_index("frames").astype(jnp.int32).reshape(1)

    extra = ((0, own - count), (0, 0))
    class_all = gather_frames(jnp.pad(frames_in[:, 0, :], extra))
    ids = video_ids * owners + frame_device
    ids = gather_frames(jnp.pad(ids, (0, own - count), constant_values=-1))

    hidden, proj = project(frames_in, attn_gain, attn_qkv)
    *saved, message, token_hidden, token_kv = message_forward(
        class_all, ids, own, msg_weight, msg_gain, msg_qkv, msg_out, attn_gain, attn_qkv
    )
    token_kv = token_kv[:count, None]
    token_hidden = token_hidden[:count, None]
    prob, mixed, residual = attend(frames_in, proj, token_kv, attn_out)
    output, cot, second, act, grad_up, branch, grad_mixed, mlp_gain_grad = mlp(
        residual, cotangent, mlp_gain, up_weight, down_weight, attn_out
    )
    tile = 384
    tiles = hidden_width // tile
    half = hidden_width // parts // tile
    down_sum = weight_grad(
        cot,
        act,
        tile,
        (parts, tiles, width // parts, tile),
        (parts, 1, width // parts, tile),
        lambda i: (0, i, 0, 0),
        "grad_down",
    )
    up_sum = weight_grad(
        second,
        grad_up,
        tile,
        (parts, width, hidden_width // parts),
        (1, width, tile),
        lambda i: (i // half, 0, i % half),
        "grad_up",
    )
    out_sum = split_grad(mixed, branch, 256, parts, "grad_attn_out")
    grad_proj, hidden, token_grad = attend_back(
        proj, token_kv, prob, grad_mixed, hidden, token_hidden, frame_len
    )
    message_grad, token_gain_grad = token_back(
        jnp.pad(token_grad.reshape(count, 2 * width), extra), message, attn_gain, attn_qkv
    )
    grad_all = gather_frames(message_grad)
    qkv_sum = split_grad(hidden, grad_proj, 768, parts, "grad_attn_qkv")
    class_grad, msg_gain_grad, msg_sums = message_back(
        block_index,
        parts,
        width // owners,
        own,
        grad_all,
        class_all,
        saved,
        msg_weight,
        msg_gain,
        msg_qkv,
        msg_out,
    )
    grad_in, attn_gain_grad = first_back(
        frames_in, grad_proj, branch, class_grad[:count, None], attn_gain, attn_qkv
    )

    def summed(values):
        values = sum_over(values, "rows", 2)
        values = values.astype(BFLOAT).reshape(owners, -1, *values.shape[1:])
        return sum_over(values, "frames", 4)

    down_sum = sum_over(down_sum, "rows", 2).astype(BFLOAT)
    if tiles != owners:
        down_sum = jnp.swapaxes(down_sum, 1, 2).reshape(width // parts, owners, -1)
        down_sum = jnp.swapaxes(down_sum, 0, 1)
    grad_down = sum_over(down_sum, "frames", 4).T
    grad_up = summed(up_sum)
    grad_out = summed(out_sum)
    grad_qkv = summed(qkv_sum)
    msg_sums = sum_over(msg_sums, "rows", 2)
    cuts = (3 * width // parts, 4 * width // parts)
    grad_msg_qkv, grad_msg_weight, grad_msg_out = jnp.split(msg_sums, cuts, axis=1)
    gains = jnp.concatenate([msg_gain_grad, attn_gain_grad + token_gain_grad, mlp_gain_grad])
    gains = add(gains, *(swap(gains, "rows", d) for d in range(1, parts)))
    gains = jnp.swapaxes(gains.reshape(3, owners, -1), 0, 1)
    gains = sum_over(gains, "frames", 8)
    return (
        output,
        grad_in,
        grad_msg_weight,
        gains[0],
        grad_msg_qkv,
        grad_msg_out,
        gains[1],
        grad_qkv,
        grad_out,
        gains[2],
        grad_up,
        grad_down,
    )


def solution(mesh):
    split = P(("frames", "rows"))
    matrix = P("frames", "rows")
    gain = P("frames")
    return jax.shard_map(
        per_device,
        mesh=mesh,
        in_specs=(split, split, split, split) + (P(),) * 10,
        out_specs=(
            split,
            split,
            matrix,
            gain,
            matrix,
            matrix,
            gain,
            matrix,
            matrix,
            gain,
            matrix,
            matrix,
        ),
        check_vma=False,
    )
```

time: 1420 us -> 560 us (0.39)
  matrix products: 412 us -> 0 us
  waiting for transfers between devices: 482 us -> 83.9 us
  Pallas kernels: 0 us -> 326 us
  local copies, waits for them, and re-layouts: 288 us -> 45.7 us
  other arithmetic: 128 us -> 21.6 us
  blocking collectives: 66.7 us -> 0 us
  starting transfers between devices: 17.9 us -> 74.5 us
    dot_general x82 -> x0, matrix products: 412 us -> none  [the longest x7 36.3 us: attend_backward(): jnp.einsum('fqhd,fkhd->fhqk', grad_heads, value_rows, preferred_element_t...]
    pallas_call x0 -> x12, Pallas kernels: none -> 326 us  [the longest x1 74.1 us: mlp(): pl.pallas_call(functools.partial(mlp_kernel, frame_len, 4), grid=(count /...]
    reduce_scatter x9 -> x0, waiting for transfers between devices: 305 us -> none  [the longest x1 72.1 us: per_device(): lax.psum_scatter(partial_sums[5], 'frames', scatter_dimension=0, tiled=True)]
    unnamed x19 -> x0, waiting for transfers between devices: 173 us -> none
    ppermute x0 -> x57, waiting for transfers between devices: none -> 83.9 us  [swap(): lax.ppermute(values, axis, [(i, i ^ distance) for i in range(lax.axis_siz...]
    ppermute x0 -> x57, starting transfers between devices: none -> 74.5 us  [swap(): lax.ppermute(values, axis, [(i, i ^ distance) for i in range(lax.axis_siz...]
    while x169 -> x0, local copies, waits for them, and re-layouts: 58.2 us -> none
    concatenate x36 -> x0, local copies, waits for them, and re-layouts: 43.2 us -> none  [the longest x14 20.8 us: split_heads(): jnp.concatenate([proj[..., width:2 * width], token[:, None, :width]], axi...]
  transfers between devices with their start and end apart: 17 -> 57, of which waited for: 10 -> 19; matrix products, arithmetic and copies ran while one was open for 37% -> 11% of each run, Pallas kernels for 0% -> 22%
where the time goes in v1:
time: 560 us; the launch traced here: 553 us
  Pallas kernels  326 us (58%)
  waiting for transfers between devices  83.9 us (15%)
  starting transfers between devices  74.5 us (13%)
  local copies, waits for them, and re-layouts  45.7 us (8%)
  other arithmetic  21.6 us (4%)
    ppermute x57, waiting for transfers between devices, swap(): lax.ppermute(values, axis, [(i, i ^ distance) for i in range(lax.axis_siz...  83.9 us
    ppermute x57, starting transfers between devices, swap(): lax.ppermute(values, axis, [(i, i ^ distance) for i in range(lax.axis_siz...  74.5 us
    pallas_call x1, Pallas kernels, mlp(): pl.pallas_call(functools.partial(mlp_kernel, frame_len, 4), grid=(count /...  74.1 us
    pallas_call x1, Pallas kernels, attend(): pl.pallas_call(functools.partial(attend_kernel, frame_len), grid=(count /...  60 us
    pallas_call x1, Pallas kernels, attend_back(): pl.pallas_call(functools.partial(attend_back_kernel, frame_len), grid=(co...  58.9 us
    pallas_call x2, Pallas kernels, weight_grad(): pl.pallas_call(weight_grad_kernel, grid=(right.shape[1] // tile,), in_spe...  47 us
    pallas_call x2, Pallas kernels, split_grad(): pl.pallas_call(split_grad_kernel, grid=(columns // tile,), in_specs=[whol...  25.1 us
    pallas_call x1, Pallas kernels, first_back(): pl.pallas_call(functools.partial(first_back_kernel, frame_len), grid=(cou...  19.2 us
  transfers between devices with their start and end apart: 57, of which 19 were waited for; matrix products, arithmetic and copies ran while one was open for 11% of the time, Pallas kernels for 22%

profile of v1, /device:TPU:0, one launch (start us, length us, event | category | flops | bytes accessed | tf_op | source)
XLA Modules:
  0.0 553.5 jit_solution(9276532111616101645)
XLA Ops:
  1.6 3.0 collective-permute-start
  14.2 16.8 %project.1 = (bf16[2800,768]{1,0:T(8,128)(2,1)}, bf16[2800,2304]{1,0:T(8,128)(2,1)}) custom-call(bf16[14,197,768]{2,1,0:T(8,128)(2,1)} %x_ref.5, f32[1,768]{1,0:T(1,128)} %reshape.118.gain_ref.attn_gain_ref, bf16[768,2304]{1,0:T(8,128)(2,1)} %w_ref.3), custom_call_target="tpu_custom_call" | custom-call | tf_op jit(solution)/shard_map/project/pallas_call | solution.py:89
  31.1 2.9 collective-permute-start.10
  43.4 3.6 collective-permute-done.13
  50.9 3.0 collective-permute-start.6
  58.1 10.1 %message_forward.1 = (bf16[128,768]{1,0:T(8,128)(2,1)}, bf16[128,768]{1,0:T(8,128)(2,1)}, bf16[128,2304]{1,0:T(8,128)(2,1)}, bf16[12,128,128]{2,1,0:T(8,128)(2,1...) custom-call(bf16[128,768]{1,0:T(8,128)(2,1)} %bitcast.237, ...), custom_call_target="tpu_custom_call" | custom-call | tf_op jit(solution)/shard_map/message_forward/pallas_call | solution.py:492
  71.1 60.0 %attend.1 = (bf16[14,12,200,200]{3,2,1,0:T(8,128)(2,1)}, bf16[2800,768]{1,0:T(8,128)(2,1)}, f32[2800,768]{1,0:T(8,128)}) custom-call(bf16[14,197,768]{2,1,0:T(8,128)(2,1)} %x_ref.5, bf16[2800,2304]{1,0:T(8,128)(2,1)} %get-tuple-element.43.proj_ref, bf16[14,1,1536]{2,1,0:T(2,128)(2,1)} %copy.85.token_ref, bf16[768,768]{1,0:T(8,128)(2,1)} %out_w_ref.6), custom_call_target="tpu_custom_call" | custom-call | tf_op jit(solution)/shard_map/attend/pallas_call | solution.py:144
  131.1 74.1 %mlp.1 = (bf16[14,197,768]{2,1,0:T(8,128)(2,1)}, bf16[2800,768]{1,0:T(8,128)(2,1)}, bf16[2800,768]{1,0:T(8,128)(2,1)}, bf16[2800,3072]{1,0:T(8,128)(2,1)}, bf16[...) custom-call(f32[2800,768]{1,0:T(8,128)} %get-tuple-element.45.res_ref, ...), custom_call_target="tpu_custom_call" | custom-call | tf_op jit(solution)/shard_map/mlp/pallas_call | solution.py:226
  205.2 58.9 %attend_back.1 = (bf16[2800,2304]{1,0:T(8,128)(2,1)}, bf16[2800,768]{1,0:T(8,128)(2,1)}, bf16[14,1,1536]{2,1,0:T(2,128)(2,1)}) custom-call(bf16[2800,2304]{1,0:T(8,128)(2,1)} %get-tuple-element.43.proj_ref, bf16[14,1,1536]{2,1,0:T(2,128)(2,1)} %copy.85.token_ref, bf16[14,12,200,200]{3,2,1,0:T(8,128)(2,1)} %get-tuple-element.47.prob_ref, ...), custom_call_target="tpu_custom_call" | custom-call | tf_op jit(solution)/shard_map/attend_back/pallas_call | solution.py:367
  265.6 3.1 token_back.1
  275.9 23.4 %grad_down.1 = bf16[4,8,192,384]{3,2,1,0:T(8,128)(2,1)} custom-call(bf16[2800,768]{1,0:T(8,128)(2,1)} %get-tuple-element.72.left_ref, bf16[2800,3072]{1,0:T(8,128)(2,1)} %get-tuple-element.73.right_ref), custom_call_target="tpu_custom_call" | custom-call | tf_op jit(solution)/shard_map/grad_down/pallas_call | solution.py:268
  299.3 3.4 dynamic-slice_bitcast_fusion
  302.7 8.1 %grad_attn_out.1 = bf16[4,768,192]{2,1,0:T(8,128)(2,1)} custom-call(bf16[2800,768]{1,0:T(8,128)(2,1)} %get-tuple-element.69.left_ref, bf16[2800,768]{1,0:T(8,128)(2,1)} %get-tuple-element.52.branch_ref.right_ref), custom_call_target="tpu_custom_call" | custom-call | tf_op jit(solution)/shard_map/grad_attn_out/pallas_call | solution.py:297
  314.3 16.9 %grad_attn_qkv.1 = bf16[4,768,576]{2,1,0:T(8,128)(2,1)} custom-call(bf16[2800,768]{1,0:T(8,128)(2,1)} %get-tuple-element.68.left_ref, bf16[2800,2304]{1,0:T(8,128)(2,1)} %get-tuple-element.51.grad_proj_ref.right_ref), custom_call_target="tpu_custom_call" | custom-call | tf_op jit(solution)/shard_map/grad_attn_qkv/pallas_call | solution.py:297
  331.2 3.0 collective-permute-start.19
  336.9 3.9 collective-permute-done.20
  341.5 11.8 %message_back.1 = (f32[16,768]{1,0:T(8,128)}, f32[1,768]{1,0:T(1,128)}, bf16[4,96,960]{2,1,0:T(8,128)(2,1)}) custom-call(s32[1]{0:T(128)} %bitcast.20.block_ref, bf16[128,768]{1,0:T(8,128)(2,1)} %bitcast.243, bf16[128,768]{1,0:T(8,128)(2,1)} %bitcast.238, bf16[128,768]{1,0:T(8,128)(2,1)} %get-tuple-element.56.start_ref, ...), custom_call_target="tpu_custom_call" | custom-call | tf_op jit(solution)/shard_map/message_back/pallas_call | solution.py:658
  354.8 19.2 %first_back.1 = (bf16[14,197,768]{2,1,0:T(8,128)(2,1)}, f32[1,768]{1,0:T(1,128)}) custom-call(bf16[14,197,768]{2,1,0:T(8,128)(2,1)} %x_ref.5, bf16[2800,2304]{1,0:T(8,128)(2,1)} %get-tuple-element.51.grad_proj_ref.right_ref, bf16[2800,768]{1,0:T(8,128)(2,1)} %get-tuple-element.52.branch_ref.right_ref, f32[14,1,768]{2,1,0:T(1,128)} %broadcast_in_dim.11.class_ref, ...), custom_call_target="tpu_custom_call" | custom-call | tf_op jit(solution)/shard_map/first_back/pallas_call | solution.py:409
  378.9 23.6 %grad_up.1 = bf16[4,768,768]{2,1,0:T(8,128)(2,1)} custom-call(bf16[2800,768]{1,0:T(8,128)(2,1)} %get-tuple-element.70.left_ref, bf16[2800,3072]{1,0:T(8,128)(2,1)} %get-tuple-element.71.right_ref), custom_call_target="tpu_custom_call" | custom-call | tf_op jit(solution)/shard_map/grad_up/pallas_call | solution.py:268
  403.3 2.9 collective-permute-start.28
  406.2 3.4 dynamic-slice_bitcast_fusion.1
  409.9 4.2 copy.89
  416.5 3.0 collective-permute-start.30
  421.1 3.0 collective-permute-start.32
  432.3 6.8 %collective-permute-done.40 = bf16[768,192]{0,1:T(8,128)(2,1)S(1)} collective-permute-done((bf16[768,192]{0,1:T(8,128)(2,1)S(1)}, bf16[768,192]{0,1:T(8,128)(2,1)S(1)}, u32[]{:S(2)}, u32[]{:S(2)}) %collective-permute-start.40) | collective-permute-done | bytes 294944 | tf_op jit(solution)/shard_map/ppermute | solution.py:672
  464.3 13.2 %collective-permute-done.34 = bf16[768,576]{0,1:T(8,128)(2,1)S(1)} collective-permute-done((bf16[768,576]{0,1:T(8,128)(2,1)S(1)}, bf16[768,576]{0,1:T(8,128)(2,1)S(1)}, u32[]{:S(2)}, u32[]{:S(2)}) %collective-permute-start.34) | collective-permute-done | bytes 884768 | tf_op jit(solution)/shard_map/ppermute | solution.py:672
  488.0 3.6 collective-permute-done.35
  497.3 5.6 %collective-permute-done.52 = bf16[8,192,384]{2,1,0:T(8,128)(2,1)} collective-permute-done((bf16[8,192,384]{2,1,0:T(8,128)(2,1)}, bf16[8,192,384]{2,1,0:T(8,128)(2,1)}, u32[]{:S(2)}, u32[]{:S(2)}) %collective-permute-start.52) | collective-permute-done | bytes 1179680 | tf_op jit(solution)/shard_map/ppermute | solution.py:672
  505.5 19.2 %collective-permute-done.46 = bf16[768,768]{1,0:T(8,128)(2,1)} collective-permute-done((bf16[768,768]{1,0:T(8,128)(2,1)}, bf16[768,768]{1,0:T(8,128)(2,1)}, u32[]{:S(2)}, u32[]{:S(2)}) %collective-permute-start.46) | collective-permute-done | bytes 1179680 | tf_op jit(solution)/shard_map/ppermute | solution.py:672
  528.1 3.5 collective-permute-start.55
  532.4 5.9 %collective-permute-done.47 = bf16[4,96,768]{2,1,0:T(8,128)(2,1)S(1)} collective-permute-done((bf16[4,96,768]{2,1,0:T(8,128)(2,1)S(1)}, bf16[4,96,768]{2,1,0:T(8,128)(2,1)S(1)}, u32[]{:S(2)}, u32[]{:S(2)}) %collective-permute-start.47) | collective-permute-done | bytes 589856 | tf_op jit(solution)/shard_map/ppermute | solution.py:672
  545.7 6.5 %collective-permute-done.49 = bf16[96,768]{1,0:T(8,128)(2,1)S(1)} collective-permute-done((bf16[96,768]{1,0:T(8,128)(2,1)S(1)}, bf16[96,768]{1,0:T(8,128)(2,1)S(1)}, u32[]{:S(2)}, u32[]{:S(2)}) %collective-permute-start.49) | collective-permute-done | bytes 147488 | tf_op jit(solution)/shard_map/ppermute | solution.py:672
  (228 shorter events, 122.0 us)
Async XLA Ops:
  1.6 47.5 %collective-permute-start = (bf16[16,768]{1,0:T(8,128)(2,1)S(1)}, bf16[16,768]{1,0:T(8,128)(2,1)S(1)}, u32[]{:S(2)}, u32[]{:S(2)}) collective-permute-start(bf16[16,768]{1,0:T(8,128)(2,1)S(1)} %pad.12), channel_id=1, source_target_pairs={{0,4},{4,0},{8,12},{12,8},{16,20},{20,16},{24,28},{28,24},{1,5},{5... | collective-permute-start | bytes 73736 | tf_op jit(solution)/shard_map/ppermute | solution.py:672
  4.6 46.3 %collective-permute-start.1 = (bf16[16,768]{1,0:T(8,128)(2,1)S(1)}, bf16[16,768]{1,0:T(8,128)(2,1)S(1)}, u32[]{:S(2)}, u32[]{:S(2)}) collective-permute-start(bf16[16,768]{1,0:T(8,128)(2,1)S(1)} %pad.12), channel_id=1, source_target_pairs={{0,8},{4,12},{8,0},{12,4},{16,24},{20,28},{24,16},{28,20},{1,9},{5... | collective-permute-start | bytes 73736 | tf_op jit(solution)/shard_map/ppermute | solution.py:672
  6.2 47.7 %collective-permute-start.2 = (bf16[16,768]{1,0:T(8,128)(2,1)S(1)}, bf16[16,768]{1,0:T(8,128)(2,1)S(1)}, u32[]{:S(2)}, u32[]{:S(2)}) collective-permute-start(bf16[16,768]{1,0:T(8,128)(2,1)S(1)} %pad.12), channel_id=1, source_target_pairs={{0,12},{4,8},{8,4},{12,0},{16,28},{20,24},{24,20},{28,16},{1,13},{... | collective-permute-start | bytes 73736 | tf_op jit(solution)/shard_map/ppermute | solution.py:672
  6.9 24.1 %collective-permute-start.7 = (s32[16]{0:T(128)S(1)}, s32[16]{0:T(128)S(1)}, u32[]{:S(2)}, u32[]{:S(2)}) collective-permute-start(s32[16]{0:T(128)S(1)} %get-tuple-element.154), channel_id=1, source_target_pairs={{0,4},{4,0},{8,12},{12,8},{16,20},{20,16},{24,28},{28,24},{1,5},{5... | collective-permute-start | bytes 200 | tf_op jit(solution)/shard_map/ppermute | solution.py:672
  8.8 22.3 %collective-permute-start.8 = (s32[16]{0:T(128)S(1)}, s32[16]{0:T(128)S(1)}, u32[]{:S(2)}, u32[]{:S(2)}) collective-permute-start(s32[16]{0:T(128)S(1)} %get-tuple-element.154), channel_id=1, source_target_pairs={{0,8},{4,12},{8,0},{12,4},{16,24},{20,28},{24,16},{28,20},{1,9},{5... | collective-permute-start | bytes 200 | tf_op jit(solution)/shard_map/ppermute | solution.py:672
  269.5 61.7 %collective-permute-start.14 = (bf16[16,768]{1,0:T(8,128)(2,1)}, bf16[16,768]{1,0:T(8,128)(2,1)S(1)}, u32[]{:S(2)}, u32[]{:S(2)}) collective-permute-start(bf16[16,768]{1,0:T(8,128)(2,1)} %get-tuple-element.55), channel_id=1, source_target_pairs={{0,4},{4,0},{8,12},{12,8},{16,20},{20,16},{24,28},{28,24},{1,5},{5... | collective-permute-start | bytes 73736 | tf_op jit(solution)/shard_map/ppermute | solution.py:672
  270.0 64.3 %collective-permute-start.15 = (bf16[16,768]{1,0:T(8,128)(2,1)}, bf16[16,768]{1,0:T(8,128)(2,1)S(1)}, u32[]{:S(2)}, u32[]{:S(2)}) collective-permute-start(bf16[16,768]{1,0:T(8,128)(2,1)} %get-tuple-element.55), channel_id=1, source_target_pairs={{0,8},{4,12},{8,0},{12,4},{16,24},{20,28},{24,16},{28,20},{1,9},{5... | collective-permute-start | bytes 73736 | tf_op jit(solution)/shard_map/ppermute | solution.py:672
  270.1 65.8 %collective-permute-start.16 = (bf16[16,768]{1,0:T(8,128)(2,1)}, bf16[16,768]{1,0:T(8,128)(2,1)S(1)}, u32[]{:S(2)}, u32[]{:S(2)}) collective-permute-start(bf16[16,768]{1,0:T(8,128)(2,1)} %get-tuple-element.55), channel_id=1, source_target_pairs={{0,12},{4,8},{8,4},{12,0},{16,28},{20,24},{24,20},{28,16},{1,13},{... | collective-permute-start | bytes 73736 | tf_op jit(solution)/shard_map/ppermute | solution.py:672
  273.0 63.0 %collective-permute-start.17 = (bf16[16,768]{1,0:T(8,128)(2,1)}, bf16[16,768]{1,0:T(8,128)(2,1)S(1)}, u32[]{:S(2)}, u32[]{:S(2)}) collective-permute-start(bf16[16,768]{1,0:T(8,128)(2,1)} %get-tuple-element.55), channel_id=1, source_target_pairs={{0,16},{4,20},{8,24},{12,28},{16,0},{20,4},{24,8},{28,12},{1,17},{... | collective-permute-start | bytes 73736 | tf_op jit(solution)/shard_map/ppermute | solution.py:672
  273.6 62.4 %collective-permute-start.18 = (bf16[16,768]{1,0:T(8,128)(2,1)}, bf16[16,768]{1,0:T(8,128)(2,1)S(1)}, u32[]{:S(2)}, u32[]{:S(2)}) collective-permute-start(bf16[16,768]{1,0:T(8,128)(2,1)} %get-tuple-element.55), channel_id=1, source_target_pairs={{0,20},{4,16},{8,28},{12,24},{16,4},{20,0},{24,12},{28,8},{1,21},{... | collective-permute-start | bytes 73736 | tf_op jit(solution)/shard_map/ppermute | solution.py:672
  336.0 92.0 %collective-permute-start.39 = (bf16[2,768,192]{1,2,0:T(8,128)(2,1)}, bf16[2,768,192]{1,2,0:T(8,128)(2,1)}, u32[]{:S(2)}, u32[]{:S(2)}) collective-permute-start(bf16[2,768,192]{1,2,0:T(8,128)(2,1)} %bitcast.50), channel_id=1, source_target_pairs={{0,1},{1,0},{2,3},{3,2},{4,5},{5,4},{6,7},{7,6},{8,9},{9,8},{10,11... | collective-permute-start | bytes 1769480 | tf_op jit(solution)/shard_map/ppermute | solution.py:672
  374.7 27.8 %collective-permute-start.23 = (f32[3,768]{1,0:T(4,128)S(1)}, f32[3,768]{1,0:T(4,128)S(1)}, u32[]{:S(2)}, u32[]{:S(2)}) collective-permute-start(f32[3,768]{1,0:T(4,128)S(1)} %pad_maximum_fusion), channel_id=1, source_target_pairs={{0,1},{1,0},{2,3},{3,2},{4,5},{5,4},{6,7},{7,6},{8,9},{9,8},{10,11... | collective-permute-start | bytes 27656 | tf_op jit(solution)/shard_map/ppermute | solution.py:672
  374.8 27.7 %collective-permute-start.24 = (f32[3,768]{1,0:T(4,128)S(1)}, f32[3,768]{1,0:T(4,128)S(1)}, u32[]{:S(2)}, u32[]{:S(2)}) collective-permute-start(f32[3,768]{1,0:T(4,128)S(1)} %pad_maximum_fusion), channel_id=1, source_target_pairs={{0,2},{1,3},{2,0},{3,1},{4,6},{5,7},{6,4},{7,5},{8,10},{9,11},{10,... | collective-permute-start | bytes 27656 | tf_op jit(solution)/shard_map/ppermute | solution.py:672
  376.3 26.2 %collective-permute-start.25 = (f32[3,768]{1,0:T(4,128)S(1)}, f32[3,768]{1,0:T(4,128)S(1)}, u32[]{:S(2)}, u32[]{:S(2)}) collective-permute-start(f32[3,768]{1,0:T(4,128)S(1)} %pad_maximum_fusion), channel_id=1, source_target_pairs={{0,3},{1,2},{2,1},{3,0},{4,7},{5,6},{6,5},{7,4},{8,11},{9,10},{10,... | collective-permute-start | bytes 27656 | tf_op jit(solution)/shard_map/ppermute | solution.py:672
  402.6 13.8 %collective-permute-start.26 = (f32[3,96]{1,0:T(4,128)S(1)}, f32[3,96]{1,0:T(4,128)S(1)}, u32[]{:S(2)}, u32[]{:S(2)}) collective-permute-start(f32[3,96]{1,0:T(4,128)S(1)} %bitcast.255), channel_id=1, source_target_pairs={{0,4},{4,0},{8,12},{12,8},{16,20},{20,16},{24,28},{28,24},{1,5},{5... | collective-permute-start | bytes 3464 | tf_op jit(solution)/shard_map/ppermute | solution.py:672
  403.3 16.1 %collective-permute-start.27 = (f32[3,96]{1,0:T(4,128)S(1)}, f32[3,96]{1,0:T(4,128)S(1)}, u32[]{:S(2)}, u32[]{:S(2)}) collective-permute-start(f32[3,96]{1,0:T(4,128)S(1)} %bitcast.253), channel_id=1, source_target_pairs={{0,8},{4,12},{8,0},{12,4},{16,24},{20,28},{24,16},{28,20},{1,9},{5... | collective-permute-start | bytes 3464 | tf_op jit(solution)/shard_map/ppermute | solution.py:672
  403.3 17.9 %collective-permute-start.28 = (f32[3,96]{1,0:T(4,128)S(1)}, f32[3,96]{1,0:T(4,128)S(1)}, u32[]{:S(2)}, u32[]{:S(2)}) collective-permute-start(f32[3,96]{1,0:T(4,128)S(1)} %bitcast.252), channel_id=1, source_target_pairs={{0,12},{4,8},{8,4},{12,0},{16,28},{20,24},{24,20},{28,16},{1,13},{... | collective-permute-start | bytes 3464 | tf_op jit(solution)/shard_map/ppermute | solution.py:672
  424.2 30.6 %collective-permute-start.51 = (bf16[2,8,192,384]{3,2,1,0:T(8,128)(2,1)}, bf16[2,8,192,384]{3,2,1,0:T(8,128)(2,1)}, u32[]{:S(2)}, u32[]{:S(2)}) collective-permute-start(bf16[2,8,192,384]{3,2,1,0:T(8,128)(2,1)} %dynamic-slice_bitcast_fusion), channel_id=1, source_target_pairs={{0,1},{1,0},{2,3},{3,2},{4,5},{5,4},{6,7},{7,6},{8,9},{9,8},{10,11... | collective-permute-start | bytes 7077896 | tf_op jit(solution)/shard_map/ppermute | solution.py:672
  424.3 35.8 %collective-permute-start.45 = (bf16[2,768,768]{2,1,0:T(8,128)(2,1)}, bf16[2,768,768]{2,1,0:T(8,128)(2,1)}, u32[]{:S(2)}, u32[]{:S(2)}) collective-permute-start(bf16[2,768,768]{2,1,0:T(8,128)(2,1)} %dynamic-slice_bitcast_fusion.1), channel_id=1, source_target_pairs={{0,1},{1,0},{2,3},{3,2},{4,5},{5,4},{6,7},{7,6},{8,9},{9,8},{10,11... | collective-permute-start | bytes 7077896 | tf_op jit(solution)/shard_map/ppermute | solution.py:672
  424.8 26.3 %collective-permute-start.33 = (bf16[2,768,576]{1,2,0:T(8,128)(2,1)}, bf16[2,768,576]{1,2,0:T(8,128)(2,1)}, u32[]{:S(2)}, u32[]{:S(2)}) collective-permute-start(bf16[2,768,576]{1,2,0:T(8,128)(2,1)} %bitcast.235), channel_id=1, source_target_pairs={{0,1},{1,0},{2,3},{3,2},{4,5},{5,4},{6,7},{7,6},{8,9},{9,8},{10,11... | collective-permute-start | bytes 5308424 | tf_op jit(solution)/shard_map/ppermute | solution.py:672
  448.3 34.2 %collective-permute-start.42 = (bf16[96,192]{0,1:T(8,128)(2,1)}, bf16[96,192]{0,1:T(8,128)(2,1)}, u32[]{:S(2)}, u32[]{:S(2)}) collective-permute-start(bf16[96,192]{0,1:T(8,128)(2,1)} %bitcast.209), channel_id=1, source_target_pairs={{0,8},{4,12},{8,0},{12,4},{16,24},{20,28},{24,16},{28,20},{1,9},{5... | collective-permute-start | bytes 110600 | tf_op jit(solution)/shard_map/ppermute | solution.py:672
  448.3 38.1 %collective-permute-start.43 = (bf16[96,192]{0,1:T(8,128)(2,1)S(1)}, bf16[96,192]{0,1:T(8,128)(2,1)}, u32[]{:S(2)}, u32[]{:S(2)}) collective-permute-start(bf16[96,192]{0,1:T(8,128)(2,1)S(1)} %bitcast.248), channel_id=1, source_target_pairs={{0,16},{4,20},{8,24},{12,28},{16,0},{20,4},{24,8},{28,12},{1,17},{... | collective-permute-start | bytes 110600 | tf_op jit(solution)/shard_map/ppermute | solution.py:672
  451.1 35.4 %collective-permute-start.44 = (bf16[96,192]{0,1:T(8,128)(2,1)S(1)}, bf16[96,192]{0,1:T(8,128)(2,1)}, u32[]{:S(2)}, u32[]{:S(2)}) collective-permute-start(bf16[96,192]{0,1:T(8,128)(2,1)S(1)} %bitcast.249), channel_id=1, source_target_pairs={{0,24},{4,28},{8,16},{12,20},{16,8},{20,12},{24,0},{28,4},{1,25},{... | collective-permute-start | bytes 110600 | tf_op jit(solution)/shard_map/ppermute | solution.py:672
  454.9 22.6 %collective-permute-start.34 = (bf16[768,576]{0,1:T(8,128)(2,1)S(1)}, bf16[768,576]{0,1:T(8,128)(2,1)S(1)}, u32[]{:S(2)}, u32[]{:S(2)}) collective-permute-start(bf16[768,576]{0,1:T(8,128)(2,1)S(1)} %dynamic-slice_bitcast_fusion.4), channel_id=1, source_target_pairs={{0,2},{1,3},{2,0},{3,1},{4,6},{5,7},{6,4},{7,5},{8,10},{9,11},{10,... | collective-permute-start | bytes 2654216 | tf_op jit(solution)/shard_map/ppermute | solution.py:672
  460.1 42.8 %collective-permute-start.52 = (bf16[8,192,384]{2,1,0:T(8,128)(2,1)}, bf16[8,192,384]{2,1,0:T(8,128)(2,1)}, u32[]{:S(2)}, u32[]{:S(2)}) collective-permute-start(bf16[8,192,384]{2,1,0:T(8,128)(2,1)} %dynamic-slice_bitcast_fusion.2), channel_id=1, source_target_pairs={{0,2},{1,3},{2,0},{3,1},{4,6},{5,7},{6,4},{7,5},{8,10},{9,11},{10,... | collective-permute-start | bytes 3538952 | tf_op jit(solution)/shard_map/ppermute | solution.py:672
  477.5 47.2 %collective-permute-start.46 = (bf16[768,768]{1,0:T(8,128)(2,1)}, bf16[768,768]{1,0:T(8,128)(2,1)}, u32[]{:S(2)}, u32[]{:S(2)}) collective-permute-start(bf16[768,768]{1,0:T(8,128)(2,1)} %dynamic-slice_bitcast_fusion.3), channel_id=1, source_target_pairs={{0,2},{1,3},{2,0},{3,1},{4,6},{5,7},{6,4},{7,5},{8,10},{9,11},{10,... | collective-permute-start | bytes 3538952 | tf_op jit(solution)/shard_map/ppermute | solution.py:672
  492.9 34.1 %collective-permute-start.36 = (bf16[96,576]{1,0:T(8,128)(2,1)S(1)}, bf16[96,576]{1,0:T(8,128)(2,1)S(1)}, u32[]{:S(2)}, u32[]{:S(2)}) collective-permute-start(bf16[96,576]{1,0:T(8,128)(2,1)S(1)} %get-tuple-element.132), channel_id=1, source_target_pairs={{0,8},{4,12},{8,0},{12,4},{16,24},{20,28},{24,16},{28,20},{1,9},{5... | collective-permute-start | bytes 331784 | tf_op jit(solution)/shard_map/ppermute | solution.py:672
  493.0 34.0 %collective-permute-start.37 = (bf16[96,576]{1,0:T(8,128)(2,1)S(1)}, bf16[96,576]{1,0:T(8,128)(2,1)S(1)}, u32[]{:S(2)}, u32[]{:S(2)}) collective-permute-start(bf16[96,576]{1,0:T(8,128)(2,1)S(1)} %get-tuple-element.134), channel_id=1, source_target_pairs={{0,16},{4,20},{8,24},{12,28},{16,0},{20,4},{24,8},{28,12},{1,17},{... | collective-permute-start | bytes 331784 | tf_op jit(solution)/shard_map/ppermute | solution.py:672
  495.6 31.3 %collective-permute-start.38 = (bf16[96,576]{1,0:T(8,128)(2,1)S(1)}, bf16[96,576]{1,0:T(8,128)(2,1)S(1)}, u32[]{:S(2)}, u32[]{:S(2)}) collective-permute-start(bf16[96,576]{1,0:T(8,128)(2,1)S(1)} %get-tuple-element.133), channel_id=1, source_target_pairs={{0,24},{4,28},{8,16},{12,20},{16,8},{20,12},{24,0},{28,4},{1,25},{... | collective-permute-start | bytes 331784 | tf_op jit(solution)/shard_map/ppermute | solution.py:672
  504.9 22.8 %collective-permute-start.53 = (bf16[4,192,384]{2,1,0:T(8,128)(2,1)S(1)}, bf16[4,192,384]{2,1,0:T(8,128)(2,1)S(1)}, u32[]{:S(2)}, u32[]{:S(2)}) collective-permute-start(bf16[4,192,384]{2,1,0:T(8,128)(2,1)S(1)} %dynamic-slice_bitcast_fusion.5), channel_id=1, source_target_pairs={{0,4},{4,0},{8,12},{12,8},{16,20},{20,16},{24,28},{28,24},{1,5},{5... | collective-permute-start | bytes 1769480 | tf_op jit(solution)/shard_map/ppermute | solution.py:672
  528.1 14.9 %collective-permute-start.55 = (bf16[192,384]{1,0:T(8,128)(2,1)S(1)}, bf16[192,384]{1,0:T(8,128)(2,1)S(1)}, u32[]{:S(2)}, u32[]{:S(2)}) collective-permute-start(bf16[192,384]{1,0:T(8,128)(2,1)S(1)} %get-tuple-element.128), channel_id=1, source_target_pairs={{0,16},{4,20},{8,24},{12,28},{16,0},{20,4},{24,8},{28,12},{1,17},{... | collective-permute-start | bytes 442376 | tf_op jit(solution)/shard_map/ppermute | solution.py:672
  538.6 13.7 %collective-permute-start.49 = (bf16[96,768]{1,0:T(8,128)(2,1)S(1)}, bf16[96,768]{1,0:T(8,128)(2,1)S(1)}, u32[]{:S(2)}, u32[]{:S(2)}) collective-permute-start(bf16[96,768]{1,0:T(8,128)(2,1)S(1)} %get-tuple-element.131), channel_id=1, source_target_pairs={{0,16},{4,20},{8,24},{12,28},{16,0},{20,4},{24,8},{28,12},{1,17},{... | collective-permute-start | bytes 442376 | tf_op jit(solution)/shard_map/ppermute | solution.py:672
  (42 other events, 382.2 us)

commit v2 on v1

v2 whole, which is shorter than its diff:
```python
import functools

import jax
import jax.numpy as jnp
from jax import lax
from jax.experimental import pallas as pl
from jax.experimental.pallas import tpu as pltpu
from jax.sharding import PartitionSpec as P

H = 12
HD = 64
PAIR = 2 * HD
GROUP = 2
EPS = 1e-05
NEG = -1e30
BASE = 128.0
DIGITS = 3
LANES = 128
FLOAT = jnp.float32
BFLOAT = jnp.bfloat16
VMEM_BYTES = 60 * 1024 * 1024


def params(**kw):
    return pltpu.CompilerParams(vmem_limit_bytes=VMEM_BYTES, **kw)


def cost(flops, moved):
    return pl.CostEstimate(flops=int(flops / 100), transcendentals=0, bytes_accessed=int(moved / 100))


def padded_len(frame_len):
    return -(-(frame_len + 1) // 8) * 8


def whole(shape):
    return pl.BlockSpec(shape, lambda *_: (0,) * len(shape), pipeline_mode=pl.Buffered(1))


def rows_of(height, width, first=0):
    return pl.BlockSpec((height, width), lambda i: (i + first, 0))


def frames_of(pad, width, first=0):
    return pl.BlockSpec((GROUP, pad, width), lambda i: (i + first, 0, 0))


def normalize(values):
    center = values - jnp.mean(values, axis=-1, keepdims=True)
    spread = jnp.mean(center * center, axis=-1, keepdims=True)
    scale_inv = lax.rsqrt(spread + EPS)
    return (center * scale_inv, scale_inv)


def norm_back(grad_normed, normed, scale_inv):
    return scale_inv * (
        grad_normed
        - jnp.mean(grad_normed, axis=-1, keepdims=True)
        - normed * jnp.mean(grad_normed * normed, axis=-1, keepdims=True)
    )


def dot(a, b):
    return jnp.dot(a, b, preferred_element_type=FLOAT)


def dot_nt(a, b):
    return lax.dot_general(a, b, (((1,), (1,)), ((), ())), preferred_element_type=FLOAT)


def dot_tn(a, b):
    return lax.dot_general(a, b, (((0,), (0,)), ((), ())), preferred_element_type=FLOAT)


def load_rows(ref, frame_len):
    values = ref[...].astype(FLOAT)
    count, pad, width = values.shape
    row = lax.broadcasted_iota(jnp.int32, values.shape, 1)
    return jnp.where(row < frame_len, values, 0.0).reshape(count * pad, width)


def project_kernel(frame_len, x_ref, gain_ref, w_ref, proj_ref):
    normed, _ = normalize(load_rows(x_ref, frame_len))
    hidden = (normed * gain_ref[...]).astype(BFLOAT)
    width = hidden.shape[1]
    for part in range(3):
        cols = slice(part * width, (part + 1) * width)
        proj_ref[:, cols] = dot(hidden, w_ref[:, cols]).astype(BFLOAT)


def alias_call(
    kernel, grid, in_specs, args, prior, out_specs, out_shape, name, flops, moved, scratch=()
):
    extra = [] if prior is None else list(prior)

    def body(*refs):
        kernel(*refs[: len(args)], *refs[len(args) + len(extra) :])

    return pl.pallas_call(
        body,
        grid=grid,
        in_specs=in_specs + [pl.BlockSpec(memory_space=pl.ANY)] * len(extra),
        out_specs=out_specs,
        out_shape=out_shape,
        input_output_aliases={len(args) + i: i for i in range(len(extra))},
        scratch_shapes=list(scratch),
        compiler_params=params(),
        cost_estimate=cost(flops, moved),
        name=name,
    )(*args, *extra)


def project(frames_in, gain, qkv, first, steps, prior):
    count, frame_len, width = frames_in.shape
    pad = padded_len(frame_len)
    block = GROUP * pad
    return alias_call(
        functools.partial(project_kernel, frame_len),
        (steps,),
        [frames_of(pad, width, first), whole((width,)), whole(qkv.shape)],
        (frames_in, gain, qkv),
        prior,
        [rows_of(block, 3 * width, first)],
        [jax.ShapeDtypeStruct((count * pad, 3 * width), BFLOAT)],
        "project",
        6 * steps * block * width * width,
        8 * steps * block * width,
    )


def last_rows(rows, change):
    cut = rows.shape[0] - 8
    return jnp.concatenate([rows[:cut], change(rows[cut:], cut)], axis=0)


def token_in(rows, token, frame_len):
    def change(tail, cut):
        row = lax.broadcasted_iota(jnp.int32, tail.shape, 0)
        return jnp.where(row == frame_len - cut, token, tail)

    return last_rows(rows, change)


def one_head(pair, h):
    lane = lax.broadcasted_iota(jnp.int32, pair.shape, 1)
    return jnp.where((lane >= HD) == (h == 1), pair, jnp.zeros_like(pair))


def attend_kernel(
    frame_len, x_ref, proj_ref, token_ref, out_w_ref, expo_ref, mixed_ref, scale_ref, res_ref
):
    width = x_ref.shape[2]
    pad = x_ref.shape[1]
    pairs = width // PAIR

    def hide(tail, cut):
        row = lax.broadcasted_iota(jnp.int32, tail.shape, 0)
        return jnp.where(row <= frame_len - cut, tail, NEG)

    def at(part, j):
        return pl.ds(part * width + j * PAIR, PAIR)

    def weigh(f, j):
        rows = pl.ds(f * pad, pad)
        query = proj_ref[rows, at(0, j)] * 0.125
        key = token_in(proj_ref[rows, at(1, j)], token_ref[f, :, at(0, j)], frame_len)
        for h in range(2):
            scores = last_rows(dot_nt(key, one_head(query, h)), hide)
            expo = jnp.exp(scores - jnp.max(scores, axis=0, keepdims=True)).astype(BFLOAT)
            expo_ref[f, 2 * j + h] = expo

    def mix(f, j):
        rows = pl.ds(f * pad, pad)
        value = token_in(proj_ref[rows, at(2, j)], token_ref[f, :, at(1, j)], frame_len)
        value_t = value.astype(FLOAT).T.astype(BFLOAT)
        outs, scales = [], []
        for h in range(2):
            ones = jnp.ones((8, pad), BFLOAT)
            out = dot(jnp.concatenate([value_t[h * HD : (h + 1) * HD], ones]), expo_ref[f, 2 * j + h])
            scale = 1.0 / out[HD : HD + 1]
            outs.append(out[:HD] * scale)
            scales.append(jnp.broadcast_to(scale, (HD, pad)))
        mixed_ref[rows, at(0, j)] = jnp.concatenate(outs, axis=0).T.astype(BFLOAT)
        scale_ref[rows, at(0, j)] = jnp.concatenate(scales, axis=0).T.astype(BFLOAT)

    units = [(f, j) for j in range(pairs) for f in range(GROUP)]
    for i in range(len(units) + 2):
        if i < len(units):
            weigh(*units[i])
        if i >= 2:
            mix(*units[i - 2])
    res_ref[...] = load_rows(x_ref, frame_len) + dot(mixed_ref[...], out_w_ref[...])


def attend(frames_in, proj, token_kv, out_w):
    count, frame_len, width = frames_in.shape
    pad = padded_len(frame_len)
    block = GROUP * pad
    heads = width // HD
    return pl.pallas_call(
        functools.partial(attend_kernel, frame_len),
        grid=(count // GROUP,),
        in_specs=[
            frames_of(pad, width),
            rows_of(block, 3 * width),
            frames_of(1, 2 * width),
            whole(out_w.shape),
        ],
        out_specs=[
            pl.BlockSpec((GROUP, heads, pad, pad), lambda i: (i, 0, 0, 0)),
            rows_of(block, width),
            rows_of(block, width),
            rows_of(block, width),
        ],
        out_shape=[
            jax.ShapeDtypeStruct((count, heads, pad, pad), BFLOAT),
            jax.ShapeDtypeStruct((count * pad, width), BFLOAT),
            jax.ShapeDtypeStruct((count * pad, width), BFLOAT),
            jax.ShapeDtypeStruct((count * pad, width), FLOAT),
        ],
        compiler_params=params(),
        cost_estimate=cost(25e9, 50e6),
        name="attend",
    )(frames_in, proj, token_kv, out_w)


def mlp_kernel(
    frame_len,
    parts,
    res_ref,
    cot_ref,
    gain_ref,
    up_ref,
    down_ref,
    out_w_ref,
    mixed_ref,
    scale_ref,
    cot_rows_ref,
    second_ref,
    act_ref,
    grad_up_ref,
    branch_ref,
    grad_mixed_ref,
    delta_ref,
    gain_grad_ref,
):
    residual = res_ref[...]
    width = residual.shape[1]
    normed, scale_inv = normalize(residual)
    gain = gain_ref[...]
    second = (normed * gain).astype(BFLOAT)
    second_ref[...] = second
    cot = load_rows(cot_ref, frame_len)
    cot_bf = cot.astype(BFLOAT)
    cot_rows_ref[...] = cot_bf
    grad_second = jnp.zeros_like(residual)
    size = up_ref.shape[1] // parts
    for part in range(parts):
        cols = slice(part * size, (part + 1) * size)
        up_part = dot(second, up_ref[:, cols])
        sigma = 0.5 * jnp.tanh(0.851 * up_part) + 0.5
        gated = up_part * sigma
        act = gated.astype(BFLOAT)
        act_ref[:, cols] = act
        grad_act = dot_nt(cot_bf, down_ref[cols, :])
        grad_up = (grad_act * (sigma + 1.702 * gated * (1.0 - sigma))).astype(BFLOAT)
        grad_up_ref[:, cols] = grad_up
        grad_second = grad_second + dot_nt(grad_up, up_ref[:, cols])
    gain_grad = jnp.sum(grad_second * normed, axis=0, keepdims=True)
    step = pl.program_id(0)
    gain_grad_ref[...] = jnp.where(step == 0, 0.0, gain_grad_ref[...]) + gain_grad
    branch = (cot + norm_back(grad_second * gain, normed, scale_inv)).astype(BFLOAT)
    branch_ref[...] = branch
    grad_mixed = dot_nt(branch, out_w_ref[...]) * scale_ref[...].astype(FLOAT)
    grad_mixed = grad_mixed.astype(BFLOAT)
    grad_mixed_ref[...] = grad_mixed
    heads = delta_ref.shape[1]
    head = lax.broadcasted_iota(jnp.int32, (heads, width), 0)
    lane = lax.broadcasted_iota(jnp.int32, (heads, width), 1)
    of_head = (lane // HD == head).astype(BFLOAT)
    product = grad_mixed * mixed_ref[...]
    pad = delta_ref.shape[2]
    for f in range(GROUP):
        delta_ref[f] = dot_nt(of_head, product[f * pad : (f + 1) * pad])


def mlp(residual, cotangent, gain, up, down, out_w, mixed, scale):
    count, frame_len, width = cotangent.shape
    pad = padded_len(frame_len)
    block = GROUP * pad
    rows = count * pad
    heads = width // HD
    hidden = up.shape[1]
    shape = jax.ShapeDtypeStruct
    return pl.pallas_call(
        functools.partial(mlp_kernel, frame_len, 4),
        grid=(count // GROUP,),
        in_specs=[
            rows_of(block, width),
            frames_of(pad, width),
            whole((width,)),
            whole(up.shape),
            whole(down.shape),
            whole(out_w.shape),
            rows_of(block, width),
            rows_of(block, width),
        ],
        out_specs=[
            rows_of(block, width),
            rows_of(block, width),
            rows_of(block, hidden),
            rows_of(block, hidden),
            rows_of(block, width),
            rows_of(block, width),
            pl.BlockSpec((GROUP, heads, pad), lambda i: (i, 0, 0)),
            pl.BlockSpec((1, width), lambda i: (0, 0)),
        ],
        out_shape=[
            shape((rows, width), BFLOAT),
            shape((rows, width), BFLOAT),
            shape((rows, hidden), BFLOAT),
            shape((rows, hidden), BFLOAT),
            shape((rows, width), BFLOAT),
            shape((rows, width), BFLOAT),
            shape((count, heads, pad), FLOAT),
            shape((1, width), FLOAT),
        ],
        compiler_params=params(),
        cost_estimate=cost(6 * rows * width * hidden, 60e6),
        name="mlp",
    )(residual, cotangent, gain, up, down, out_w, mixed, scale)


def output_kernel(res_ref, act_ref, down_ref, output_ref):
    out = res_ref[...] + dot(act_ref[...], down_ref[...])
    output_ref[...] = out.astype(BFLOAT).reshape(output_ref.shape)


def mlp_output(residual, act, down, shape, first, steps, prior):
    count, frame_len, width = shape
    pad = padded_len(frame_len)
    block = GROUP * pad
    hidden = down.shape[0]
    return alias_call(
        output_kernel,
        (steps,),
        [rows_of(block, width, first), rows_of(block, hidden, first), whole(down.shape)],
        (residual, act, down),
        prior,
        [frames_of(pad, width, first)],
        [jax.ShapeDtypeStruct(shape, BFLOAT)],
        "mlp_output",
        2 * steps * block * width * hidden,
        8 * steps * block * width,
    )


def weight_grad_kernel(core_ref, left_ref, right_ref, *refs):
    send_ref, keep_ref = refs[-2:]
    total = dot_tn(left_ref[...], right_ref[...]).astype(BFLOAT)
    step = pl.program_id(0)

    @pl.when(step < 2)
    def _():
        send_ref[0] = total

    @pl.when(step >= 2)
    def _():
        keep_ref[0] = total


def up_grad(core, left, right, parts, prior):
    rows, width = left.shape
    lanes = right.shape[1] // parts

    def block(i, core_ref):
        return 2 * (i % 2) + jnp.where(i < 2, 1 - core_ref[0], core_ref[0])

    return pl.pallas_call(
        weight_grad_kernel,
        grid_spec=pltpu.PrefetchScalarGridSpec(
            num_scalar_prefetch=1,
            grid=(parts,),
            in_specs=[
                pl.BlockSpec(left.shape, lambda i, c: (0, 0), pipeline_mode=pl.Buffered(1)),
                pl.BlockSpec((rows, lanes), lambda i, c: (0, block(i, c))),
                pl.BlockSpec(memory_space=pl.ANY),
                pl.BlockSpec(memory_space=pl.ANY),
            ],
            out_specs=[
                pl.BlockSpec((1, width, lanes), lambda i, c: (jnp.minimum(i, 1), 0, 0)),
                pl.BlockSpec((1, width, lanes), lambda i, c: (jnp.maximum(i - 2, 0), 0, 0)),
            ],
        ),
        out_shape=[jax.ShapeDtypeStruct(p.shape, BFLOAT) for p in prior],
        input_output_aliases={3: 0, 4: 1},
        compiler_params=params(),
        cost_estimate=cost(2 * left.size * right.shape[1], 2 * (left.size + right.size)),
        name="grad_up",
    )(core, left, right, *prior)


def by_core(core, blocks):
    pairs = [(blocks[2 * y], blocks[2 * y + 1]) for y in range(len(blocks) // 2)]
    first = core == 0
    send = [jnp.where(first, odd, even) for even, odd in pairs]
    return send, [jnp.where(first, even, odd) for even, odd in pairs]


def down_grad_kernel(core_ref, left_ref, right_ref, send_ref, keep_ref):
    total = dot_tn(left_ref[...], right_ref[...]).astype(BFLOAT)
    parts, pieces, height, columns = 2 * send_ref.shape[0], *send_ref.shape[1:]
    for piece in range(pieces):
        cols = slice(piece * columns, (piece + 1) * columns)
        blocks = [total[part * height : (part + 1) * height, cols] for part in range(parts)]
        for ref, values in zip((send_ref, keep_ref), by_core(core_ref[0], blocks)):
            for y, value in enumerate(values):
                ref[y, piece] = value


def down_grad(core, left, right, parts, tile):
    rows, width = left.shape
    tiles = right.shape[1] // tile
    shape = (parts // 2, tiles, width // parts, tile)
    spec = pl.BlockSpec((parts // 2, 2, width // parts, tile), lambda i: (0, i, 0, 0))
    return pl.pallas_call(
        down_grad_kernel,
        grid=(tiles // 2,),
        in_specs=[
            pl.BlockSpec(memory_space=pltpu.SMEM),
            whole(left.shape),
            pl.BlockSpec((rows, 2 * tile), lambda i: (0, i)),
        ],
        out_specs=[spec, spec],
        out_shape=[jax.ShapeDtypeStruct(shape, BFLOAT)] * 2,
        compiler_params=params(),
        cost_estimate=cost(2 * left.size * right.shape[1], 2 * (left.size + right.size)),
        name="grad_down",
    )(core, left, right)


def with_gain(block, gain, lanes):
    column = jnp.broadcast_to(gain, (8, gain.shape[1])).T.astype(BFLOAT)
    blank = jnp.zeros((block.shape[0], lanes - block.shape[1] - 8), BFLOAT)
    return jnp.concatenate([block, column, blank], axis=1)


def store_split(core, total_ref, gain, send_refs, keep_refs):
    halves = send_refs[0].shape[0]
    parts = 2 * halves
    size = total_ref.shape[1] // parts
    lanes = sum(ref.shape[2] for ref in send_refs)
    for y in range(halves):
        blocks = [
            with_gain(total_ref[:, part * size : (part + 1) * size].astype(BFLOAT), gain, lanes)
            for part in (2 * y, 2 * y + 1)
        ]
        for refs, (value,) in zip((send_refs, keep_refs), by_core(core, blocks)):
            offset = 0
            for ref in refs:
                ref[y] = value[:, offset : offset + ref.shape[2]]
                offset += ref.shape[2]


def split_grad_kernel(core_ref, left_ref, right_ref, gain_ref, send_ref, keep_ref, all_ref):
    step = pl.program_id(0)
    tile = right_ref.shape[1]
    all_ref[:, pl.ds(pl.multiple_of(step * tile, tile), tile)] = dot_tn(
        left_ref[...], right_ref[...]
    ).astype(BFLOAT)

    @pl.when(step == pl.num_programs(0) - 1)
    def _():
        store_split(core_ref[0], all_ref, gain_ref[...], [send_ref], [keep_ref])


def split_grad(core, left, right, gain, tile, parts, shape, index, name):
    rows, width = left.shape
    columns = right.shape[1]
    size = -(-columns // parts // LANES) * LANES
    spec = pl.BlockSpec((parts // 2, width, size), lambda i: (0, 0, index))
    return pl.pallas_call(
        split_grad_kernel,
        grid=(columns // tile,),
        in_specs=[
            pl.BlockSpec(memory_space=pltpu.SMEM),
            whole(left.shape),
            pl.BlockSpec((rows, tile), lambda i: (0, i)),
            whole(gain.shape),
        ],
        out_specs=[spec, spec],
        out_shape=[jax.ShapeDtypeStruct(shape, BFLOAT)] * 2,
        scratch_shapes=[pltpu.VMEM((width, columns), BFLOAT)],
        compiler_params=params(),
        cost_estimate=cost(2 * left.size * columns, 2 * (left.size + right.size)),
        name=name,
    )(core, left, right, gain)


def attend_back_kernel(
    frame_len,
    core_ref,
    proj_ref,
    token_ref,
    expo_ref,
    grad_mixed_ref,
    delta_ref,
    x_ref,
    branch_ref,
    message_ref,
    gain_ref,
    w_ref,
    grad_in_ref,
    class_ref,
    message_grad_ref,
    send_0_ref,
    send_1_ref,
    keep_0_ref,
    keep_1_ref,
    scores_ref,
    grad_proj_ref,
    total_ref,
    gain_grad_ref,
):
    pad = expo_ref.shape[2]
    width = grad_mixed_ref.shape[1]
    pairs = width // PAIR
    step = pl.program_id(0)

    @pl.when(step == 0)
    def _():
        total_ref[...] = jnp.zeros_like(total_ref)
        gain_grad_ref[...] = jnp.zeros_like(gain_grad_ref)

    def at(part, j):
        return pl.ds(part * width + j * PAIR, PAIR)

    def weigh(f, j):
        rows = pl.ds(f * pad, pad)
        value = token_in(proj_ref[rows, at(2, j)], token_ref[f, :, at(1, j)], frame_len)
        grad = grad_mixed_ref[rows, at(0, j)]
        for h in range(2):
            head = 2 * j + h
            grad_prob = dot_nt(value, one_head(grad, h)) - delta_ref[f, head : head + 1, :]
            scores_ref[f, head] = expo_ref[f, head] * grad_prob.astype(BFLOAT)

    def mix(f, j):
        rows = pl.ds(f * pad, pad)
        query = proj_ref[rows, at(0, j)]
        key = token_in(proj_ref[rows, at(1, j)], token_ref[f, :, at(0, j)], frame_len)
        grad = grad_mixed_ref[rows, at(0, j)]
        key_t = key.astype(FLOAT).T.astype(BFLOAT)
        grad_query, grad_key, grad_value = [], [], []
        for h in range(2):
            scores = scores_ref[f, 2 * j + h]
            grad_value.append(dot(expo_ref[f, 2 * j + h], one_head(grad, h)))
            grad_key.append(dot(scores, one_head(query, h)))
            grad_query.append(dot(key_t[h * HD : (h + 1) * HD], scores))
        grad_query = jnp.concatenate(grad_query, axis=0).T * 0.125
        grad_proj_ref[rows, at(0, j)] = grad_query.astype(BFLOAT)
        grad_key = (grad_key[0] + grad_key[1]) * 0.125
        grad_proj_ref[rows, at(1, j)] = grad_key.astype(BFLOAT)
        grad_value = grad_value[0] + grad_value[1]
        grad_proj_ref[rows, at(2, j)] = grad_value.astype(BFLOAT)

    units = [(f, j) for j in range(pairs) for f in range(GROUP)]
    for i in range(len(units) + 2):
        if i < len(units):
            weigh(*units[i])
        if i >= 2:
            mix(*units[i - 2])

    values = load_rows(x_ref, frame_len)
    values = jnp.concatenate(
        [
            token_in(values[f * pad : (f + 1) * pad], message_ref[f].astype(FLOAT), frame_len)
            for f in range(GROUP)
        ]
    )
    normed, scale_inv = normalize(values)
    hidden = (normed * gain_ref[...]).astype(BFLOAT)
    for part in range(3):
        cols = slice(part * width, (part + 1) * width)
        total_ref[:, cols] += dot_tn(hidden, grad_proj_ref[:, cols])
    grad = dot_nt(grad_proj_ref[...], w_ref[...])
    gain_grad_ref[...] += jnp.sum(grad * normed, axis=0, keepdims=True)
    total = branch_ref[...].astype(FLOAT) + norm_back(grad * gain_ref[...], normed, scale_inv)
    total = total.reshape(GROUP, pad, width)
    grad_in_ref[...] = total.astype(BFLOAT)
    for f in range(GROUP):
        class_ref[f] = total[f, :1]
        message_grad_ref[f] = total[f, frame_len : frame_len + 1].astype(BFLOAT)

    @pl.when(step == pl.num_programs(0) - 1)
    def _():
        store_split(
            core_ref[0],
            total_ref,
            gain_grad_ref[...],
            [send_0_ref, send_1_ref],
            [keep_0_ref, keep_1_ref],
        )


def attend_back(
    core, proj, token_kv, expo, grad_mixed, delta, frames_in, branch, message, gain, qkv, parts
):
    count, heads, pad, _ = expo.shape
    frame_len, width = frames_in.shape[1:]
    block = GROUP * pad
    lanes = -(-3 * width // parts // LANES) * LANES
    first = lanes // (2 * LANES) * LANES + LANES
    sums = [(parts // 2, width, n) for n in (first, lanes - first)] * 2
    shape = jax.ShapeDtypeStruct
    return pl.pallas_call(
        functools.partial(attend_back_kernel, frame_len),
        grid=(count // GROUP,),
        in_specs=[
            pl.BlockSpec(memory_space=pltpu.SMEM),
            rows_of(block, 3 * width),
            frames_of(1, 2 * width),
            pl.BlockSpec((GROUP, heads, pad, pad), lambda i: (i, 0, 0, 0)),
            rows_of(block, width),
            pl.BlockSpec((GROUP, heads, pad), lambda i: (i, 0, 0)),
            frames_of(pad, width),
            rows_of(block, width),
            frames_of(1, width),
            whole((width,)),
            whole(qkv.shape),
        ],
        out_specs=[frames_of(pad, width), frames_of(1, width), frames_of(1, width)]
        + [whole(s) for s in sums],
        out_shape=[
            shape((count, frame_len, width), BFLOAT),
            shape((count, 1, width), FLOAT),
            shape((count, 1, width), BFLOAT),
        ]
        + [shape(s, BFLOAT) for s in sums],
        scratch_shapes=[
            pltpu.VMEM((GROUP, heads, pad, pad), BFLOAT),
            pltpu.VMEM((block, 3 * width), BFLOAT),
            pltpu.VMEM((width, 3 * width), FLOAT),
            pltpu.VMEM((1, width), FLOAT),
        ],
        compiler_params=params(),
        cost_estimate=cost(45e9, 50e6),
        name="attend_back",
    )(core, proj, token_kv, expo, grad_mixed, delta, frames_in, branch, message, gain, qkv)


def in_turn(count, slots, first, second):
    if slots > 256:

        def both(j, carry):
            first(j)
            second(j)
            return carry

        lax.fori_loop(0, count, both, 0)
        return
    for j in range(count + 2):
        if j < count:
            first(j)
        if j >= 2:
            second(j - 2)


def message_kernel(
    own,
    class_ref,
    weight_ref,
    gain_ref,
    qkv_ref,
    out_w_ref,
    attn_gain_ref,
    key_w_ref,
    value_w_ref,
    start_ref,
    hidden_ref,
    proj_ref,
    prob_ref,
    mixed_ref,
    message_ref,
    token_kv_ref,
):
    width = weight_ref.shape[0]
    start = dot(class_ref[:, :width], weight_ref[...]).astype(BFLOAT)
    start_ref[...] = start
    normed, _ = normalize(start.astype(FLOAT))
    hidden = (normed * gain_ref[...]).astype(BFLOAT)
    hidden_ref[...] = hidden
    proj_ref[...] = dot(hidden, qkv_ref[...]).astype(BFLOAT)
    digits = class_ref[:, width:].astype(FLOAT)
    lane = lax.broadcasted_iota(jnp.int32, digits.shape, 1)
    weights = jnp.where(lane == 0, 1.0, jnp.where(lane == 1, BASE, BASE * BASE))
    digits = jnp.where(lane < DIGITS, digits * weights, 0.0)
    id_col = jnp.sum(digits, axis=1, keepdims=True)
    id_row = jnp.sum(digits.T, axis=0, keepdims=True)
    visible = id_col == id_row

    def at(part, j):
        start = part * width + j * PAIR
        return pl.ds(start if isinstance(j, int) else pl.multiple_of(start, PAIR), PAIR)

    def weigh(j):
        query = proj_ref[:, at(0, j)] * 0.125
        for h in range(2):
            scores = jnp.where(visible, dot_nt(proj_ref[:, at(1, j)], one_head(query, h)), NEG)
            expo = jnp.exp(scores - jnp.max(scores, axis=0, keepdims=True))
            prob = expo * (1.0 / jnp.sum(expo, axis=0, keepdims=True))
            prob_ref[2 * j + h] = prob.astype(BFLOAT)

    def mix(j):
        value_t = proj_ref[:, at(2, j)].astype(FLOAT).T.astype(BFLOAT)
        outs = [dot(value_t[h * HD : (h + 1) * HD], prob_ref[2 * j + h]) for h in range(2)]
        mixed_ref[:, at(0, j)] = jnp.concatenate(outs, axis=0).T.astype(BFLOAT)

    in_turn(width // PAIR, start.shape[0], weigh, mix)
    message = start[:own].astype(FLOAT) + dot(mixed_ref[:own, :], out_w_ref[...])
    message = message.astype(BFLOAT)
    message_ref[...] = message
    normed, _ = normalize(message.astype(FLOAT))
    token_hidden = (normed * attn_gain_ref[...]).astype(BFLOAT)
    token_kv_ref[:, :width] = dot(token_hidden, key_w_ref[...]).astype(BFLOAT)
    token_kv_ref[:, width:] = dot(token_hidden, value_w_ref[...]).astype(BFLOAT)


def message_forward(class_all, own, weight, gain, qkv, out_w, attn_gain, attn_qkv):
    slots = class_all.shape[0]
    width = weight.shape[0]
    heads = width // HD
    shape = jax.ShapeDtypeStruct
    part = lambda index: pl.BlockSpec((width, width), lambda i, index=index: (0, index))
    return pl.pallas_call(
        functools.partial(message_kernel, own),
        grid=(1,),
        in_specs=[
            whole(class_all.shape),
            whole(weight.shape),
            whole((width,)),
            whole(qkv.shape),
            whole(out_w.shape),
            whole((width,)),
            part(1),
            part(2),
        ],
        out_specs=[
            whole((slots, width)),
            whole((slots, width)),
            whole((slots, 3 * width)),
            whole((heads, slots, slots)),
            whole((slots, width)),
            whole((own, width)),
            whole((own, 2 * width)),
        ],
        out_shape=[
            shape((slots, width), BFLOAT),
            shape((slots, width), BFLOAT),
            shape((slots, 3 * width), BFLOAT),
            shape((heads, slots, slots), BFLOAT),
            shape((slots, width), BFLOAT),
            shape((own, width), BFLOAT),
            shape((own, 2 * width), BFLOAT),
        ],
        compiler_params=params(),
        cost_estimate=cost(7e9, 9e6),
        name="message_forward",
    )(
        class_all,
        weight,
        gain,
        qkv,
        out_w,
        attn_gain,
        attn_qkv,
        attn_qkv,
    )


def message_back_kernel(
    own,
    parts,
    together,
    block_ref,
    grad_ref,
    class_ref,
    start_ref,
    hidden_ref,
    proj_ref,
    prob_ref,
    mixed_ref,
    weight_ref,
    gain_ref,
    qkv_ref,
    out_w_ref,
    class_grad_ref,
    sums_ref,
    grad_mixed_ref,
    grad_proj_ref,
    scores_ref,
):
    width = weight_ref.shape[0]
    grad = grad_ref[...]
    j = pl.program_id(0)

    @pl.when(j == 0)
    def _():
        grad_mixed_ref[...] = dot_nt(grad, out_w_ref[...]).astype(BFLOAT)

    def finish():
        grad_proj = grad_proj_ref[...]
        grad_hidden = dot_nt(grad_proj, qkv_ref[...])
        normed, scale_inv = normalize(start_ref[...].astype(FLOAT))
        gain_grad = jnp.sum(grad_hidden * normed, axis=0, keepdims=True)
        back = norm_back(grad_hidden * gain_ref[...], normed, scale_inv)
        start_grad = (grad.astype(FLOAT) + back).astype(BFLOAT)
        class_grad_ref[...] = dot_nt(start_grad[:own], weight_ref[...])
        size = sums_ref.shape[1]
        row = lax.broadcasted_iota(jnp.int32, (size, width), 0)
        column = lax.broadcasted_iota(jnp.int32, (size, width), 1)
        mine = column == row + block_ref[0] * size
        pick = mine.astype(BFLOAT)
        gain_grad = jnp.sum(jnp.where(mine, gain_grad, 0.0), axis=1, keepdims=True)
        lanes = sums_ref.shape[2] - 5 * width // parts
        for part in range(parts):
            sums_ref[part, :, 5 * width // parts :] = jnp.broadcast_to(
                gain_grad, (size, lanes)
            ).astype(BFLOAT)
        offset = 0
        for left, right in (
            (hidden_ref[...], grad_proj),
            (class_ref[:, :width], start_grad),
            (mixed_ref[...], grad),
        ):
            total = dot(dot_nt(pick, left).astype(BFLOAT), right).astype(BFLOAT)
            columns = total.shape[1] // parts
            for part in range(parts):
                sums_ref[part, :, offset : offset + columns] = total[
                    :, part * columns : (part + 1) * columns
                ]
            offset += columns

    def at(part, k):
        if together == 1:
            return pl.ds(pl.multiple_of(part * width + j * PAIR, PAIR), PAIR)
        return pl.ds(part * width + k * PAIR, PAIR)

    def weigh(k):
        value = proj_ref[:, at(2, k)]
        for h in range(2):
            grad_prob = dot_nt(value, one_head(grad_mixed_ref[:, at(0, k)], h))
            prob = prob_ref[2 * k + h].astype(FLOAT)
            part = prob * grad_prob
            scores = part - prob * jnp.sum(part, axis=0, keepdims=True)
            scores_ref[2 * k + h] = scores.astype(BFLOAT)

    def mix(k):
        query, key, grad_m = proj_ref[:, at(0, k)], proj_ref[:, at(1, k)], grad_mixed_ref[:, at(0, k)]
        key_t = key.astype(FLOAT).T.astype(BFLOAT)
        grad_query, grad_key, grad_value = [], [], []
        for h in range(2):
            scores = scores_ref[2 * k + h]
            grad_value.append(dot(prob_ref[2 * k + h], one_head(grad_m, h)))
            grad_key.append(dot(scores, one_head(query, h)))
            grad_query.append(dot(key_t[h * HD : (h + 1) * HD], scores))
        grad_query = jnp.concatenate(grad_query, axis=0).T * 0.125
        grad_proj_ref[:, at(0, k)] = grad_query.astype(BFLOAT)
        grad_proj_ref[:, at(1, k)] = ((grad_key[0] + grad_key[1]) * 0.125).astype(BFLOAT)
        grad_proj_ref[:, at(2, k)] = (grad_value[0] + grad_value[1]).astype(BFLOAT)

    if together == 1:
        weigh(0)
        mix(0)
    else:
        in_turn(together, grad.shape[0], weigh, mix)

    @pl.when(j == pl.num_programs(0) - 1)
    def _():
        finish()


def message_back(block, parts, size, own, grad_all, class_all, saved, weight, gain, qkv, out_w):
    slots, width = grad_all.shape
    start, hidden, proj, prob, mixed = saved
    shape = jax.ShapeDtypeStruct
    sums = (parts, size, -(-(5 * width // parts + 1) // LANES) * LANES)
    together = width // PAIR if slots <= 256 else 1
    args = (grad_all, class_all, start, hidden, proj, prob, mixed, weight, gain, qkv, out_w)
    return pl.pallas_call(
        functools.partial(message_back_kernel, own, parts, together),
        grid=(width // PAIR // together,),
        in_specs=[pl.BlockSpec(memory_space=pltpu.SMEM)]
        + [pl.BlockSpec((2 * together, slots, slots), lambda j: (j, 0, 0)) if a is prob else whole(a.shape) for a in args],
        out_specs=[whole((own, width)), whole(sums)],
        out_shape=[shape((own, width), FLOAT), shape(sums, BFLOAT)],
        scratch_shapes=[
            pltpu.VMEM((slots, width), BFLOAT),
            pltpu.VMEM((slots, 3 * width), BFLOAT),
            pltpu.VMEM((2 * together, slots, slots), BFLOAT),
        ],
        compiler_params=params(),
        cost_estimate=cost(8e9, 9e6),
        name="message_back",
    )(block, *args)


def swap(values, axis, distance):
    return lax.ppermute(values, axis, [(i, i ^ distance) for i in range(lax.axis_size(axis))])


def tied(values, *others):
    return lax.optimization_barrier((values, others))[0]


def pick(values, index, axis=0):
    return lax.dynamic_index_in_dim(values, index, axis, keepdims=False)


def add(*terms):
    total = terms[0].astype(FLOAT)
    for term in terms[1:]:
        total = total + term.astype(FLOAT)
    return total


class Gather:
    def __init__(self, axis, values):
        self.axis, self.values = axis, values
        self.distance, self.left = 1, lax.axis_size(axis)

    def begin(self):
        while self.left > 8:
            self.finish(self.start(2))
        self.got = self.start(2 if self.left == 8 else self.left)

    def start(self, size):
        got = [swap(self.values, self.axis, d * self.distance) for d in range(1, size)]
        self.distance, self.left = self.distance * size, self.left // size
        return got

    def finish(self, got):
        self.values = jnp.concatenate([self.values, *got])

    def end(self, *after):
        self.finish(tied(self.got, *after))
        return self.values


class Sum:
    def __init__(self, values):
        self.values = values

    @classmethod
    def of_cores(cls, sent, kept):
        self = cls(None)
        self.keep, self.sent = kept, sent
        self.got = [swap(sent, "rows", 1)]
        return self

    def begin(self, axis, distance, dim):
        bit = (lax.axis_index(axis) // distance) % 2
        self.keep = pick(self.values, bit, dim)
        self.sent = pick(self.values, 1 - bit, dim)
        self.got = [swap(self.sent, axis, distance)]
        return self.sent

    def end(self, *after):
        self.values = add(*tied(self.got, *after), self.keep).astype(BFLOAT)
        return self.values

    def begin_frames(self, dim=0):
        self.left, self.distance, self.dim = lax.axis_size("frames"), 1, dim
        shape = self.values.shape
        if len(shape) == 2 + dim:
            self.values = self.values.reshape(*shape[:dim], self.left, -1, shape[-1])
        while self.left > 8:
            self.step_frames()
            self.end()
        return self.step_frames()

    def step_frames(self):
        shape, dim = self.values.shape, self.dim
        self.values = self.values.reshape(*shape[:dim], self.left // 2, 2, *shape[dim + 1 :])
        sent = self.begin("frames", self.distance, dim + 1)
        self.left, self.distance = self.left // 2, self.distance * 2
        return sent

    def begin_last(self):
        index = lax.axis_index("frames") // self.distance
        self.keep = pick(self.values, index)
        sent = [pick(self.values, index ^ d) for d in range(1, self.left)]
        self.got = [
            swap(block, "frames", (d + 1) * self.distance) for d, block in enumerate(sent)
        ]
        return sent

    def end_last(self, *after):
        return add(*tied(self.got, *after), self.keep)


def per_device(
    frames_in,
    cotangent,
    video_ids,
    frame_device,
    msg_weight,
    msg_gain,
    msg_qkv,
    msg_out,
    attn_gain,
    attn_qkv,
    attn_out,
    mlp_gain,
    up_weight,
    down_weight,
):
    count, frame_len, width = frames_in.shape
    owners, parts = lax.axis_size("frames"), lax.axis_size("rows")
    hidden_width = up_weight.shape[1]
    own = -(-count // 16) * 16
    steps = count // GROUP
    block_index = lax.axis_index("frames").astype(jnp.int32).reshape(1)
    extra = ((0, own - count), (0, 0))

    ids = (video_ids * owners + frame_device)[:, None]
    base = int(BASE)
    digits = jnp.concatenate([ids % base, ids // base % base, ids // (base * base)], axis=1)
    digits = jnp.pad(digits, ((0, own - count), (0, LANES - DIGITS)), constant_values=-1)
    payload = jnp.concatenate([jnp.pad(frames_in[:, 0, :], extra), digits.astype(BFLOAT)], axis=1)
    gather = Gather("frames", payload)
    gather.begin()
    frames = tied(frames_in, payload)
    early = steps // 2
    projected = project(frames, attn_gain, attn_qkv, 0, early, None)
    gather.end(projected[0])
    gather.begin()
    (proj,) = project(
        tied(frames, gather.values), attn_gain, attn_qkv, early, steps - early, projected
    )
    class_all = gather.end(proj)

    *saved, message, token_kv = message_forward(
        class_all, own, msg_weight, msg_gain, msg_qkv, msg_out, attn_gain, attn_qkv
    )
    token_kv = token_kv[:count, None]
    message = message[:count, None]
    expo, mixed, scale, residual = attend(frames_in, proj, token_kv, attn_out)
    cot, second, act, grad_up, branch, grad_mixed, delta, mlp_gain_grad = mlp(
        residual, cotangent, mlp_gain, up_weight, down_weight, attn_out, mixed, scale
    )

    core = (lax.axis_index("rows") % 2).astype(jnp.int32).reshape(1)
    tile = 3 * LANES
    tiles = hidden_width // tile
    down = Sum.of_cores(*down_grad(core, cot, act, parts, tile))
    lanes = hidden_width // parts
    out_lanes = -(-width // parts // LANES) * LANES
    shape = (parts // 2, width, lanes + out_lanes)
    out_sums = split_grad(
        core,
        tied(mixed, down.sent),
        branch,
        mlp_gain_grad,
        256,
        parts,
        shape,
        lanes // out_lanes,
        "grad_attn_out",
    )
    values = down.end(*out_sums)
    split = tiles * 5 // 8
    down_a, down_b = Sum(values[:, :split]), Sum(values[:, split:])
    sent = down_a.begin("rows", 2, 0)
    up = Sum.of_cores(*up_grad(core, tied(second, sent), grad_up, parts, out_sums))

    def finish_output(first, number, prior, *others):
        return mlp_output(
            tied(residual, *others), act, down_weight, frames_in.shape, first, number, prior
        )

    pieces = (2, 2, steps - 4)
    down_a.end(up.sent)
    output = finish_output(0, pieces[0], None, up.sent, down_b.begin("rows", 2, 0))
    down.values = jnp.concatenate([down_a.values, down_b.end(output)])
    if tiles != owners:
        moved = jnp.swapaxes(down.values, 0, 1).reshape(width // parts, owners, -1)
        down.values = jnp.swapaxes(moved, 0, 1)
    up.end(output)
    sent = [down.begin_frames(), up.begin("rows", 2, 0)]
    grad_in, class_rows, message_grad, *qkv_sums = attend_back(
        core,
        proj,
        token_kv,
        expo,
        tied(grad_mixed, sent),
        delta,
        frames_in,
        branch,
        message,
        attn_gain,
        attn_qkv,
        parts,
    )
    message_grad = jnp.pad(message_grad.reshape(count, width), extra)
    gather = Gather("frames", message_grad)
    gather.begin()
    qkv_a, qkv_b = (Sum.of_cores(qkv_sums[i], qkv_sums[2 + i]) for i in range(2))
    down.end(message_grad)
    values = up.end(message_grad)
    split = values.shape[-1] // 2
    up_a, up_b = Sum(values[..., :split]), Sum(values[..., split:])
    sent = [message_grad, down.begin_last(), up_a.begin_frames()]
    output = finish_output(pieces[0], pieces[1], output, sent)
    gather.end(output)
    gather.begin()
    qkv_a.end(output)
    qkv_b.end(output)
    up_a.end(output)
    sent = [gather.values, qkv_a.begin("rows", 2, 0), qkv_b.begin_frames(1), up_b.begin_frames()]
    grad_down = down.end_last(output).T
    output = finish_output(sum(pieces[:2]), pieces[2], output, sent)
    grad_all = gather.end(output)
    up.values = jnp.concatenate([up_a.values, up_b.end(output)], axis=2)
    up.left, up.distance = up_a.left, up_a.distance
    qkv_a.end(output)
    qkv_b.end(output)
    sent = [up.begin_last(), qkv_a.begin_frames(), qkv_b.begin("rows", 2, 0)]
    class_grad, msg_sums = message_back(
        block_index,
        parts,
        width // owners,
        own,
        tied(grad_all, sent),
        class_all,
        saved,
        msg_weight,
        msg_gain,
        msg_qkv,
        msg_out,
    )
    msg = Sum(msg_sums.reshape(2, 2, *msg_sums.shape[1:]))
    msg.begin("rows", 1, 1)
    qkv = Sum(jnp.concatenate([qkv_a.end(msg_sums), qkv_b.end(msg_sums)], axis=2))
    qkv.left, qkv.distance = qkv_a.left, qkv_a.distance
    qkv.begin_last()
    msg.end()
    msg.begin("rows", 2, 0)
    class_rows = (class_rows[:, 0] + class_grad[:count]).astype(BFLOAT)
    grad_in = lax.dynamic_update_slice(grad_in, class_rows[:, None], (0, 0, 0))
    grad_up = up.end_last(msg_sums)
    msg_total = add(msg.got[0], msg.keep)
    grad_qkv = qkv.end_last()
    third, fourth, fifth = (n * width // parts for n in (3, 4, 5))
    return (
        output[0],
        grad_in,
        msg_total[:, third:fourth],
        msg_total[:, fifth],
        msg_total[:, :third],
        msg_total[:, fourth:fifth],
        grad_qkv[:, third],
        grad_qkv[:, :third],
        grad_up[:, lanes : lanes + width // parts],
        grad_up[:, lanes + width // parts],
        grad_up[:, :lanes],
        grad_down,
    )


def solution(mesh):
    split = P(("frames", "rows"))
    matrix = P("frames", "rows")
    gain = P("frames")
    return jax.shard_map(
        per_device,
        mesh=mesh,
        in_specs=(split, split, split, split) + (P(),) * 10,
        out_specs=(
            split,
            split,
            matrix,
            gain,
            matrix,
            matrix,
            gain,
            matrix,
            matrix,
            gain,
            matrix,
            matrix,
        ),
        check_vma=False,
    )
```

time: 560 us -> 378 us (0.68)
  Pallas kernels: 326 us -> 250 us
  waiting for transfers between devices: 83.9 us -> 23.8 us
  starting transfers between devices: 74.5 us -> 38.3 us
  local copies, waits for them, and re-layouts: 45.7 us -> 29.5 us
  other arithmetic: 21.6 us -> 28.5 us
    ppermute x57 -> x33, waiting for transfers between devices: 83.9 us -> 23.8 us  [swap(): lax.ppermute(values, axis, [(i, i ^ distance) for i in range(lax.axis_siz...]
    pallas_call x1, Pallas kernels: 60 us -> 22.1 us  [attend(): pl.pallas_call(functools.partial(attend_kernel, frame_len), grid=(count /...]
    ppermute x57 -> x33, starting transfers between devices: 74.5 us -> 38.3 us  [swap(): lax.ppermute(values, axis, [(i, i ^ distance) for i in range(lax.axis_siz...]
    pallas_call x8 -> x9, Pallas kernels: 123 us -> 104 us  [the longest x5 48.1 us: alias_call(): pl.pallas_call(body, grid=grid, in_specs=in_specs + [pl.BlockSpec(memory_...]
    pallas_call x1, Pallas kernels: 74.1 us -> 63.5 us  [mlp(): pl.pallas_call(functools.partial(mlp_kernel, frame_len, 4), grid=(count /...]
    dynamic_slice x5 -> x0, local copies, waits for them, and re-layouts: 10.3 us -> none  [pick(): return lax.dynamic_index_in_dim(values, index, axis, keepdims=False)]
    convert_element_type x13 -> x15, other arithmetic: 14 us -> 22.1 us  [end(): self.values = add(*tied(self.got, *after), self.keep).astype(BFLOAT)]
    pallas_call x1, Pallas kernels: 58.9 us -> 53 us  [attend_back(): pl.pallas_call(functools.partial(attend_back_kernel, frame_len), grid=(co...]
  transfers between devices with their start and end apart: 57 -> 33, of which waited for: 19 -> 5; matrix products, arithmetic and copies ran while one was open for 11% -> 11% of each run, Pallas kernels for 22% -> 32%
where the time goes in v2:
time: 378 us; the launch traced here: 371 us
  Pallas kernels  250 us (66%)
  starting transfers between devices  38.3 us (10%)
  local copies, waits for them, and re-layouts  29.5 us (8%)
  other arithmetic  28.5 us (8%)
  waiting for transfers between devices  23.8 us (6%)
    pallas_call x1, Pallas kernels, mlp(): pl.pallas_call(functools.partial(mlp_kernel, frame_len, 4), grid=(count /...  63.5 us
    pallas_call x1, Pallas kernels, attend_back(): pl.pallas_call(functools.partial(attend_back_kernel, frame_len), grid=(co...  53 us
    pallas_call x5, Pallas kernels, alias_call(): pl.pallas_call(body, grid=grid, in_specs=in_specs + [pl.BlockSpec(memory_...  48.1 us
    ppermute x33, starting transfers between devices, swap(): lax.ppermute(values, axis, [(i, i ^ distance) for i in range(lax.axis_siz...  38.3 us
    ppermute x33, waiting for transfers between devices, swap(): lax.ppermute(values, axis, [(i, i ^ distance) for i in range(lax.axis_siz...  23.8 us
    pallas_call x1, Pallas kernels, attend(): pl.pallas_call(functools.partial(attend_kernel, frame_len), grid=(count /...  22.1 us
    convert_element_type x15, other arithmetic, end(): self.values = add(*tied(self.got, *after), self.keep).astype(BFLOAT)  22.1 us
    pallas_call x1, Pallas kernels, up_grad(): pl.pallas_call(weight_grad_kernel, grid_spec=pltpu.PrefetchScalarGridSpec...  20.6 us
  transfers between devices with their start and end apart: 33, of which 5 were waited for; matrix products, arithmetic and copies ran while one was open for 11% of the time, Pallas kernels for 32%

profile of v2, /device:TPU:0, one launch (start us, length us, event | category | flops | bytes accessed | tf_op | source)
XLA Modules:
  0.0 371.3 jit_solution(6294732016505456511)
XLA Ops:
  2.5 3.0 collective-permute-start
  5.5 9.1 %project.2.refs_3_ = bf16[2800,2304]{1,0:T(8,128)(2,1)} custom-call(bf16[14,197,768]{2,1,0:T(8,128)(2,1)} %x_ref.3, f32[768]{0:T(1024)} %gain_ref.6, bf16[768,2304]{1,0:T(8,128)(2,1)} %w_ref.1), custom_call_target="tpu_custom_call" | custom-call | flops 42467328 | bytes 73728 | tf_op jit(solution)/shard_map/project/pallas_call | solution.py:99
  14.6 1.6 collective-permute-start.1
  16.2 2.6 collective-permute-start.2
  19.1 11.1 %project.3.proj_ref = bf16[2800,2304]{1,0:T(8,128)(2,1)} custom-call(bf16[14,197,768]{2,1,0:T(8,128)(2,1)} %x_ref.3, f32[768]{0:T(1024)} %gain_ref.6, bf16[768,2304]{1,0:T(8,128)(2,1)} %w_ref.1, bf16[2800,2304]{1,0:T(8,128)(2,1)} %project.2.refs_3_), custom_call_target="tpu_custom_call", output_to_operand_aliasing={{}: (3, {})} | custom-call | flops 56623104 | bytes 98304 | tf_op jit(solution)/shard_map/project/pallas_call | solution.py:99
  30.9 6.7 %message_forward.1 = (bf16[128,768]{1,0:T(8,128)(2,1)}, bf16[128,768]{1,0:T(8,128)(2,1)}, bf16[128,2304]{1,0:T(8,128)(2,1)}, bf16[12,128,128]{2,1,0:T(8,128)(2,1...) custom-call(bf16[128,896]{1,0:T(8,128)(2,1)} %copy-done.8, ...), custom_call_target="tpu_custom_call" | custom-call | flops 70000000 | bytes 90000 | tf_op jit(solution)/shard_map/message_forward/pallas_call | solution.py:734
  39.1 22.1 %attend.1 = (bf16[14,12,200,200]{3,2,1,0:T(8,128)(2,1)}, bf16[2800,768]{1,0:T(8,128)(2,1)}, bf16[2800,768]{1,0:T(8,128)(2,1)}, f32[2800,768]{1,0:T(8,128)}) custom-call(bf16[14,197,768]{2,1,0:T(8,128)(2,1)} %x_ref.3, bf16[2800,2304]{1,0:T(8,128)(2,1)} %project.3.proj_ref, bf16[14,1,1536]{2,1,0:T(2,128)(2,1)} %copy.58.token_ref, bf16[768,768]{1,0:T(8,128)(2,1)} %out_w_ref.6), custom_call_target="tpu_custom_call" | custom-call | flops 250000000 | bytes 500000 | tf_op jit(solution)/shard_map/attend/pallas_call | solution.py:200
  61.3 63.5 %mlp.1 = (bf16[2800,768]{1,0:T(8,128)(2,1)}, bf16[2800,768]{1,0:T(8,128)(2,1)}, bf16[2800,3072]{1,0:T(8,128)(2,1)}, bf16[2800,3072]{1,0:T(8,128)(2,1)}, bf16[280...) custom-call(f32[2800,768]{1,0:T(8,128)} %get-tuple-element.131.res_ref.refs_0_, ...), custom_call_target="tpu_custom_call" | custom-call | flops 396361728 | bytes 600000 | tf_op jit(solution)/shard_map/mlp/pallas_call | solution.py:295
  124.8 18.9 %grad_down.1 = (bf16[2,8,192,384]{3,2,1,0:T(8,128)(2,1)}, bf16[2,8,192,384]{3,2,1,0:T(8,128)(2,1)}) custom-call(s32[1]{0:T(128)} %bitcast.5.core_ref, bf16[2800,768]{1,0:T(8,128)(2,1)} %get-tuple-element.98.left_ref, bf16[2800,3072]{1,0:T(8,128)(2,1)} %get-tuple-element.99.right_ref.refs_1_), custom_call_target="tpu_custom_call" | custom-call | flops 132120576 | bytes 215040 | tf_op jit(solution)/shard_map/grad_down/pallas_call | solution.py:426
  143.7 8.5 %grad_attn_out.1 = (bf16[2,768,1024]{2,1,0:T(8,128)(2,1)}, bf16[2,768,1024]{2,1,0:T(8,128)(2,1)}) custom-call(s32[1]{0:T(128)} %bitcast.5.core_ref, bf16[2800,768]{1,0:T(8,128)(2,1)} %get-tuple-element.101.mixed_ref.left_ref, bf16[2800,768]{1,0:T(8,128)(2,1)} %get-tuple-element.102.right_ref.branch_ref, f32[1,768]{1,0:T(1,128)} %get-tuple-element.103.gain_ref), custom_call_target="tpu_custom_call" | custom-call | flops 33030144 | bytes 86016 | tf_op jit(solution)/shard_map/grad_attn_out/pallas_call | solution.py:482
  153.6 3.1 add_convert_fusion.1
  158.9 20.6 %grad_up.1 = (bf16[2,768,1024]{2,1,0:T(8,128)(2,1)}, bf16[2,768,1024]{2,1,0:T(8,128)(2,1)}) custom-call(s32[1]{0:T(128)} %bitcast.5.core_ref, bf16[2800,768]{1,0:T(8,128)(2,1)} %get-tuple-element.109.left_ref, bf16[2800,3072]{1,0:T(8,128)(2,1)} %get-tuple-element.110.right_ref, ...), custom_call_target="tpu_custom_call", output_to_operand_aliasing={{0}: (3, {}), {1}: (4, {})} | custom-call | flops 132120576 | bytes 215040 | tf_op jit(solution)/shard_map/grad_up/pallas_call | solution.py:379
  183.3 8.5 %mlp_output.3.refs_3_ = bf16[14,197,768]{2,1,0:T(8,128)(2,1)} custom-call(f32[2800,768]{1,0:T(8,128)} %get-tuple-element.131.res_ref.refs_0_, bf16[2800,3072]{1,0:T(8,128)(2,1)} %get-tuple-element.99.right_ref.refs_1_, bf16[3072,768]{1,0:T(8,128)(2,1)} %refs_2_.9), custom_call_target="tpu_custom_call" | custom-call | flops 37748736 | bytes 49152 | tf_op jit(solution)/shard_map/mlp_output/pallas_call | solution.py:99
  191.7 2.6 collective-permute-done.6
  195.0 4.4 %add_convert_fusion = bf16[2,768,1024]{2,1,0:T(8,128)(2,1)S(1)} fusion(bf16[2,768,1024]{2,1,0:T(8,128)(2,1)} %get-tuple-element.116, bf16[2,768,1024]{2,1,0:T(8,128)(2,1)} %collective-permute-done.7), kind=kLoop, calls=%fused_computation | loop fusion | flops 6291456 | bytes 9437184 | tf_op jit(solution)/shard_map/convert_element_type | solution.py:968
  202.5 7.7 %collective-permute-done.5 = bf16[5,192,384]{2,1,0:T(8,128)(2,1)} collective-permute-done((bf16[5,192,384]{2,1,0:T(8,128)(2,1)}, bf16[5,192,384]{2,1,0:T(8,128)(2,1)}, u32[]{:S(2)}, u32[]{:S(2)}) %collective-permute-start.5) | collective-permute-done | bytes 737312 | tf_op jit(solution)/shard_map/ppermute | solution.py:908
  214.6 53.0 %attend_back.1 = (bf16[14,197,768]{2,1,0:T(8,128)(2,1)}, f32[14,1,768]{2,1,0:T(1,128)}, bf16[14,1,768]{2,1,0:T(2,128)(2,1)}, bf16[2,768,384]{2,1,0:T(8,128)(2,1)...) custom-call(s32[1]{0:T(128)} %bitcast.5.core_ref, ...), custom_call_target="tpu_custom_call" | custom-call | flops 450000000 | bytes 500000 | tf_op jit(solution)/shard_map/attend_back/pallas_call | solution.py:615
  272.2 3.5 collective-permute-start.31
  275.7 2.1 fusion
  278.8 8.5 %mlp_output.4.refs_3_ = bf16[14,197,768]{2,1,0:T(8,128)(2,1)} custom-call(f32[2800,768]{1,0:T(8,128)} %get-tuple-element.131.res_ref.refs_0_, bf16[2800,3072]{1,0:T(8,128)(2,1)} %get-tuple-element.99.right_ref.refs_1_, bf16[3072,768]{1,0:T(8,128)(2,1)} %refs_2_.9, bf16[14,197,768]{2,1,0:T(8,128)(2,1)} %mlp_output.3.refs_3_), custom_call_target="tpu_custom_call", output_to_operand_aliasing={{}: (3, {})} | custom-call | flops 37748736 | bytes 49152 | tf_op jit(solution)/shard_map/mlp_output/pallas_call | solution.py:99
  288.9 1.7 add_convert_fusion.2
  294.8 1.6 collective-permute-start.17
  298.1 3.8 %collective-permute-start.14 = (bf16[32,768]{1,0:T(8,128)(2,1)}, bf16[32,768]{1,0:T(8,128)(2,1)}, u32[]{:S(2)}, u32[]{:S(2)}) collective-permute-start(bf16[32,768]{1,0:T(8,128)(2,1)} %pad_maximum_fusion.2), channel_id=1, source_target_pairs={{0,16},{4,20},{8,24},{12,28},{16,0},{20,4},{24,8},{28,12},{1,17},{... | collective-permute-start | bytes 147464 | tf_op jit(solution)/shard_map/ppermute | solution.py:908
  302.2 1.9 fusion.11
  305.7 10.9 %mlp_output.5 = bf16[14,197,768]{2,1,0:T(8,128)(2,1)} custom-call(f32[2800,768]{1,0:T(8,128)} %get-tuple-element.131.res_ref.refs_0_, bf16[2800,3072]{1,0:T(8,128)(2,1)} %get-tuple-element.99.right_ref.refs_1_, bf16[3072,768]{1,0:T(8,128)(2,1)} %refs_2_.9, bf16[14,197,768]{2,1,0:T(8,128)(2,1)} %mlp_output.4.refs_3_), custom_call_target="tpu_custom_call", output_to_operand_aliasing={{}: (3, {})} | custom-call | flops 56623104 | bytes 73728 | tf_op jit(solution)/shard_map/mlp_output/pallas_call | solution.py:99
  319.5 7.1 %collective-permute-done.19 = bf16[2,4,96,256]{3,2,1,0:T(8,128)(2,1)S(1)} collective-permute-done((bf16[2,4,96,256]{3,2,1,0:T(8,128)(2,1)}, bf16[2,4,96,256]{3,2,1,0:T(8,128)(2,1)S(1)}, u32[]{:S(2)}, u32[]{:S(2)}) %collective-permute-start.19) | collective-permute-done | bytes 393248 | tf_op jit(solution)/shard_map/ppermute | solution.py:908
  328.0 3.5 collective-permute-start.28
  337.5 8.4 %message_back.1 = (f32[16,768]{1,0:T(8,128)}, bf16[4,96,1024]{2,1,0:T(8,128)(2,1)}) custom-call(s32[1]{0:T(128)} %bitcast.26.block_ref, bf16[128,768]{1,0:T(8,128)(2,1)} %copy-done.16, bf16[128,896]{1,0:T(8,128)(2,1)} %copy-done.8, bf16[128,768]{1,0:T(8,128)(2,1)} %get-tuple-element.142.start_ref, bf16[128,768]{1,0:T(8,128)(2,1)} %get-tuple-element.143.hidden_ref, ...), custom_call_target="tpu_custom_call" | custom-call | flops 80000000 | bytes 90000 | tf_op jit(solution)/shard_map/message_back/pallas_call | solution.py:889
  345.9 1.8 dynamic-slice_bitcast_fusion.5
  351.5 1.9 dynamic_update_slice.3
  354.8 3.8 %collective-permute-start.25 = (bf16[96,640]{1,0:T(8,128)(2,1)S(1)}, bf16[96,640]{1,0:T(8,128)(2,1)S(1)}, u32[]{:S(2)}, u32[]{:S(2)}) collective-permute-start(bf16[96,640]{1,0:T(8,128)(2,1)S(1)} %get-tuple-element.170), channel_id=1, source_target_pairs={{0,16},{4,20},{8,24},{12,28},{16,0},{20,4},{24,8},{28,12},{1,17},{... | collective-permute-start | bytes 368648 | tf_op jit(solution)/shard_map/ppermute | solution.py:908
  362.5 5.6 %collective-permute-done.25 = bf16[96,640]{1,0:T(8,128)(2,1)S(1)} collective-permute-done((bf16[96,640]{1,0:T(8,128)(2,1)S(1)}, bf16[96,640]{1,0:T(8,128)(2,1)S(1)}, u32[]{:S(2)}, u32[]{:S(2)}) %collective-permute-start.25) | collective-permute-done | bytes 122912 | tf_op jit(solution)/shard_map/ppermute | solution.py:908
  (158 shorter events, 56.9 us)
Async XLA Ops:
  2.5 12.1 %collective-permute-start = (bf16[16,896]{1,0:T(8,128)(2,1)S(1)}, bf16[16,896]{1,0:T(8,128)(2,1)S(1)}, u32[]{:S(2)}, u32[]{:S(2)}) collective-permute-start(bf16[16,896]{1,0:T(8,128)(2,1)S(1)} %get-tuple-element.174), channel_id=1, source_target_pairs={{0,4},{4,0},{8,12},{12,8},{16,20},{20,16},{24,28},{28,24},{1,5},{5... | collective-permute-start | bytes 86024 | tf_op jit(solution)/shard_map/ppermute | solution.py:908
  14.6 15.5 %collective-permute-start.1 = (bf16[32,896]{1,0:T(8,128)(2,1)S(1)}, bf16[32,896]{1,0:T(8,128)(2,1)S(1)}, u32[]{:S(2)}, u32[]{:S(2)}) collective-permute-start(bf16[32,896]{1,0:T(8,128)(2,1)S(1)} %pad_maximum_fusion.1), channel_id=1, source_target_pairs={{0,8},{4,12},{8,0},{12,4},{16,24},{20,28},{24,16},{28,20},{1,9},{5... | collective-permute-start | bytes 172040 | tf_op jit(solution)/shard_map/ppermute | solution.py:908
  16.2 13.9 %collective-permute-start.2 = (bf16[32,896]{1,0:T(8,128)(2,1)S(1)}, bf16[32,896]{1,0:T(8,128)(2,1)S(1)}, u32[]{:S(2)}, u32[]{:S(2)}) collective-permute-start(bf16[32,896]{1,0:T(8,128)(2,1)S(1)} %pad_maximum_fusion.1), channel_id=1, source_target_pairs={{0,16},{4,20},{8,24},{12,28},{16,0},{20,4},{24,8},{28,12},{1,17},{... | collective-permute-start | bytes 172040 | tf_op jit(solution)/shard_map/ppermute | solution.py:908
  18.8 11.3 %collective-permute-start.3 = (bf16[32,896]{1,0:T(8,128)(2,1)S(1)}, bf16[32,896]{1,0:T(8,128)(2,1)S(1)}, u32[]{:S(2)}, u32[]{:S(2)}) collective-permute-start(bf16[32,896]{1,0:T(8,128)(2,1)S(1)} %pad_maximum_fusion.1), channel_id=1, source_target_pairs={{0,24},{4,28},{8,16},{12,20},{16,8},{20,12},{24,0},{28,4},{1,25},{... | collective-permute-start | bytes 172040 | tf_op jit(solution)/shard_map/ppermute | solution.py:908
  143.7 8.5 %collective-permute-start.4 = (bf16[2,8,192,384]{3,2,1,0:T(8,128)(2,1)}, bf16[2,8,192,384]{3,2,1,0:T(8,128)(2,1)S(1)}, u32[]{:S(2)}, u32[]{:S(2)}) collective-permute-start(bf16[2,8,192,384]{3,2,1,0:T(8,128)(2,1)} %get-tuple-element.100), channel_id=1, source_target_pairs={{0,1},{1,0},{2,3},{3,2},{4,5},{5,4},{6,7},{7,6},{8,9},{9,8},{10,11... | collective-permute-start | bytes 7077896 | tf_op jit(solution)/shard_map/ppermute | solution.py:908
  179.5 14.8 %collective-permute-start.7 = (bf16[2,768,1024]{2,1,0:T(8,128)(2,1)}, bf16[2,768,1024]{2,1,0:T(8,128)(2,1)}, u32[]{:S(2)}, u32[]{:S(2)}) collective-permute-start(bf16[2,768,1024]{2,1,0:T(8,128)(2,1)} %get-tuple-element.111), channel_id=1, source_target_pairs={{0,1},{1,0},{2,3},{3,2},{4,5},{5,4},{6,7},{7,6},{8,9},{9,8},{10,11... | collective-permute-start | bytes 9437192 | tf_op jit(solution)/shard_map/ppermute | solution.py:908
  181.2 13.1 %collective-permute-start.6 = (bf16[3,192,384]{2,1,0:T(8,128)(2,1)S(1)}, bf16[3,192,384]{2,1,0:T(8,128)(2,1)S(1)}, u32[]{:S(2)}, u32[]{:S(2)}) collective-permute-start(bf16[3,192,384]{2,1,0:T(8,128)(2,1)S(1)} %dynamic-slice_bitcast_fusion.4), channel_id=1, source_target_pairs={{0,2},{1,3},{2,0},{3,1},{4,6},{5,7},{6,4},{7,5},{8,10},{9,11},{10,... | collective-permute-start | bytes 1327112 | tf_op jit(solution)/shard_map/ppermute | solution.py:908
  182.8 27.4 %collective-permute-start.5 = (bf16[5,192,384]{2,1,0:T(8,128)(2,1)}, bf16[5,192,384]{2,1,0:T(8,128)(2,1)}, u32[]{:S(2)}, u32[]{:S(2)}) collective-permute-start(bf16[5,192,384]{2,1,0:T(8,128)(2,1)} %dynamic-slice_bitcast_fusion.1), channel_id=1, source_target_pairs={{0,2},{1,3},{2,0},{3,1},{4,6},{5,7},{6,4},{7,5},{8,10},{9,11},{10,... | collective-permute-start | bytes 2211848 | tf_op jit(solution)/shard_map/ppermute | solution.py:908
  200.8 74.9 %collective-permute-start.10 = (bf16[768,1024]{1,0:T(8,128)(2,1)}, bf16[768,1024]{1,0:T(8,128)(2,1)}, u32[]{:S(2)}, u32[]{:S(2)}) collective-permute-start(bf16[768,1024]{1,0:T(8,128)(2,1)} %dynamic-slice_bitcast_fusion), channel_id=1, source_target_pairs={{0,2},{1,3},{2,0},{3,1},{4,6},{5,7},{6,4},{7,5},{8,10},{9,11},{10,... | collective-permute-start | bytes 4718600 | tf_op jit(solution)/shard_map/ppermute | solution.py:908
  213.6 55.4 %collective-permute-start.9 = (bf16[4,192,384]{2,1,0:T(8,128)(2,1)}, bf16[4,192,384]{2,1,0:T(8,128)(2,1)}, u32[]{:S(2)}, u32[]{:S(2)}) collective-permute-start(bf16[4,192,384]{2,1,0:T(8,128)(2,1)} %dynamic-slice_bitcast_fusion.3), channel_id=1, source_target_pairs={{0,4},{4,0},{8,12},{12,8},{16,20},{20,16},{24,28},{28,24},{1,5},{5... | collective-permute-start | bytes 1769480 | tf_op jit(solution)/shard_map/ppermute | solution.py:908
  268.4 18.9 %collective-permute-start.11 = (bf16[2,768,384]{2,1,0:T(8,128)(2,1)}, bf16[2,768,384]{2,1,0:T(8,128)(2,1)}, u32[]{:S(2)}, u32[]{:S(2)}) collective-permute-start(bf16[2,768,384]{2,1,0:T(8,128)(2,1)} %get-tuple-element.125), channel_id=1, source_target_pairs={{0,1},{1,0},{2,3},{3,2},{4,5},{5,4},{6,7},{7,6},{8,9},{9,8},{10,11... | collective-permute-start | bytes 3538952 | tf_op jit(solution)/shard_map/ppermute | solution.py:908
  271.3 26.5 %collective-permute-start.30 = (bf16[192,384]{1,0:T(8,128)(2,1)}, bf16[192,384]{1,0:T(8,128)(2,1)}, u32[]{:S(2)}, u32[]{:S(2)}) collective-permute-start(bf16[192,384]{1,0:T(8,128)(2,1)} %get-tuple-element.167), channel_id=1, source_target_pairs={{0,8},{4,12},{8,0},{12,4},{16,24},{20,28},{24,16},{28,20},{1,9},{5... | collective-permute-start | bytes 442376 | tf_op jit(solution)/shard_map/ppermute | solution.py:908
  272.2 26.0 %collective-permute-start.31 = (bf16[192,384]{1,0:T(8,128)(2,1)}, bf16[192,384]{1,0:T(8,128)(2,1)}, u32[]{:S(2)}, u32[]{:S(2)}) collective-permute-start(bf16[192,384]{1,0:T(8,128)(2,1)} %get-tuple-element.166), channel_id=1, source_target_pairs={{0,16},{4,20},{8,24},{12,28},{16,0},{20,4},{24,8},{28,12},{1,17},{... | collective-permute-start | bytes 442376 | tf_op jit(solution)/shard_map/ppermute | solution.py:908
  275.6 26.3 %collective-permute-start.32 = (bf16[192,384]{1,0:T(8,128)(2,1)}, bf16[192,384]{1,0:T(8,128)(2,1)}, u32[]{:S(2)}, u32[]{:S(2)}) collective-permute-start(bf16[192,384]{1,0:T(8,128)(2,1)} %get-tuple-element.165), channel_id=1, source_target_pairs={{0,24},{4,28},{8,16},{12,20},{16,8},{20,12},{24,0},{28,4},{1,25},{... | collective-permute-start | bytes 442376 | tf_op jit(solution)/shard_map/ppermute | solution.py:908
  275.7 15.8 %collective-permute-start.12 = (bf16[2,768,256]{2,1,0:T(8,128)(2,1)}, bf16[2,768,256]{2,1,0:T(8,128)(2,1)}, u32[]{:S(2)}, u32[]{:S(2)}) collective-permute-start(bf16[2,768,256]{2,1,0:T(8,128)(2,1)} %get-tuple-element.128), channel_id=1, source_target_pairs={{0,1},{1,0},{2,3},{3,2},{4,5},{5,4},{6,7},{7,6},{8,9},{9,8},{10,11... | collective-permute-start | bytes 2359304 | tf_op jit(solution)/shard_map/ppermute | solution.py:908
  291.5 12.6 %collective-permute-start.16 = (bf16[4,96,512]{2,1,0:T(8,128)(2,1)S(1)}, bf16[4,96,512]{2,1,0:T(8,128)(2,1)S(1)}, u32[]{:S(2)}, u32[]{:S(2)}) collective-permute-start(bf16[4,96,512]{2,1,0:T(8,128)(2,1)S(1)} %copy-done.14), channel_id=1, source_target_pairs={{0,4},{4,0},{8,12},{12,8},{16,20},{20,16},{24,28},{28,24},{1,5},{5... | collective-permute-start | bytes 1179656 | tf_op jit(solution)/shard_map/ppermute | solution.py:908
  294.8 22.4 %collective-permute-start.17 = (bf16[4,96,512]{2,1,0:T(8,128)(2,1)}, bf16[4,96,512]{2,1,0:T(8,128)(2,1)}, u32[]{:S(2)}, u32[]{:S(2)}) collective-permute-start(bf16[4,96,512]{2,1,0:T(8,128)(2,1)} %dynamic-slice_bitcast_fusion.6), channel_id=1, source_target_pairs={{0,4},{4,0},{8,12},{12,8},{16,20},{20,16},{24,28},{28,24},{1,5},{5... | collective-permute-start | bytes 1179656 | tf_op jit(solution)/shard_map/ppermute | solution.py:908
  297.8 18.8 %collective-permute-start.13 = (bf16[32,768]{1,0:T(8,128)(2,1)}, bf16[32,768]{1,0:T(8,128)(2,1)}, u32[]{:S(2)}, u32[]{:S(2)}) collective-permute-start(bf16[32,768]{1,0:T(8,128)(2,1)} %pad_maximum_fusion.2), channel_id=1, source_target_pairs={{0,8},{4,12},{8,0},{12,4},{16,24},{20,28},{24,16},{28,20},{1,9},{5... | collective-permute-start | bytes 147464 | tf_op jit(solution)/shard_map/ppermute | solution.py:908
  298.1 19.1 %collective-permute-start.14 = (bf16[32,768]{1,0:T(8,128)(2,1)}, bf16[32,768]{1,0:T(8,128)(2,1)}, u32[]{:S(2)}, u32[]{:S(2)}) collective-permute-start(bf16[32,768]{1,0:T(8,128)(2,1)} %pad_maximum_fusion.2), channel_id=1, source_target_pairs={{0,16},{4,20},{8,24},{12,28},{16,0},{20,4},{24,8},{28,12},{1,17},{... | collective-permute-start | bytes 147464 | tf_op jit(solution)/shard_map/ppermute | solution.py:908
  302.0 15.3 %collective-permute-start.15 = (bf16[32,768]{1,0:T(8,128)(2,1)}, bf16[32,768]{1,0:T(8,128)(2,1)}, u32[]{:S(2)}, u32[]{:S(2)}) collective-permute-start(bf16[32,768]{1,0:T(8,128)(2,1)} %pad_maximum_fusion.2), channel_id=1, source_target_pairs={{0,24},{4,28},{8,16},{12,20},{16,8},{20,12},{24,0},{28,4},{1,25},{... | collective-permute-start | bytes 147464 | tf_op jit(solution)/shard_map/ppermute | solution.py:908
  304.1 30.8 %collective-permute-start.18 = (bf16[768,384]{1,0:T(8,128)(2,1)}, bf16[768,384]{1,0:T(8,128)(2,1)}, u32[]{:S(2)}, u32[]{:S(2)}) collective-permute-start(bf16[768,384]{1,0:T(8,128)(2,1)} %dynamic-slice_bitcast_fusion.2), channel_id=1, source_target_pairs={{0,2},{1,3},{2,0},{3,1},{4,6},{5,7},{6,4},{7,5},{8,10},{9,11},{10,... | collective-permute-start | bytes 1769480 | tf_op jit(solution)/shard_map/ppermute | solution.py:908
  316.6 9.9 %collective-permute-start.19 = (bf16[2,4,96,256]{3,2,1,0:T(8,128)(2,1)}, bf16[2,4,96,256]{3,2,1,0:T(8,128)(2,1)S(1)}, u32[]{:S(2)}, u32[]{:S(2)}) collective-permute-start(bf16[2,4,96,256]{3,2,1,0:T(8,128)(2,1)} %dynamic-slice_bitcast_fusion.7), channel_id=1, source_target_pairs={{0,4},{4,0},{8,12},{12,8},{16,20},{20,16},{24,28},{28,24},{1,5},{5... | collective-permute-start | bytes 1179656 | tf_op jit(solution)/shard_map/ppermute | solution.py:908
  327.4 20.3 %collective-permute-start.27 = (bf16[96,1024]{1,0:T(8,128)(2,1)}, bf16[96,1024]{1,0:T(8,128)(2,1)}, u32[]{:S(2)}, u32[]{:S(2)}) collective-permute-start(bf16[96,1024]{1,0:T(8,128)(2,1)} %get-tuple-element.163), channel_id=1, source_target_pairs={{0,8},{4,12},{8,0},{12,4},{16,24},{20,28},{24,16},{28,20},{1,9},{5... | collective-permute-start | bytes 589832 | tf_op jit(solution)/shard_map/ppermute | solution.py:908
  328.0 19.7 %collective-permute-start.28 = (bf16[96,1024]{1,0:T(8,128)(2,1)}, bf16[96,1024]{1,0:T(8,128)(2,1)}, u32[]{:S(2)}, u32[]{:S(2)}) collective-permute-start(bf16[96,1024]{1,0:T(8,128)(2,1)} %get-tuple-element.164), channel_id=1, source_target_pairs={{0,16},{4,20},{8,24},{12,28},{16,0},{20,4},{24,8},{28,12},{1,17},{... | collective-permute-start | bytes 589832 | tf_op jit(solution)/shard_map/ppermute | solution.py:908
  331.5 16.2 %collective-permute-start.29 = (bf16[96,1024]{1,0:T(8,128)(2,1)}, bf16[96,1024]{1,0:T(8,128)(2,1)}, u32[]{:S(2)}, u32[]{:S(2)}) collective-permute-start(bf16[96,1024]{1,0:T(8,128)(2,1)} %get-tuple-element.162), channel_id=1, source_target_pairs={{0,24},{4,28},{8,16},{12,20},{16,8},{20,12},{24,0},{28,4},{1,25},{... | collective-permute-start | bytes 589832 | tf_op jit(solution)/shard_map/ppermute | solution.py:908
  331.9 15.8 %collective-permute-start.23 = (bf16[4,96,256]{2,1,0:T(8,128)(2,1)S(1)}, bf16[4,96,256]{2,1,0:T(8,128)(2,1)}, u32[]{:S(2)}, u32[]{:S(2)}) collective-permute-start(bf16[4,96,256]{2,1,0:T(8,128)(2,1)S(1)} %dynamic-slice_bitcast_fusion.11), channel_id=1, source_target_pairs={{0,2},{1,3},{2,0},{3,1},{4,6},{5,7},{6,4},{7,5},{8,10},{9,11},{10,... | collective-permute-start | bytes 589832 | tf_op jit(solution)/shard_map/ppermute | solution.py:908
  337.0 16.4 %collective-permute-start.22 = (bf16[4,96,384]{2,1,0:T(8,128)(2,1)}, bf16[4,96,384]{2,1,0:T(8,128)(2,1)}, u32[]{:S(2)}, u32[]{:S(2)}) collective-permute-start(bf16[4,96,384]{2,1,0:T(8,128)(2,1)} %dynamic-slice_bitcast_fusion.9), channel_id=1, source_target_pairs={{0,4},{4,0},{8,12},{12,8},{16,20},{20,16},{24,28},{28,24},{1,5},{5... | collective-permute-start | bytes 884744 | tf_op jit(solution)/shard_map/ppermute | solution.py:908
  347.7 11.2 %collective-permute-start.20 = (bf16[2,96,1024]{2,1,0:T(8,128)(2,1)}, bf16[2,96,1024]{2,1,0:T(8,128)(2,1)}, u32[]{:S(2)}, u32[]{:S(2)}) collective-permute-start(bf16[2,96,1024]{2,1,0:T(8,128)(2,1)} %dynamic-slice_bitcast_fusion.5), channel_id=1, source_target_pairs={{0,1},{1,0},{2,3},{3,2},{4,5},{5,4},{6,7},{7,6},{8,9},{9,8},{10,11... | collective-permute-start | bytes 1179656 | tf_op jit(solution)/shard_map/ppermute | solution.py:908
  354.5 8.0 %collective-permute-start.24 = (bf16[96,640]{1,0:T(8,128)(2,1)S(1)}, bf16[96,640]{1,0:T(8,128)(2,1)S(1)}, u32[]{:S(2)}, u32[]{:S(2)}) collective-permute-start(bf16[96,640]{1,0:T(8,128)(2,1)S(1)} %get-tuple-element.169), channel_id=1, source_target_pairs={{0,8},{4,12},{8,0},{12,4},{16,24},{20,28},{24,16},{28,20},{1,9},{5... | collective-permute-start | bytes 368648 | tf_op jit(solution)/shard_map/ppermute | solution.py:908
  354.8 13.2 %collective-permute-start.25 = (bf16[96,640]{1,0:T(8,128)(2,1)S(1)}, bf16[96,640]{1,0:T(8,128)(2,1)S(1)}, u32[]{:S(2)}, u32[]{:S(2)}) collective-permute-start(bf16[96,640]{1,0:T(8,128)(2,1)S(1)} %get-tuple-element.170), channel_id=1, source_target_pairs={{0,16},{4,20},{8,24},{12,28},{16,0},{20,4},{24,8},{28,12},{1,17},{... | collective-permute-start | bytes 368648 | tf_op jit(solution)/shard_map/ppermute | solution.py:908
  358.6 9.4 %collective-permute-start.26 = (bf16[96,640]{1,0:T(8,128)(2,1)S(1)}, bf16[96,640]{1,0:T(8,128)(2,1)S(1)}, u32[]{:S(2)}, u32[]{:S(2)}) collective-permute-start(bf16[96,640]{1,0:T(8,128)(2,1)S(1)} %get-tuple-element.168), channel_id=1, source_target_pairs={{0,24},{4,28},{8,16},{12,20},{16,8},{20,12},{24,0},{28,4},{1,25},{... | collective-permute-start | bytes 368648 | tf_op jit(solution)/shard_map/ppermute | solution.py:908
  360.1 8.7 %collective-permute-start.21 = (bf16[96,1024]{1,0:T(8,128)(2,1)S(1)}, bf16[96,1024]{1,0:T(8,128)(2,1)S(1)}, u32[]{:S(2)}, u32[]{:S(2)}) collective-permute-start(bf16[96,1024]{1,0:T(8,128)(2,1)S(1)} %dynamic-slice_bitcast_fusion.10), channel_id=1, source_target_pairs={{0,2},{1,3},{2,0},{3,1},{4,6},{5,7},{6,4},{7,5},{8,10},{9,11},{10,... | collective-permute-start | bytes 589832 | tf_op jit(solution)/shard_map/ppermute | solution.py:908
  (21 other events, 99.8 us)

commit v3 on v2

--- a/solution.py
+++ b/solution.py
@@ -2,6 +2,7 @@
 
 import jax
 import jax.numpy as jnp
+import numpy as np
 from jax import lax
 from jax.experimental import pallas as pl
 from jax.experimental.pallas import tpu as pltpu
@@ -173,15 +174,14 @@
         rows = pl.ds(f * pad, pad)
         value = token_in(proj_ref[rows, at(2, j)], token_ref[f, :, at(1, j)], frame_len)
         value_t = value.astype(FLOAT).T.astype(BFLOAT)
-        outs, scales = [], []
+        outs = []
         for h in range(2):
             ones = jnp.ones((8, pad), BFLOAT)
             out = dot(jnp.concatenate([value_t[h * HD : (h + 1) * HD], ones]), expo_ref[f, 2 * j + h])
             scale = 1.0 / out[HD : HD + 1]
             outs.append(out[:HD] * scale)
-            scales.append(jnp.broadcast_to(scale, (HD, pad)))
+            scale_ref[f, 2 * j + h : 2 * j + h + 1, :] = scale
         mixed_ref[rows, at(0, j)] = jnp.concatenate(outs, axis=0).T.astype(BFLOAT)
-        scale_ref[rows, at(0, j)] = jnp.concatenate(scales, axis=0).T.astype(BFLOAT)
 
     units = [(f, j) for j in range(pairs) for f in range(GROUP)]
     for i in range(len(units) + 2):
@@ -189,7 +189,8 @@
             weigh(*units[i])
         if i >= 2:
             mix(*units[i - 2])
-    res_ref[...] = load_rows(x_ref, frame_len) + dot(mixed_ref[...], out_w_ref[...])
+    residual = load_rows(x_ref, frame_len) + dot(mixed_ref[...], out_w_ref[...])
+    res_ref[...] = residual.astype(BFLOAT)
 
 
 def attend(frames_in, proj, token_kv, out_w):
@@ -209,14 +210,14 @@
         out_specs=[
             pl.BlockSpec((GROUP, heads, pad, pad), lambda i: (i, 0, 0, 0)),
             rows_of(block, width),
-            rows_of(block, width),
+            frames_of(heads, pad),
             rows_of(block, width),
         ],
         out_shape=[
             jax.ShapeDtypeStruct((count, heads, pad, pad), BFLOAT),
             jax.ShapeDtypeStruct((count * pad, width), BFLOAT),
+            jax.ShapeDtypeStruct((count, heads, pad), FLOAT),
             jax.ShapeDtypeStruct((count * pad, width), BFLOAT),
-            jax.ShapeDtypeStruct((count * pad, width), FLOAT),
         ],
         compiler_params=params(),
         cost_estimate=cost(25e9, 50e6),
@@ -244,7 +245,7 @@
     delta_ref,
     gain_grad_ref,
 ):
-    residual = res_ref[...]
+    residual = res_ref[...].astype(FLOAT)
     width = residual.shape[1]
     normed, scale_inv = normalize(residual)
     gain = gain_ref[...]
@@ -271,15 +272,20 @@
     gain_grad_ref[...] = jnp.where(step == 0, 0.0, gain_grad_ref[...]) + gain_grad
     branch = (cot + norm_back(grad_second * gain, normed, scale_inv)).astype(BFLOAT)
     branch_ref[...] = branch
-    grad_mixed = dot_nt(branch, out_w_ref[...]) * scale_ref[...].astype(FLOAT)
+    heads, pad = delta_ref.shape[1:]
+    head = lax.broadcasted_iota(jnp.int32, (heads, width), 0)
+    lane = lax.broadcasted_iota(jnp.int32, (heads, width), 1)
+    of_head = (lane // HD == head).astype(FLOAT)
+    scales = []
+    for f in range(GROUP):
+        high = scale_ref[f].astype(BFLOAT).astype(FLOAT)
+        rows = jnp.concatenate([high, scale_ref[f] - high]).astype(BFLOAT)
+        scales.append(dot_tn(rows, jnp.concatenate([of_head, of_head]).astype(BFLOAT)))
+    of_head = of_head.astype(BFLOAT)
+    grad_mixed = dot_nt(branch, out_w_ref[...]) * jnp.concatenate(scales)
     grad_mixed = grad_mixed.astype(BFLOAT)
     grad_mixed_ref[...] = grad_mixed
-    heads = delta_ref.shape[1]
-    head = lax.broadcasted_iota(jnp.int32, (heads, width), 0)
-    lane = lax.broadcasted_iota(jnp.int32, (heads, width), 1)
-    of_head = (lane // HD == head).astype(BFLOAT)
     product = grad_mixed * mixed_ref[...]
-    pad = delta_ref.shape[2]
     for f in range(GROUP):
         delta_ref[f] = dot_nt(of_head, product[f * pad : (f + 1) * pad])
 
@@ -303,7 +309,7 @@
             whole(down.shape),
             whole(out_w.shape),
             rows_of(block, width),
-            rows_of(block, width),
+            frames_of(heads, pad),
         ],
         out_specs=[
             rows_of(block, width),
@@ -332,7 +338,7 @@
 
 
 def output_kernel(res_ref, act_ref, down_ref, output_ref):
-    out = res_ref[...] + dot(act_ref[...], down_ref[...])
+    out = res_ref[...].astype(FLOAT) + dot(act_ref[...], down_ref[...])
     output_ref[...] = out.astype(BFLOAT).reshape(output_ref.shape)
 
 
@@ -912,6 +918,13 @@
     return lax.optimization_barrier((values, others))[0]
 
 
+def meet(outputs, *transfers):
+    outputs, got = lax.optimization_barrier((outputs, [transfer.got for transfer in transfers]))
+    for transfer, values in zip(transfers, got):
+        transfer.got = values
+    return outputs
+
+
 def pick(values, index, axis=0):
     return lax.dynamic_index_in_dim(values, index, axis, keepdims=False)
 
@@ -928,10 +941,10 @@
         self.axis, self.values = axis, values
         self.distance, self.left = 1, lax.axis_size(axis)
 
-    def begin(self):
+    def begin(self, direct=True):
         while self.left > 8:
             self.finish(self.start(2))
-        self.got = self.start(2 if self.left == 8 else self.left)
+        self.got = self.start(self.left if direct and self.left < 8 else 2)
 
     def start(self, size):
         got = [swap(self.values, self.axis, d * self.distance) for d in range(1, size)]
@@ -941,61 +954,77 @@
     def finish(self, got):
         self.values = jnp.concatenate([self.values, *got])
 
-    def end(self, *after):
-        self.finish(tied(self.got, *after))
+    def end(self):
+        self.finish(self.got)
         return self.values
 
 
 class Sum:
-    def __init__(self, values):
-        self.values = values
+    def __init__(self, terms):
+        self.terms = terms
 
     @classmethod
     def of_cores(cls, sent, kept):
-        self = cls(None)
-        self.keep, self.sent = kept, sent
+        self = cls([kept])
+        self.sent = sent
         self.got = [swap(sent, "rows", 1)]
         return self
 
+    def part(self, index):
+        return Sum([term[index] for term in self.terms])
+
+    def total(self):
+        return add(*self.terms)
+
     def begin(self, axis, distance, dim):
         bit = (lax.axis_index(axis) // distance) % 2
-        self.keep = pick(self.values, bit, dim)
-        self.sent = pick(self.values, 1 - bit, dim)
-        self.got = [swap(self.sent, axis, distance)]
-        return self.sent
-
-    def end(self, *after):
-        self.values = add(*tied(self.got, *after), self.keep).astype(BFLOAT)
-        return self.values
+        sent = add(*(pick(term, 1 - bit, dim) for term in self.terms)).astype(BFLOAT)
+        self.terms = [pick(term, bit, dim) for term in self.terms]
+        self.got = [swap(sent, axis, distance)]
+        return sent
+
+    def end(self, apart=False):
+        self.terms = self.got + self.terms
+        if not apart:
+            self.terms = [self.total().astype(BFLOAT)]
 
     def begin_frames(self, dim=0):
         self.left, self.distance, self.dim = lax.axis_size("frames"), 1, dim
-        shape = self.values.shape
+        shape = self.terms[0].shape
         if len(shape) == 2 + dim:
-            self.values = self.values.reshape(*shape[:dim], self.left, -1, shape[-1])
+            shape = (*shape[:dim], self.left, -1, shape[-1])
+            self.terms = [term.reshape(shape) for term in self.terms]
         while self.left > 8:
             self.step_frames()
             self.end()
         return self.step_frames()
 
     def step_frames(self):
-        shape, dim = self.values.shape, self.dim
-        self.values = self.values.reshape(*shape[:dim], self.left // 2, 2, *shape[dim + 1 :])
+        shape, dim = self.terms[0].shape, self.dim
+        shape = (*shape[:dim], self.left // 2, 2, *shape[dim + 1 :])
+        self.terms = [term.reshape(shape) for term in self.terms]
         sent = self.begin("frames", self.distance, dim + 1)
         self.left, self.distance = self.left // 2, self.distance * 2
         return sent
 
     def begin_last(self):
         index = lax.axis_index("frames") // self.distance
-        self.keep = pick(self.values, index)
-        sent = [pick(self.values, index ^ d) for d in range(1, self.left)]
+        sent = [
+            add(*(pick(term, index ^ d) for term in self.terms)).astype(BFLOAT)
+            for d in range(1, self.left)
+        ]
+        self.terms = [pick(term, index) for term in self.terms]
         self.got = [
             swap(block, "frames", (d + 1) * self.distance) for d, block in enumerate(sent)
         ]
         return sent
 
-    def end_last(self, *after):
-        return add(*tied(self.got, *after), self.keep)
+
+def joined(first, second, axis):
+    self = Sum([jnp.concatenate([first.total(), second.total()], axis=axis).astype(BFLOAT)])
+    if hasattr(first, "left"):
+        self.left, self.distance, self.dim = first.left, first.distance, first.dim
+    return self
 
 
 def per_device(
@@ -1031,13 +1060,14 @@
     gather.begin()
     frames = tied(frames_in, payload)
     early = steps // 2
-    projected = project(frames, attn_gain, attn_qkv, 0, early, None)
-    gather.end(projected[0])
+    projected = meet(project(frames, attn_gain, attn_qkv, 0, early, None), gather)
+    gather.end()
     gather.begin()
     (proj,) = project(
         tied(frames, gather.values), attn_gain, attn_qkv, early, steps - early, projected
     )
-    class_all = gather.end(proj)
+    proj = meet(proj, gather)
+    class_all = gather.end()
 
     *saved, message, token_kv = message_forward(
         class_all, own, msg_weight, msg_gain, msg_qkv, msg_out, attn_gain, attn_qkv
@@ -1067,11 +1097,13 @@
         lanes // out_lanes,
         "grad_attn_out",
     )
-    values = down.end(*out_sums)
+    out_sums = meet(out_sums, down)
+    down.end(apart=True)
     split = tiles * 5 // 8
-    down_a, down_b = Sum(values[:, :split]), Sum(values[:, split:])
+    down_a, down_b = down.part(np.s_[:, :split]), down.part(np.s_[:, split:])
     sent = down_a.begin("rows", 2, 0)
-    up = Sum.of_cores(*up_grad(core, tied(second, sent), grad_up, parts, out_sums))
+    up_sums = up_grad(core, tied(second, sent), grad_up, parts, out_sums)
+    up = Sum.of_cores(*meet(up_sums, down_a))
 
     def finish_output(first, number, prior, *others):
         return mlp_output(
@@ -1079,15 +1111,19 @@
         )
 
     pieces = (2, 2, steps - 4)
-    down_a.end(up.sent)
-    output = finish_output(0, pieces[0], None, up.sent, down_b.begin("rows", 2, 0))
-    down.values = jnp.concatenate([down_a.values, down_b.end(output)])
+    down_a.end(apart=True)
+    sent = [up.sent, down_b.begin("rows", 2, 0)]
+    output = meet(finish_output(0, pieces[0], None, sent), down_b, up)
+    down_b.end(apart=True)
+    down = joined(down_a, down_b, 0)
     if tiles != owners:
-        moved = jnp.swapaxes(down.values, 0, 1).reshape(width // parts, owners, -1)
-        down.values = jnp.swapaxes(moved, 0, 1)
-    up.end(output)
-    sent = [down.begin_frames(), up.begin("rows", 2, 0)]
-    grad_in, class_rows, message_grad, *qkv_sums = attend_back(
+        moved = jnp.swapaxes(down.terms[0], 0, 1).reshape(width // parts, owners, -1)
+        down.terms = [jnp.swapaxes(moved, 0, 1)]
+    up.end(apart=True)
+    split = shape[-1] // 2
+    up_a, up_b = up.part(np.s_[..., :split]), up.part(np.s_[..., split:])
+    sent = [down.begin_frames(), up_a.begin("rows", 2, 0), up_b.begin_frames(1)]
+    grads = attend_back(
         core,
         proj,
         token_kv,
@@ -1101,31 +1137,50 @@
         attn_qkv,
         parts,
     )
+    grad_in, class_rows, message_grad, *qkv_sums = meet(grads, down, up_a, up_b)
     message_grad = jnp.pad(message_grad.reshape(count, width), extra)
     gather = Gather("frames", message_grad)
     gather.begin()
     qkv_a, qkv_b = (Sum.of_cores(qkv_sums[i], qkv_sums[2 + i]) for i in range(2))
-    down.end(message_grad)
-    values = up.end(message_grad)
-    split = values.shape[-1] // 2
-    up_a, up_b = Sum(values[..., :split]), Sum(values[..., split:])
-    sent = [message_grad, down.begin_last(), up_a.begin_frames()]
+    for one in (down, up_a, up_b):
+        one.end()
+    gather.got = tied(gather.got, up_a.terms, up_b.terms, down.terms)
+    gather.end()
+    gather.begin(direct=False)
+    sent = [gather.values, down.step_frames(), up_a.begin_frames(), up_b.begin("rows", 2, 0)]
+    sent = meet(sent, qkv_a, qkv_b)
+    qkv_a.end()
+    qkv_b.end()
+    sent = [sent, qkv_a.begin("rows", 2, 0), qkv_b.begin_frames(1)]
     output = finish_output(pieces[0], pieces[1], output, sent)
-    gather.end(output)
-    gather.begin()
-    qkv_a.end(output)
-    qkv_b.end(output)
-    up_a.end(output)
-    sent = [gather.values, qkv_a.begin("rows", 2, 0), qkv_b.begin_frames(1), up_b.begin_frames()]
-    grad_down = down.end_last(output).T
+    output = meet(output, gather, down, up_a, up_b, qkv_a, qkv_b)
+    gather.end()
+    gather.begin(direct=False)
+    down.end(apart=True)
+    up_a.end(apart=True)
+    up_b.end(apart=True)
+    up = joined(up_a, up_b, 2)
+    qkv_a.end()
+    qkv_b.end()
+    sent = [
+        gather.values,
+        down.begin_last(),
+        up.step_frames(),
+        qkv_a.begin_frames(),
+        qkv_b.begin("rows", 2, 0),
+    ]
     output = finish_output(sum(pieces[:2]), pieces[2], output, sent)
-    grad_all = gather.end(output)
-    up.values = jnp.concatenate([up_a.values, up_b.end(output)], axis=2)
-    up.left, up.distance = up_a.left, up_a.distance
-    qkv_a.end(output)
-    qkv_b.end(output)
-    sent = [up.begin_last(), qkv_a.begin_frames(), qkv_b.begin("rows", 2, 0)]
-    class_grad, msg_sums = message_back(
+    output = meet(output, gather, down, up, qkv_a, qkv_b)
+    gather.end()
+    grad_all = gather.values
+    up.end(apart=True)
+    qkv_a.end(apart=True)
+    qkv_b.end(apart=True)
+    qkv = joined(qkv_a, qkv_b, 2)
+    down.end(apart=True)
+    grad_down = down.total().T
+    sent = [up.begin_last(), qkv.begin_last(), grad_down]
+    grads = message_back(
         block_index,
         parts,
         width // owners,
@@ -1138,18 +1193,18 @@
         msg_qkv,
         msg_out,
     )
-    msg = Sum(msg_sums.reshape(2, 2, *msg_sums.shape[1:]))
+    class_grad, msg_sums = meet(grads, up, qkv)
+    msg = Sum([msg_sums.reshape(2, 2, *msg_sums.shape[1:])])
     msg.begin("rows", 1, 1)
-    qkv = Sum(jnp.concatenate([qkv_a.end(msg_sums), qkv_b.end(msg_sums)], axis=2))
-    qkv.left, qkv.distance = qkv_a.left, qkv_a.distance
-    qkv.begin_last()
+    up.end(apart=True)
+    qkv.end(apart=True)
+    grad_up, grad_qkv = up.total(), qkv.total()
+    class_rows = (class_rows[:, 0] + class_grad[:count]).astype(BFLOAT)
+    grad_in = lax.dynamic_update_slice(grad_in, class_rows[:, None], (0, 0, 0))
     msg.end()
     msg.begin("rows", 2, 0)
-    class_rows = (class_rows[:, 0] + class_grad[:count]).astype(BFLOAT)
-    grad_in = lax.dynamic_update_slice(grad_in, class_rows[:, None], (0, 0, 0))
-    grad_up = up.end_last(msg_sums)
-    msg_total = add(msg.got[0], msg.keep)
-    grad_qkv = qkv.end_last()
+    msg.end(apart=True)
+    msg_total = msg.total()
     third, fourth, fifth = (n * width // parts for n in (3, 4, 5))
     return (
         output[0],

time: 378 us -> 357 us (0.944)
  waiting for transfers between devices: 23.8 us -> 13.1 us
  starting transfers between devices: 38.3 us -> 34 us
    ppermute x33 -> x31, waiting for transfers between devices: 23.8 us -> 13.1 us  [swap(): lax.ppermute(values, axis, [(i, i ^ distance) for i in range(lax.axis_siz...]
    convert_element_type x15 -> x14, other arithmetic: 22.1 us -> 11.7 us  [the longest x8 7.33 us: end(): self.terms = [self.total().astype(BFLOAT)]]
    slice x3 -> x7, local copies, waits for them, and re-layouts: 0.36 us -> 9.55 us  [the longest x6 8.85 us: part(): return Sum([term[index] for term in self.terms])]
    another operation x0 -> x5, other arithmetic: none -> 7.28 us
    squeeze x13 -> x10, local copies, waits for them, and re-layouts: 9.89 us -> 4.97 us  [pick(): return lax.dynamic_index_in_dim(values, index, axis, keepdims=False)]
    ppermute x33 -> x31, starting transfers between devices: 38.3 us -> 34 us  [swap(): lax.ppermute(values, axis, [(i, i ^ distance) for i in range(lax.axis_siz...]
    unnamed x49 -> x85, local copies, waits for them, and re-layouts: 9 us -> 5.33 us
  transfers between devices with their start and end apart: 33 -> 31, of which waited for: 5 -> 5; matrix products, arithmetic and copies ran while one was open for 11% -> 8% of each run, Pallas kernels for 32% -> 39%
where the time goes in v3:
time: 357 us; the launch traced here: 350 us
  Pallas kernels  248 us (69%)
  starting transfers between devices  34 us (10%)
  local copies, waits for them, and re-layouts  29.3 us (8%)
  other arithmetic  24.9 us (7%)
  waiting for transfers between devices  13.1 us (4%)
    pallas_call x1, Pallas kernels, mlp(): pl.pallas_call(functools.partial(mlp_kernel, frame_len, 4), grid=(count /...  62.2 us
    pallas_call x1, Pallas kernels, attend_back(): pl.pallas_call(functools.partial(attend_back_kernel, frame_len), grid=(co...  53.1 us
    pallas_call x5, Pallas kernels, alias_call(): pl.pallas_call(body, grid=grid, in_specs=in_specs + [pl.BlockSpec(memory_...  47.6 us
    ppermute x31, starting transfers between devices, swap(): lax.ppermute(values, axis, [(i, i ^ distance) for i in range(lax.axis_siz...  34 us
    pallas_call x1, Pallas kernels, attend(): pl.pallas_call(functools.partial(attend_kernel, frame_len), grid=(count /...  21.5 us
    pallas_call x1, Pallas kernels, up_grad(): pl.pallas_call(weight_grad_kernel, grid_spec=pltpu.PrefetchScalarGridSpec...  20.5 us
    pallas_call x1, Pallas kernels, down_grad(): pl.pallas_call(down_grad_kernel, grid=(tiles // 2,), in_specs=[pl.BlockSp...  18.9 us
    ppermute x31, waiting for transfers between devices, swap(): lax.ppermute(values, axis, [(i, i ^ distance) for i in range(lax.axis_siz...  13.1 us
  transfers between devices with their start and end apart: 31, of which 5 were waited for; matrix products, arithmetic and copies ran while one was open for 8% of the time, Pallas kernels for 39%

profile of v3, /device:TPU:0, one launch (start us, length us, event | category | flops | bytes accessed | tf_op | source)
XLA Modules:
  0.0 350.5 jit_solution(8234992569314816462)
XLA Ops:
  2.5 3.0 collective-permute-start
  5.5 9.1 %project.2.refs_3_ = bf16[2800,2304]{1,0:T(8,128)(2,1)} custom-call(bf16[14,197,768]{2,1,0:T(8,128)(2,1)} %x_ref.3, f32[768]{0:T(1024)} %gain_ref.6, bf16[768,2304]{1,0:T(8,128)(2,1)} %w_ref.1), custom_call_target="tpu_custom_call" | custom-call | flops 42467328 | bytes 73728 | tf_op jit(solution)/shard_map/project/pallas_call | solution.py:100
  14.6 1.6 collective-permute-start.1
  16.2 2.6 collective-permute-start.2
  19.1 11.1 %project.3.proj_ref = bf16[2800,2304]{1,0:T(8,128)(2,1)} custom-call(bf16[14,197,768]{2,1,0:T(8,128)(2,1)} %x_ref.3, f32[768]{0:T(1024)} %gain_ref.6, bf16[768,2304]{1,0:T(8,128)(2,1)} %w_ref.1, bf16[2800,2304]{1,0:T(8,128)(2,1)} %project.2.refs_3_), custom_call_target="tpu_custom_call", output_to_operand_aliasing={{}: (3, {})} | custom-call | flops 56623104 | bytes 98304 | tf_op jit(solution)/shard_map/project/pallas_call | solution.py:100
  30.9 6.7 %message_forward.1 = (bf16[128,768]{1,0:T(8,128)(2,1)}, bf16[128,768]{1,0:T(8,128)(2,1)}, bf16[128,2304]{1,0:T(8,128)(2,1)}, bf16[12,128,128]{2,1,0:T(8,128)(2,1...) custom-call(bf16[128,896]{1,0:T(8,128)(2,1)} %copy-done.20, ...), custom_call_target="tpu_custom_call" | custom-call | flops 70000000 | bytes 90000 | tf_op jit(solution)/shard_map/message_forward/pallas_call | solution.py:740
  39.1 21.5 %attend.1 = (bf16[14,12,200,200]{3,2,1,0:T(8,128)(2,1)}, bf16[2800,768]{1,0:T(8,128)(2,1)}, f32[14,12,200]{2,1,0:T(8,128)}, bf16[2800,768]{1,0:T(8,128)(2,1)}) custom-call(bf16[14,197,768]{2,1,0:T(8,128)(2,1)} %x_ref.3, bf16[2800,2304]{1,0:T(8,128)(2,1)} %project.3.proj_ref, bf16[14,1,1536]{2,1,0:T(2,128)(2,1)} %copy.58.token_ref, bf16[768,768]{1,0:T(8,128)(2,1)} %out_w_ref.6), custom_call_target="tpu_custom_call" | custom-call | flops 250000000 | bytes 500000 | tf_op jit(solution)/shard_map/attend/pallas_call | solution.py:201
  60.7 62.2 %mlp.1 = (bf16[2800,768]{1,0:T(8,128)(2,1)}, bf16[2800,768]{1,0:T(8,128)(2,1)}, bf16[2800,3072]{1,0:T(8,128)(2,1)}, bf16[2800,3072]{1,0:T(8,128)(2,1)}, bf16[280...) custom-call(bf16[2800,768]{1,0:T(8,128)(2,1)} %get-tuple-element.168.res_ref.refs_0_, ...), custom_call_target="tpu_custom_call" | custom-call | flops 396361728 | bytes 600000 | tf_op jit(solution)/shard_map/mlp/pallas_call | solution.py:301
  122.9 18.9 %grad_down.1 = (bf16[2,8,192,384]{3,2,1,0:T(8,128)(2,1)}, bf16[2,8,192,384]{3,2,1,0:T(8,128)(2,1)}) custom-call(s32[1]{0:T(128)} %bitcast.5.core_ref, bf16[2800,768]{1,0:T(8,128)(2,1)} %get-tuple-element.117.left_ref, bf16[2800,3072]{1,0:T(8,128)(2,1)} %get-tuple-element.118.right_ref.refs_1_), custom_call_target="tpu_custom_call" | custom-call | flops 132120576 | bytes 215040 | tf_op jit(solution)/shard_map/grad_down/pallas_call | solution.py:432
  143.4 8.4 %grad_attn_out.1 = (bf16[2,768,1024]{2,1,0:T(8,128)(2,1)}, bf16[2,768,1024]{2,1,0:T(8,128)(2,1)}) custom-call(s32[1]{0:T(128)} %bitcast.5.core_ref, bf16[2800,768]{1,0:T(8,128)(2,1)} %get-tuple-element.120.mixed_ref.left_ref, bf16[2800,768]{1,0:T(8,128)(2,1)} %get-tuple-element.121.right_ref.branch_ref, f32[1,768]{1,0:T(1,128)} %get-tuple-element.122.gain_ref), custom_call_target="tpu_custom_call" | custom-call | flops 33030144 | bytes 86016 | tf_op jit(solution)/shard_map/grad_attn_out/pallas_call | solution.py:488
  155.9 20.5 %grad_up.1 = (bf16[2,768,1024]{2,1,0:T(8,128)(2,1)}, bf16[2,768,1024]{2,1,0:T(8,128)(2,1)}) custom-call(s32[1]{0:T(128)} %bitcast.5.core_ref, bf16[2800,768]{1,0:T(8,128)(2,1)} %get-tuple-element.127.left_ref, bf16[2800,3072]{1,0:T(8,128)(2,1)} %get-tuple-element.128.right_ref, ...), custom_call_target="tpu_custom_call", output_to_operand_aliasing={{0}: (3, {}), {1}: (4, {})} | custom-call | flops 132120576 | bytes 215040 | tf_op jit(solution)/shard_map/grad_up/pallas_call | solution.py:385
  177.9 1.6 slice.67
  181.0 2.3 fusion.2
  183.2 8.4 %mlp_output.3.refs_3_ = bf16[14,197,768]{2,1,0:T(8,128)(2,1)} custom-call(bf16[2800,768]{1,0:T(8,128)(2,1)} %get-tuple-element.168.res_ref.refs_0_, bf16[2800,3072]{1,0:T(8,128)(2,1)} %get-tuple-element.118.right_ref.refs_1_, bf16[3072,768]{1,0:T(8,128)(2,1)} %refs_2_.9), custom_call_target="tpu_custom_call" | custom-call | flops 37748736 | bytes 49152 | tf_op jit(solution)/shard_map/mlp_output/pallas_call | solution.py:100
  192.9 2.7 fusion.40
  195.7 1.5 fusion.5
  205.4 53.1 %attend_back.1 = (bf16[14,197,768]{2,1,0:T(8,128)(2,1)}, f32[14,1,768]{2,1,0:T(1,128)}, bf16[14,1,768]{2,1,0:T(2,128)(2,1)}, bf16[2,768,384]{2,1,0:T(8,128)(2,1)...) custom-call(s32[1]{0:T(128)} %bitcast.5.core_ref, ...), custom_call_target="tpu_custom_call" | custom-call | flops 450000000 | bytes 500000 | tf_op jit(solution)/shard_map/attend_back/pallas_call | solution.py:621
  260.5 1.7 fusion
  265.3 1.8 collective-permute-start.16
  274.0 3.5 %collective-permute-done.14 = bf16[32,768]{1,0:T(8,128)(2,1)} collective-permute-done((bf16[32,768]{1,0:T(8,128)(2,1)S(1)}, bf16[32,768]{1,0:T(8,128)(2,1)}, u32[]{:S(2)}, u32[]{:S(2)}) %collective-permute-start.14) | collective-permute-done | bytes 49184 | tf_op jit(solution)/shard_map/ppermute | solution.py:914
  278.2 8.5 %mlp_output.4.refs_3_ = bf16[14,197,768]{2,1,0:T(8,128)(2,1)} custom-call(bf16[2800,768]{1,0:T(8,128)(2,1)} %get-tuple-element.168.res_ref.refs_0_, bf16[2800,3072]{1,0:T(8,128)(2,1)} %get-tuple-element.118.right_ref.refs_1_, bf16[3072,768]{1,0:T(8,128)(2,1)} %refs_2_.9, bf16[14,197,768]{2,1,0:T(8,128)(2,1)} %mlp_output.3.refs_3_), custom_call_target="tpu_custom_call", output_to_operand_aliasing={{}: (3, {})} | custom-call | flops 37748736 | bytes 49152 | tf_op jit(solution)/shard_map/mlp_output/pallas_call | solution.py:100
  294.1 1.7 collective-permute-start.23
  296.8 3.0 collective-permute-start.21
  300.7 10.6 %mlp_output.5 = bf16[14,197,768]{2,1,0:T(8,128)(2,1)} custom-call(bf16[2800,768]{1,0:T(8,128)(2,1)} %get-tuple-element.168.res_ref.refs_0_, bf16[2800,3072]{1,0:T(8,128)(2,1)} %get-tuple-element.118.right_ref.refs_1_, bf16[3072,768]{1,0:T(8,128)(2,1)} %refs_2_.9, bf16[14,197,768]{2,1,0:T(8,128)(2,1)} %mlp_output.4.refs_3_), custom_call_target="tpu_custom_call", output_to_operand_aliasing={{}: (3, {})} | custom-call | flops 56623104 | bytes 73728 | tf_op jit(solution)/shard_map/mlp_output/pallas_call | solution.py:100
  316.3 2.8 collective-permute-start.27
  319.4 1.9 collective-permute-start.25
  321.4 1.7 fusion.19
  323.1 1.6 pad_maximum_fusion.1.grad_ref
  324.6 8.4 %message_back.1 = (f32[16,768]{1,0:T(8,128)}, bf16[4,96,1024]{2,1,0:T(8,128)(2,1)}) custom-call(s32[1]{0:T(128)} %bitcast.44.block_ref, bf16[128,768]{1,0:T(8,128)(2,1)} %pad_maximum_fusion.1.grad_ref, bf16[128,896]{1,0:T(8,128)(2,1)} %copy-done.20, bf16[128,768]{1,0:T(8,128)(2,1)} %get-tuple-element.179.start_ref, ...), custom_call_target="tpu_custom_call" | custom-call | flops 80000000 | bytes 90000 | tf_op jit(solution)/shard_map/message_back/pallas_call | solution.py:895
  333.2 3.6 %collective-permute-done.25 = bf16[96,1024]{1,0:T(8,128)(2,1)S(1)} collective-permute-done((bf16[96,1024]{1,0:T(8,128)(2,1)S(1)}, bf16[96,1024]{1,0:T(8,128)(2,1)S(1)}, u32[]{:S(2)}, u32[]{:S(2)}) %collective-permute-start.25) | collective-permute-done | bytes 196640 | tf_op jit(solution)/shard_map/ppermute | solution.py:914
  338.5 1.9 dynamic_update_slice.3
  343.4 4.7 %collective-permute-done.30 = bf16[96,1024]{1,0:T(8,128)(2,1)S(1)} collective-permute-done((bf16[96,1024]{1,0:T(8,128)(2,1)S(1)}, bf16[96,1024]{1,0:T(8,128)(2,1)S(1)}, u32[]{:S(2)}, u32[]{:S(2)}) %collective-permute-start.30) | collective-permute-done | bytes 196640 | tf_op jit(solution)/shard_map/ppermute | solution.py:914
  (197 shorter events, 55.9 us)
Async XLA Ops:
  2.5 12.1 %collective-permute-start = (bf16[16,896]{1,0:T(8,128)(2,1)S(1)}, bf16[16,896]{1,0:T(8,128)(2,1)S(1)}, u32[]{:S(2)}, u32[]{:S(2)}) collective-permute-start(bf16[16,896]{1,0:T(8,128)(2,1)S(1)} %get-tuple-element.202), channel_id=1, source_target_pairs={{0,4},{4,0},{8,12},{12,8},{16,20},{20,16},{24,28},{28,24},{1,5},{5... | collective-permute-start | bytes 86024 | tf_op jit(solution)/shard_map/ppermute | solution.py:914
  14.6 15.5 %collective-permute-start.1 = (bf16[32,896]{1,0:T(8,128)(2,1)S(1)}, bf16[32,896]{1,0:T(8,128)(2,1)S(1)}, u32[]{:S(2)}, u32[]{:S(2)}) collective-permute-start(bf16[32,896]{1,0:T(8,128)(2,1)S(1)} %pad_maximum_fusion.3), channel_id=1, source_target_pairs={{0,8},{4,12},{8,0},{12,4},{16,24},{20,28},{24,16},{28,20},{1,9},{5... | collective-permute-start | bytes 172040 | tf_op jit(solution)/shard_map/ppermute | solution.py:914
  16.2 13.9 %collective-permute-start.2 = (bf16[32,896]{1,0:T(8,128)(2,1)S(1)}, bf16[32,896]{1,0:T(8,128)(2,1)S(1)}, u32[]{:S(2)}, u32[]{:S(2)}) collective-permute-start(bf16[32,896]{1,0:T(8,128)(2,1)S(1)} %pad_maximum_fusion.3), channel_id=1, source_target_pairs={{0,16},{4,20},{8,24},{12,28},{16,0},{20,4},{24,8},{28,12},{1,17},{... | collective-permute-start | bytes 172040 | tf_op jit(solution)/shard_map/ppermute | solution.py:914
  18.8 11.3 %collective-permute-start.3 = (bf16[32,896]{1,0:T(8,128)(2,1)S(1)}, bf16[32,896]{1,0:T(8,128)(2,1)S(1)}, u32[]{:S(2)}, u32[]{:S(2)}) collective-permute-start(bf16[32,896]{1,0:T(8,128)(2,1)S(1)} %pad_maximum_fusion.3), channel_id=1, source_target_pairs={{0,24},{4,28},{8,16},{12,20},{16,8},{20,12},{24,0},{28,4},{1,25},{... | collective-permute-start | bytes 172040 | tf_op jit(solution)/shard_map/ppermute | solution.py:914
  141.8 9.9 %collective-permute-start.4 = (bf16[2,8,192,384]{3,2,1,0:T(8,128)(2,1)}, bf16[2,8,192,384]{3,2,1,0:T(8,128)(2,1)}, u32[]{:S(2)}, u32[]{:S(2)}) collective-permute-start(bf16[2,8,192,384]{3,2,1,0:T(8,128)(2,1)} %get-tuple-element.119), channel_id=1, source_target_pairs={{0,1},{1,0},{2,3},{3,2},{4,5},{5,4},{6,7},{7,6},{8,9},{9,8},{10,11... | collective-permute-start | bytes 7077896 | tf_op jit(solution)/shard_map/ppermute | solution.py:914
  154.4 22.1 %collective-permute-start.5 = (bf16[5,192,384]{2,1,0:T(8,128)(2,1)}, bf16[5,192,384]{2,1,0:T(8,128)(2,1)}, u32[]{:S(2)}, u32[]{:S(2)}) collective-permute-start(bf16[5,192,384]{2,1,0:T(8,128)(2,1)} %fusion.12), channel_id=1, source_target_pairs={{0,2},{1,3},{2,0},{3,1},{4,6},{5,7},{6,4},{7,5},{8,10},{9,11},{10,... | collective-permute-start | bytes 2211848 | tf_op jit(solution)/shard_map/ppermute | solution.py:914
  176.4 16.5 %collective-permute-start.7 = (bf16[2,768,1024]{2,1,0:T(8,128)(2,1)}, bf16[2,768,1024]{2,1,0:T(8,128)(2,1)}, u32[]{:S(2)}, u32[]{:S(2)}) collective-permute-start(bf16[2,768,1024]{2,1,0:T(8,128)(2,1)} %get-tuple-element.134), channel_id=1, source_target_pairs={{0,1},{1,0},{2,3},{3,2},{4,5},{5,4},{6,7},{7,6},{8,9},{9,8},{10,11... | collective-permute-start | bytes 9437192 | tf_op jit(solution)/shard_map/ppermute | solution.py:914
  180.4 12.5 %collective-permute-start.6 = (bf16[3,192,384]{2,1,0:T(8,128)(2,1)S(1)}, bf16[3,192,384]{2,1,0:T(8,128)(2,1)}, u32[]{:S(2)}, u32[]{:S(2)}) collective-permute-start(bf16[3,192,384]{2,1,0:T(8,128)(2,1)S(1)} %fusion.14), channel_id=1, source_target_pairs={{0,2},{1,3},{2,0},{3,1},{4,6},{5,7},{6,4},{7,5},{8,10},{9,11},{10,... | collective-permute-start | bytes 1327112 | tf_op jit(solution)/shard_map/ppermute | solution.py:914
  198.3 60.2 %collective-permute-start.10 = (bf16[2,4,96,512]{3,2,1,0:T(8,128)(2,1)}, bf16[2,4,96,512]{3,2,1,0:T(8,128)(2,1)}, u32[]{:S(2)}, u32[]{:S(2)}) collective-permute-start(bf16[2,4,96,512]{3,2,1,0:T(8,128)(2,1)} %fusion.7), channel_id=1, source_target_pairs={{0,4},{4,0},{8,12},{12,8},{16,20},{20,16},{24,28},{28,24},{1,5},{5... | collective-permute-start | bytes 2359304 | tf_op jit(solution)/shard_map/ppermute | solution.py:914
  199.8 58.8 %collective-permute-start.9 = (bf16[768,512]{1,0:T(8,128)(2,1)}, bf16[768,512]{1,0:T(8,128)(2,1)}, u32[]{:S(2)}, u32[]{:S(2)}) collective-permute-start(bf16[768,512]{1,0:T(8,128)(2,1)} %fusion.6), channel_id=1, source_target_pairs={{0,2},{1,3},{2,0},{3,1},{4,6},{5,7},{6,4},{7,5},{8,10},{9,11},{10,... | collective-permute-start | bytes 2359304 | tf_op jit(solution)/shard_map/ppermute | solution.py:914
  203.3 55.3 %collective-permute-start.8 = (bf16[4,192,384]{2,1,0:T(8,128)(2,1)}, bf16[4,192,384]{2,1,0:T(8,128)(2,1)}, u32[]{:S(2)}, u32[]{:S(2)}) collective-permute-start(bf16[4,192,384]{2,1,0:T(8,128)(2,1)} %dynamic-slice_bitcast_fusion.1), channel_id=1, source_target_pairs={{0,4},{4,0},{8,12},{12,8},{16,20},{20,16},{24,28},{28,24},{1,5},{5... | collective-permute-start | bytes 1769480 | tf_op jit(solution)/shard_map/ppermute | solution.py:914
  205.4 55.1 %copy-start.4 = (bf16[2,768,512]{2,1,0:T(8,128)(2,1)S(1)}, bf16[2,768,512]{2,1,0:T(8,128)(2,1)}, u32[]{:S(2)}) copy-start(bf16[2,768,512]{2,1,0:T(8,128)(2,1)} %copy-done.3) | copy-start | bytes 4718596
  259.4 9.7 %collective-permute-start.11 = (bf16[16,768]{1,0:T(8,128)(2,1)S(1)}, bf16[16,768]{1,0:T(8,128)(2,1)S(1)}, u32[]{:S(2)}, u32[]{:S(2)}) collective-permute-start(bf16[16,768]{1,0:T(8,128)(2,1)S(1)} %pad.14), channel_id=1, source_target_pairs={{0,4},{4,0},{8,12},{12,8},{16,20},{20,16},{24,28},{28,24},{1,5},{5... | collective-permute-start | bytes 73736 | tf_op jit(solution)/shard_map/ppermute | solution.py:914
  260.0 9.2 %collective-permute-start.12 = (bf16[2,768,384]{2,1,0:T(8,128)(2,1)}, bf16[2,768,384]{2,1,0:T(8,128)(2,1)S(1)}, u32[]{:S(2)}, u32[]{:S(2)}) collective-permute-start(bf16[2,768,384]{2,1,0:T(8,128)(2,1)} %get-tuple-element.154), channel_id=1, source_target_pairs={{0,1},{1,0},{2,3},{3,2},{4,5},{5,4},{6,7},{7,6},{8,9},{9,8},{10,11... | collective-permute-start | bytes 3538952 | tf_op jit(solution)/shard_map/ppermute | solution.py:914
  260.0 9.2 %collective-permute-start.13 = (bf16[2,768,256]{2,1,0:T(8,128)(2,1)}, bf16[2,768,256]{2,1,0:T(8,128)(2,1)S(1)}, u32[]{:S(2)}, u32[]{:S(2)}) collective-permute-start(bf16[2,768,256]{2,1,0:T(8,128)(2,1)} %get-tuple-element.155), channel_id=1, source_target_pairs={{0,1},{1,0},{2,3},{3,2},{4,5},{5,4},{6,7},{7,6},{8,9},{9,8},{10,11... | collective-permute-start | bytes 2359304 | tf_op jit(solution)/shard_map/ppermute | solution.py:914
  263.1 23.6 %collective-permute-start.17 = (bf16[4,96,512]{2,1,0:T(8,128)(2,1)S(1)}, bf16[4,96,512]{2,1,0:T(8,128)(2,1)}, u32[]{:S(2)}, u32[]{:S(2)}) collective-permute-start(bf16[4,96,512]{2,1,0:T(8,128)(2,1)S(1)} %dynamic-slice_bitcast_fusion.4), channel_id=1, source_target_pairs={{0,2},{1,3},{2,0},{3,1},{4,6},{5,7},{6,4},{7,5},{8,10},{9,11},{10,... | collective-permute-start | bytes 1179656 | tf_op jit(solution)/shard_map/ppermute | solution.py:914
  265.3 21.4 %collective-permute-start.16 = (bf16[4,96,512]{2,1,0:T(8,128)(2,1)S(1)}, bf16[4,96,512]{2,1,0:T(8,128)(2,1)}, u32[]{:S(2)}, u32[]{:S(2)}) collective-permute-start(bf16[4,96,512]{2,1,0:T(8,128)(2,1)S(1)} %dynamic-slice_bitcast_fusion.5), channel_id=1, source_target_pairs={{0,4},{4,0},{8,12},{12,8},{16,20},{20,16},{24,28},{28,24},{1,5},{5... | collective-permute-start | bytes 1179656 | tf_op jit(solution)/shard_map/ppermute | solution.py:914
  270.6 16.3 %collective-permute-start.18 = (bf16[768,384]{1,0:T(8,128)(2,1)}, bf16[768,384]{1,0:T(8,128)(2,1)}, u32[]{:S(2)}, u32[]{:S(2)}) collective-permute-start(bf16[768,384]{1,0:T(8,128)(2,1)} %dynamic-slice_bitcast_fusion), channel_id=1, source_target_pairs={{0,2},{1,3},{2,0},{3,1},{4,6},{5,7},{6,4},{7,5},{8,10},{9,11},{10,... | collective-permute-start | bytes 1769480 | tf_op jit(solution)/shard_map/ppermute | solution.py:914
  272.8 13.9 %collective-permute-start.19 = (bf16[2,4,96,256]{3,2,1,0:T(8,128)(2,1)}, bf16[2,4,96,256]{3,2,1,0:T(8,128)(2,1)}, u32[]{:S(2)}, u32[]{:S(2)}) collective-permute-start(bf16[2,4,96,256]{3,2,1,0:T(8,128)(2,1)} %dynamic-slice_bitcast_fusion.3), channel_id=1, source_target_pairs={{0,4},{4,0},{8,12},{12,8},{16,20},{20,16},{24,28},{28,24},{1,5},{5... | collective-permute-start | bytes 1179656 | tf_op jit(solution)/shard_map/ppermute | solution.py:914
  273.3 4.2 %collective-permute-start.14 = (bf16[32,768]{1,0:T(8,128)(2,1)S(1)}, bf16[32,768]{1,0:T(8,128)(2,1)}, u32[]{:S(2)}, u32[]{:S(2)}) collective-permute-start(bf16[32,768]{1,0:T(8,128)(2,1)S(1)} %pad_maximum_fusion.4), channel_id=1, source_target_pairs={{0,8},{4,12},{8,0},{12,4},{16,24},{20,28},{24,16},{28,20},{1,9},{5... | collective-permute-start | bytes 147464 | tf_op jit(solution)/shard_map/ppermute | solution.py:914
  277.5 9.2 %collective-permute-start.15 = (bf16[2,192,384]{2,1,0:T(8,128)(2,1)}, bf16[2,192,384]{2,1,0:T(8,128)(2,1)}, u32[]{:S(2)}, u32[]{:S(2)}) collective-permute-start(bf16[2,192,384]{2,1,0:T(8,128)(2,1)} %dynamic-slice_bitcast_fusion.7), channel_id=1, source_target_pairs={{0,8},{4,12},{8,0},{12,4},{16,24},{20,28},{24,16},{28,20},{1,9},{5... | collective-permute-start | bytes 884744 | tf_op jit(solution)/shard_map/ppermute | solution.py:914
  290.0 21.3 %collective-permute-start.24 = (bf16[4,96,256]{2,1,0:T(8,128)(2,1)}, bf16[4,96,256]{2,1,0:T(8,128)(2,1)}, u32[]{:S(2)}, u32[]{:S(2)}) collective-permute-start(bf16[4,96,256]{2,1,0:T(8,128)(2,1)} %dynamic-slice_bitcast_fusion.9), channel_id=1, source_target_pairs={{0,2},{1,3},{2,0},{3,1},{4,6},{5,7},{6,4},{7,5},{8,10},{9,11},{10,... | collective-permute-start | bytes 589832 | tf_op jit(solution)/shard_map/ppermute | solution.py:914
  292.2 19.2 %collective-permute-start.22 = (bf16[2,96,1024]{2,1,0:T(8,128)(2,1)S(1)}, bf16[2,96,1024]{2,1,0:T(8,128)(2,1)S(1)}, u32[]{:S(2)}, u32[]{:S(2)}) collective-permute-start(bf16[2,96,1024]{2,1,0:T(8,128)(2,1)S(1)} %fusion.16), channel_id=1, source_target_pairs={{0,8},{4,12},{8,0},{12,4},{16,24},{20,28},{24,16},{28,20},{1,9},{5... | collective-permute-start | bytes 1179656 | tf_op jit(solution)/shard_map/ppermute | solution.py:914
  294.1 17.2 %collective-permute-start.23 = (bf16[4,96,384]{2,1,0:T(8,128)(2,1)}, bf16[4,96,384]{2,1,0:T(8,128)(2,1)S(1)}, u32[]{:S(2)}, u32[]{:S(2)}) collective-permute-start(bf16[4,96,384]{2,1,0:T(8,128)(2,1)} %dynamic-slice_bitcast_fusion.6), channel_id=1, source_target_pairs={{0,4},{4,0},{8,12},{12,8},{16,20},{20,16},{24,28},{28,24},{1,5},{5... | collective-permute-start | bytes 884744 | tf_op jit(solution)/shard_map/ppermute | solution.py:914
  296.8 14.5 %collective-permute-start.21 = (bf16[192,384]{1,0:T(8,128)(2,1)S(1)}, bf16[192,384]{1,0:T(8,128)(2,1)S(1)}, u32[]{:S(2)}, u32[]{:S(2)}) collective-permute-start(bf16[192,384]{1,0:T(8,128)(2,1)S(1)} %fusion.20), channel_id=1, source_target_pairs={{0,16},{4,20},{8,24},{12,28},{16,0},{20,4},{24,8},{28,12},{1,17},{... | collective-permute-start | bytes 442376 | tf_op jit(solution)/shard_map/ppermute | solution.py:914
  300.6 10.7 %collective-permute-start.20 = (bf16[64,768]{1,0:T(8,128)(2,1)S(1)}, bf16[64,768]{1,0:T(8,128)(2,1)}, u32[]{:S(2)}, u32[]{:S(2)}) collective-permute-start(bf16[64,768]{1,0:T(8,128)(2,1)S(1)} %pad_maximum_fusion.2), channel_id=1, source_target_pairs={{0,16},{4,20},{8,24},{12,28},{16,0},{20,4},{24,8},{28,12},{1,17},{... | collective-permute-start | bytes 294920 | tf_op jit(solution)/shard_map/ppermute | solution.py:914
  315.1 18.0 %collective-permute-start.26 = (bf16[96,640]{1,0:T(8,128)(2,1)}, bf16[96,640]{1,0:T(8,128)(2,1)S(1)}, u32[]{:S(2)}, u32[]{:S(2)}) collective-permute-start(bf16[96,640]{1,0:T(8,128)(2,1)} %get-tuple-element.197), channel_id=1, source_target_pairs={{0,8},{4,12},{8,0},{12,4},{16,24},{20,28},{24,16},{28,20},{1,9},{5... | collective-permute-start | bytes 368648 | tf_op jit(solution)/shard_map/ppermute | solution.py:914
  316.3 16.9 %collective-permute-start.27 = (bf16[96,640]{1,0:T(8,128)(2,1)}, bf16[96,640]{1,0:T(8,128)(2,1)S(1)}, u32[]{:S(2)}, u32[]{:S(2)}) collective-permute-start(bf16[96,640]{1,0:T(8,128)(2,1)} %get-tuple-element.198), channel_id=1, source_target_pairs={{0,16},{4,20},{8,24},{12,28},{16,0},{20,4},{24,8},{28,12},{1,17},{... | collective-permute-start | bytes 368648 | tf_op jit(solution)/shard_map/ppermute | solution.py:914
  319.1 14.0 %collective-permute-start.28 = (bf16[96,640]{1,0:T(8,128)(2,1)S(1)}, bf16[96,640]{1,0:T(8,128)(2,1)S(1)}, u32[]{:S(2)}, u32[]{:S(2)}) collective-permute-start(bf16[96,640]{1,0:T(8,128)(2,1)S(1)} %get-tuple-element.196), channel_id=1, source_target_pairs={{0,24},{4,28},{8,16},{12,20},{16,8},{20,12},{24,0},{28,4},{1,25},{... | collective-permute-start | bytes 368648 | tf_op jit(solution)/shard_map/ppermute | solution.py:914
  319.4 17.3 %collective-permute-start.25 = (bf16[96,1024]{1,0:T(8,128)(2,1)S(1)}, bf16[96,1024]{1,0:T(8,128)(2,1)S(1)}, u32[]{:S(2)}, u32[]{:S(2)}) collective-permute-start(bf16[96,1024]{1,0:T(8,128)(2,1)S(1)} %fusion.18), channel_id=1, source_target_pairs={{0,16},{4,20},{8,24},{12,28},{16,0},{20,4},{24,8},{28,12},{1,17},{... | collective-permute-start | bytes 589832 | tf_op jit(solution)/shard_map/ppermute | solution.py:914
  338.4 2.2 collective-permute-start.29
  340.7 7.3 %collective-permute-start.30 = (bf16[96,1024]{1,0:T(8,128)(2,1)S(1)}, bf16[96,1024]{1,0:T(8,128)(2,1)S(1)}, u32[]{:S(2)}, u32[]{:S(2)}) collective-permute-start(bf16[96,1024]{1,0:T(8,128)(2,1)S(1)} %dynamic-slice_bitcast_fusion.8), channel_id=1, source_target_pairs={{0,2},{1,3},{2,0},{3,1},{4,6},{5,7},{6,4},{7,5},{8,10},{9,11},{10,... | collective-permute-start | bytes 589832 | tf_op jit(solution)/shard_map/ppermute | solution.py:914
  (39 other events, 166.1 us)

commit v4 on v3

--- a/solution.py
+++ b/solution.py
@@ -166,7 +166,7 @@
         query = proj_ref[rows, at(0, j)] * 0.125
         key = token_in(proj_ref[rows, at(1, j)], token_ref[f, :, at(0, j)], frame_len)
         for h in range(2):
-            scores = last_rows(dot_nt(key, one_head(query, h)), hide)
+            scores = last_rows(dot_nt(one_head(key, h), query), hide)
             expo = jnp.exp(scores - jnp.max(scores, axis=0, keepdims=True)).astype(BFLOAT)
             expo_ref[f, 2 * j + h] = expo
 
@@ -547,7 +547,7 @@
         grad = grad_mixed_ref[rows, at(0, j)]
         for h in range(2):
             head = 2 * j + h
-            grad_prob = dot_nt(value, one_head(grad, h)) - delta_ref[f, head : head + 1, :]
+            grad_prob = dot_nt(one_head(value, h), grad) - delta_ref[f, head : head + 1, :]
             scores_ref[f, head] = expo_ref[f, head] * grad_prob.astype(BFLOAT)
 
     def mix(f, j):
@@ -673,7 +673,16 @@
 
 def message_kernel(
     own,
-    class_ref,
+    pieces,
+    *refs,
+):
+    gathered = jnp.concatenate([ref[...] for ref in refs[:pieces]])
+    message_body(own, gathered, *refs[pieces:])
+
+
+def message_body(
+    own,
+    gathered,
     weight_ref,
     gain_ref,
     qkv_ref,
@@ -681,6 +690,7 @@
     attn_gain_ref,
     key_w_ref,
     value_w_ref,
+    class_ref,
     start_ref,
     hidden_ref,
     proj_ref,
@@ -690,13 +700,14 @@
     token_kv_ref,
 ):
     width = weight_ref.shape[0]
-    start = dot(class_ref[:, :width], weight_ref[...]).astype(BFLOAT)
+    class_ref[...] = gathered[:, :width]
+    start = dot(gathered[:, :width], weight_ref[...]).astype(BFLOAT)
     start_ref[...] = start
     normed, _ = normalize(start.astype(FLOAT))
     hidden = (normed * gain_ref[...]).astype(BFLOAT)
     hidden_ref[...] = hidden
     proj_ref[...] = dot(hidden, qkv_ref[...]).astype(BFLOAT)
-    digits = class_ref[:, width:].astype(FLOAT)
+    digits = gathered[:, width:].astype(FLOAT)
     lane = lax.broadcasted_iota(jnp.int32, digits.shape, 1)
     weights = jnp.where(lane == 0, 1.0, jnp.where(lane == 1, BASE, BASE * BASE))
     digits = jnp.where(lane < DIGITS, digits * weights, 0.0)
@@ -731,17 +742,17 @@
     token_kv_ref[:, width:] = dot(token_hidden, value_w_ref[...]).astype(BFLOAT)
 
 
-def message_forward(class_all, own, weight, gain, qkv, out_w, attn_gain, attn_qkv):
-    slots = class_all.shape[0]
+def message_forward(class_parts, own, weight, gain, qkv, out_w, attn_gain, attn_qkv):
+    slots = sum(part.shape[0] for part in class_parts)
     width = weight.shape[0]
     heads = width // HD
     shape = jax.ShapeDtypeStruct
     part = lambda index: pl.BlockSpec((width, width), lambda i, index=index: (0, index))
     return pl.pallas_call(
-        functools.partial(message_kernel, own),
+        functools.partial(message_kernel, own, len(class_parts)),
         grid=(1,),
-        in_specs=[
-            whole(class_all.shape),
+        in_specs=[whole(p.shape) for p in class_parts]
+        + [
             whole(weight.shape),
             whole((width,)),
             whole(qkv.shape),
@@ -753,6 +764,7 @@
         out_specs=[
             whole((slots, width)),
             whole((slots, width)),
+            whole((slots, width)),
             whole((slots, 3 * width)),
             whole((heads, slots, slots)),
             whole((slots, width)),
@@ -760,6 +772,7 @@
             whole((own, 2 * width)),
         ],
         out_shape=[
+            shape((slots, width), BFLOAT),
             shape((slots, width), BFLOAT),
             shape((slots, width), BFLOAT),
             shape((slots, 3 * width), BFLOAT),
@@ -772,7 +785,7 @@
         cost_estimate=cost(7e9, 9e6),
         name="message_forward",
     )(
-        class_all,
+        *class_parts,
         weight,
         gain,
         qkv,
@@ -787,8 +800,20 @@
     own,
     parts,
     together,
+    pieces,
     block_ref,
-    grad_ref,
+    *refs,
+):
+    grad = jnp.concatenate([ref[...] for ref in refs[:pieces]])
+    message_back_body(own, parts, together, block_ref, grad, *refs[pieces:])
+
+
+def message_back_body(
+    own,
+    parts,
+    together,
+    block_ref,
+    grad,
     class_ref,
     start_ref,
     hidden_ref,
@@ -806,7 +831,6 @@
     scores_ref,
 ):
     width = weight_ref.shape[0]
-    grad = grad_ref[...]
     j = pl.program_id(0)
 
     @pl.when(j == 0)
@@ -885,15 +909,15 @@
         finish()
 
 
-def message_back(block, parts, size, own, grad_all, class_all, saved, weight, gain, qkv, out_w):
-    slots, width = grad_all.shape
-    start, hidden, proj, prob, mixed = saved
+def message_back(block, parts, size, own, grad_parts, saved, weight, gain, qkv, out_w):
+    class_all, start, hidden, proj, prob, mixed = saved
+    slots, width = class_all.shape
     shape = jax.ShapeDtypeStruct
     sums = (parts, size, -(-(5 * width // parts + 1) // LANES) * LANES)
     together = width // PAIR if slots <= 256 else 1
-    args = (grad_all, class_all, start, hidden, proj, prob, mixed, weight, gain, qkv, out_w)
+    args = (*grad_parts, class_all, start, hidden, proj, prob, mixed, weight, gain, qkv, out_w)
     return pl.pallas_call(
-        functools.partial(message_back_kernel, own, parts, together),
+        functools.partial(message_back_kernel, own, parts, together, len(grad_parts)),
         grid=(width // PAIR // together,),
         in_specs=[pl.BlockSpec(memory_space=pltpu.SMEM)]
         + [pl.BlockSpec((2 * together, slots, slots), lambda j: (j, 0, 0)) if a is prob else whole(a.shape) for a in args],
@@ -925,8 +949,12 @@
     return outputs
 
 
-def pick(values, index, axis=0):
-    return lax.dynamic_index_in_dim(values, index, axis, keepdims=False)
+def pick(values, index, axis=0, window=None):
+    starts, sizes = [0] * values.ndim, list(values.shape)
+    starts[axis], sizes[axis] = index, 1
+    if window is not None:
+        starts[window[0]], sizes[window[0]] = window[1:]
+    return lax.squeeze(lax.dynamic_slice(values, starts, sizes), (axis,))
 
 
 def add(*terms):
@@ -952,7 +980,8 @@
         return got
 
     def finish(self, got):
-        self.values = jnp.concatenate([self.values, *got])
+        self.pieces = [self.values, *got]
+        self.values = jnp.concatenate(self.pieces)
 
     def end(self):
         self.finish(self.got)
@@ -976,10 +1005,10 @@
     def total(self):
         return add(*self.terms)
 
-    def begin(self, axis, distance, dim):
+    def begin(self, axis, distance, dim, window=None):
         bit = (lax.axis_index(axis) // distance) % 2
-        sent = add(*(pick(term, 1 - bit, dim) for term in self.terms)).astype(BFLOAT)
-        self.terms = [pick(term, bit, dim) for term in self.terms]
+        sent = add(*(pick(term, 1 - bit, dim, window) for term in self.terms)).astype(BFLOAT)
+        self.terms = [pick(term, bit, dim, window) for term in self.terms]
         self.got = [swap(sent, axis, distance)]
         return sent
 
@@ -1067,10 +1096,10 @@
         tied(frames, gather.values), attn_gain, attn_qkv, early, steps - early, projected
     )
     proj = meet(proj, gather)
-    class_all = gather.end()
+    gather.end()
 
     *saved, message, token_kv = message_forward(
-        class_all, own, msg_weight, msg_gain, msg_qkv, msg_out, attn_gain, attn_qkv
+        gather.pieces, own, msg_weight, msg_gain, msg_qkv, msg_out, attn_gain, attn_qkv
     )
     token_kv = token_kv[:count, None]
     message = message[:count, None]
@@ -1100,8 +1129,8 @@
     out_sums = meet(out_sums, down)
     down.end(apart=True)
     split = tiles * 5 // 8
-    down_a, down_b = down.part(np.s_[:, :split]), down.part(np.s_[:, split:])
-    sent = down_a.begin("rows", 2, 0)
+    down_a, down_b = Sum(down.terms), Sum(down.terms)
+    sent = down_a.begin("rows", 2, 0, (1, 0, split))
     up_sums = up_grad(core, tied(second, sent), grad_up, parts, out_sums)
     up = Sum.of_cores(*meet(up_sums, down_a))
 
@@ -1112,7 +1141,7 @@
 
     pieces = (2, 2, steps - 4)
     down_a.end(apart=True)
-    sent = [up.sent, down_b.begin("rows", 2, 0)]
+    sent = [up.sent, down_b.begin("rows", 2, 0, (1, split, tiles - split))]
     output = meet(finish_output(0, pieces[0], None, sent), down_b, up)
     down_b.end(apart=True)
     down = joined(down_a, down_b, 0)
@@ -1172,7 +1201,6 @@
     output = finish_output(sum(pieces[:2]), pieces[2], output, sent)
     output = meet(output, gather, down, up, qkv_a, qkv_b)
     gather.end()
-    grad_all = gather.values
     up.end(apart=True)
     qkv_a.end(apart=True)
     qkv_b.end(apart=True)
@@ -1185,26 +1213,24 @@
         parts,
         width // owners,
         own,
-        tied(grad_all, sent),
-        class_all,
+        tied(gather.pieces, sent),
         saved,
         msg_weight,
         msg_gain,
         msg_qkv,
         msg_out,
     )
-    class_grad, msg_sums = meet(grads, up, qkv)
+    class_grad, msg_sums = meet(grads, qkv)
     msg = Sum([msg_sums.reshape(2, 2, *msg_sums.shape[1:])])
     msg.begin("rows", 1, 1)
-    up.end(apart=True)
-    qkv.end(apart=True)
-    grad_up, grad_qkv = up.total(), qkv.total()
+    msg.end()
+    sent = msg.begin("rows", 2, 0)
+    class_grad, qkv.got = tied((class_grad, qkv.got), sent)
     class_rows = (class_rows[:, 0] + class_grad[:count]).astype(BFLOAT)
     grad_in = lax.dynamic_update_slice(grad_in, class_rows[:, None], (0, 0, 0))
-    msg.end()
-    msg.begin("rows", 2, 0)
-    msg.end(apart=True)
-    msg_total = msg.total()
+    for one in (up, qkv, msg):
+        one.end(apart=True)
+    grad_up, grad_qkv, msg_total = up.total(), qkv.total(), msg.total()
     third, fourth, fifth = (n * width // parts for n in (3, 4, 5))
     return (
         output[0],

time: 357 us -> 351 us (0.983)
  local copies, waits for them, and re-layouts: 29.3 us -> 24 us
    slice x6 -> x2, local copies, waits for them, and re-layouts: 8.85 us -> 2.32 us  [part(): return Sum([term[index] for term in self.terms])]
  transfers between devices with their start and end apart: 31 -> 31, of which waited for: 5 -> 5; matrix products, arithmetic and copies ran while one was open for 8% -> 8% of each run, Pallas kernels for 39% -> 40%
where the time goes in v4:
time: 351 us; the launch traced here: 345 us
  Pallas kernels  246 us (70%)
  starting transfers between devices  32.8 us (9%)
  other arithmetic  25 us (7%)
  local copies, waits for them, and re-layouts  24 us (7%)
  waiting for transfers between devices  14.6 us (4%)
    pallas_call x1, Pallas kernels, mlp(): pl.pallas_call(functools.partial(mlp_kernel, frame_len, 4), grid=(count /...  62.1 us
    pallas_call x1, Pallas kernels, attend_back(): pl.pallas_call(functools.partial(attend_back_kernel, frame_len), grid=(co...  52.9 us
    pallas_call x5, Pallas kernels, alias_call(): pl.pallas_call(body, grid=grid, in_specs=in_specs + [pl.BlockSpec(memory_...  47.6 us
    ppermute x31, starting transfers between devices, swap(): lax.ppermute(values, axis, [(i, i ^ distance) for i in range(lax.axis_siz...  32.8 us
    pallas_call x1, Pallas kernels, attend(): pl.pallas_call(functools.partial(attend_kernel, frame_len), grid=(count /...  20.9 us
    pallas_call x1, Pallas kernels, up_grad(): pl.pallas_call(weight_grad_kernel, grid_spec=pltpu.PrefetchScalarGridSpec...  20.4 us
    pallas_call x1, Pallas kernels, down_grad(): pl.pallas_call(down_grad_kernel, grid=(tiles // 2,), in_specs=[pl.BlockSp...  18.9 us
    ppermute x31, waiting for transfers between devices, swap(): lax.ppermute(values, axis, [(i, i ^ distance) for i in range(lax.axis_siz...  14.6 us
  transfers between devices with their start and end apart: 31, of which 5 were waited for; matrix products, arithmetic and copies ran while one was open for 8% of the time, Pallas kernels for 40%

profile of v4, /device:TPU:0, one launch (start us, length us, event | category | flops | bytes accessed | tf_op | source)
XLA Modules:
  0.0 344.5 jit_solution(5238210746131934611)
XLA Ops:
  2.5 3.0 collective-permute-start
  5.5 9.1 %project.2.refs_3_ = bf16[2800,2304]{1,0:T(8,128)(2,1)} custom-call(bf16[14,197,768]{2,1,0:T(8,128)(2,1)} %x_ref.3, f32[768]{0:T(1024)} %gain_ref.3, bf16[768,2304]{1,0:T(8,128)(2,1)} %w_ref.1), custom_call_target="tpu_custom_call" | custom-call | flops 42467328 | bytes 73728 | tf_op jit(solution)/shard_map/project/pallas_call | solution.py:100
  14.6 1.6 collective-permute-start.1
  16.2 2.6 collective-permute-start.2
  19.0 11.0 %project.3.proj_ref = bf16[2800,2304]{1,0:T(8,128)(2,1)} custom-call(bf16[14,197,768]{2,1,0:T(8,128)(2,1)} %x_ref.3, f32[768]{0:T(1024)} %gain_ref.3, bf16[768,2304]{1,0:T(8,128)(2,1)} %w_ref.1, bf16[2800,2304]{1,0:T(8,128)(2,1)} %project.2.refs_3_), custom_call_target="tpu_custom_call", output_to_operand_aliasing={{}: (3, {})} | custom-call | flops 56623104 | bytes 98304 | tf_op jit(solution)/shard_map/project/pallas_call | solution.py:100
  31.4 6.7 %message_forward.1 = (bf16[128,768]{1,0:T(8,128)(2,1)}, bf16[128,768]{1,0:T(8,128)(2,1)}, bf16[128,768]{1,0:T(8,128)(2,1)}, bf16[128,2304]{1,0:T(8,128)(2,1)}, b...) custom-call(bf16[32,896]{1,0:T(8,128)(2,1)} %copy-done.19, ...), custom_call_target="tpu_custom_call" | custom-call | flops 70000000 | bytes 90000 | tf_op jit(solution)/shard_map/message_forward/pallas_call | solution.py:751
  39.6 20.9 %attend.1 = (bf16[14,12,200,200]{3,2,1,0:T(8,128)(2,1)}, bf16[2800,768]{1,0:T(8,128)(2,1)}, f32[14,12,200]{2,1,0:T(8,128)}, bf16[2800,768]{1,0:T(8,128)(2,1)}) custom-call(bf16[14,197,768]{2,1,0:T(8,128)(2,1)} %x_ref.3, bf16[2800,2304]{1,0:T(8,128)(2,1)} %project.3.proj_ref, bf16[14,1,1536]{2,1,0:T(2,128)(2,1)} %copy.58.token_ref, bf16[768,768]{1,0:T(8,128)(2,1)} %out_w_ref.3), custom_call_target="tpu_custom_call" | custom-call | flops 250000000 | bytes 500000 | tf_op jit(solution)/shard_map/attend/pallas_call | solution.py:201
  60.5 62.1 %mlp.1 = (bf16[2800,768]{1,0:T(8,128)(2,1)}, bf16[2800,768]{1,0:T(8,128)(2,1)}, bf16[2800,3072]{1,0:T(8,128)(2,1)}, bf16[2800,3072]{1,0:T(8,128)(2,1)}, bf16[280...) custom-call(bf16[2800,768]{1,0:T(8,128)(2,1)} %get-tuple-element.173.res_ref.refs_0_, ...), custom_call_target="tpu_custom_call" | custom-call | flops 396361728 | bytes 600000 | tf_op jit(solution)/shard_map/mlp/pallas_call | solution.py:301
  122.7 18.9 %grad_down.1 = (bf16[2,8,192,384]{3,2,1,0:T(8,128)(2,1)}, bf16[2,8,192,384]{3,2,1,0:T(8,128)(2,1)}) custom-call(s32[1]{0:T(128)} %bitcast.5.core_ref, bf16[2800,768]{1,0:T(8,128)(2,1)} %get-tuple-element.122.left_ref, bf16[2800,3072]{1,0:T(8,128)(2,1)} %get-tuple-element.123.right_ref.refs_1_), custom_call_target="tpu_custom_call" | custom-call | flops 132120576 | bytes 215040 | tf_op jit(solution)/shard_map/grad_down/pallas_call | solution.py:432
  141.6 8.5 %grad_attn_out.1 = (bf16[2,768,1024]{2,1,0:T(8,128)(2,1)}, bf16[2,768,1024]{2,1,0:T(8,128)(2,1)}) custom-call(s32[1]{0:T(128)} %bitcast.5.core_ref, bf16[2800,768]{1,0:T(8,128)(2,1)} %get-tuple-element.125.mixed_ref.left_ref, bf16[2800,768]{1,0:T(8,128)(2,1)} %get-tuple-element.126.right_ref.branch_ref, f32[1,768]{1,0:T(1,128)} %get-tuple-element.127.gain_ref), custom_call_target="tpu_custom_call" | custom-call | flops 33030144 | bytes 86016 | tf_op jit(solution)/shard_map/grad_attn_out/pallas_call | solution.py:488
  153.0 20.4 %grad_up.1 = (bf16[2,768,1024]{2,1,0:T(8,128)(2,1)}, bf16[2,768,1024]{2,1,0:T(8,128)(2,1)}) custom-call(s32[1]{0:T(128)} %bitcast.5.core_ref, bf16[2800,768]{1,0:T(8,128)(2,1)} %get-tuple-element.132.left_ref, bf16[2800,3072]{1,0:T(8,128)(2,1)} %get-tuple-element.133.right_ref, ...), custom_call_target="tpu_custom_call", output_to_operand_aliasing={{0}: (3, {}), {1}: (4, {})} | custom-call | flops 132120576 | bytes 215040 | tf_op jit(solution)/shard_map/grad_up/pallas_call | solution.py:385
  173.7 1.9 fusion.14
  176.1 1.6 fusion.2
  177.8 8.4 %mlp_output.3.refs_3_ = bf16[14,197,768]{2,1,0:T(8,128)(2,1)} custom-call(bf16[2800,768]{1,0:T(8,128)(2,1)} %get-tuple-element.173.res_ref.refs_0_, bf16[2800,3072]{1,0:T(8,128)(2,1)} %get-tuple-element.123.right_ref.refs_1_, bf16[3072,768]{1,0:T(8,128)(2,1)} %refs_2_.9), custom_call_target="tpu_custom_call" | custom-call | flops 37748736 | bytes 49152 | tf_op jit(solution)/shard_map/mlp_output/pallas_call | solution.py:100
  186.4 1.7 collective-permute-done.6
  189.6 2.1 fusion.40
  199.9 52.9 %attend_back.1 = (bf16[14,197,768]{2,1,0:T(8,128)(2,1)}, f32[14,1,768]{2,1,0:T(1,128)}, bf16[14,1,768]{2,1,0:T(2,128)(2,1)}, bf16[2,768,384]{2,1,0:T(8,128)(2,1)...) custom-call(s32[1]{0:T(128)} %bitcast.5.core_ref, ...), custom_call_target="tpu_custom_call" | custom-call | flops 450000000 | bytes 500000 | tf_op jit(solution)/shard_map/attend_back/pallas_call | solution.py:621
  254.8 1.7 fusion.1
  268.7 3.4 collective-permute-done.14
  272.8 8.5 %mlp_output.4.refs_3_ = bf16[14,197,768]{2,1,0:T(8,128)(2,1)} custom-call(bf16[2800,768]{1,0:T(8,128)(2,1)} %get-tuple-element.173.res_ref.refs_0_, bf16[2800,3072]{1,0:T(8,128)(2,1)} %get-tuple-element.123.right_ref.refs_1_, bf16[3072,768]{1,0:T(8,128)(2,1)} %refs_2_.9, bf16[14,197,768]{2,1,0:T(8,128)(2,1)} %mlp_output.3.refs_3_), custom_call_target="tpu_custom_call", output_to_operand_aliasing={{}: (3, {})} | custom-call | flops 37748736 | bytes 49152 | tf_op jit(solution)/shard_map/mlp_output/pallas_call | solution.py:100
  281.3 4.2 %collective-permute-done.18 = bf16[768,384]{1,0:T(8,128)(2,1)} collective-permute-done((bf16[768,384]{1,0:T(8,128)(2,1)S(1)}, bf16[768,384]{1,0:T(8,128)(2,1)}, u32[]{:S(2)}, u32[]{:S(2)}) %collective-permute-start.18) | collective-permute-done | bytes 589856 | tf_op jit(solution)/shard_map/ppermute | solution.py:938
  287.9 1.8 fusion.20
  289.7 1.7 collective-permute-start.21
  293.6 2.5 collective-permute-start.22
  298.8 10.6 %mlp_output.5 = bf16[14,197,768]{2,1,0:T(8,128)(2,1)} custom-call(bf16[2800,768]{1,0:T(8,128)(2,1)} %get-tuple-element.173.res_ref.refs_0_, bf16[2800,3072]{1,0:T(8,128)(2,1)} %get-tuple-element.123.right_ref.refs_1_, bf16[3072,768]{1,0:T(8,128)(2,1)} %refs_2_.9, bf16[14,197,768]{2,1,0:T(8,128)(2,1)} %mlp_output.4.refs_3_), custom_call_target="tpu_custom_call", output_to_operand_aliasing={{}: (3, {})} | custom-call | flops 56623104 | bytes 73728 | tf_op jit(solution)/shard_map/mlp_output/pallas_call | solution.py:100
  312.3 2.2 collective-permute-start.26
  316.0 1.9 collective-permute-start.30
  317.9 1.7 fusion.19
  319.7 8.3 %message_back.1 = (f32[16,768]{1,0:T(8,128)}, bf16[4,96,1024]{2,1,0:T(8,128)(2,1)}) custom-call(s32[1]{0:T(128)} %bitcast.44.block_ref, bf16[64,768]{1,0:T(8,128)(2,1)} %copy-done.17, bf16[64,768]{1,0:T(8,128)(2,1)} %copy-done.28, bf16[128,768]{1,0:T(8,128)(2,1)} %get-tuple-element.185.refs_2_, bf16[128,768]{1,0:T(8,128)(2,1)} %get-tuple-element.186.refs_3_, ...), custom_call_target="tpu_custom_call" | custom-call | flops 80000000 | bytes 90000 | tf_op jit(solution)/shard_map/message_back/pallas_call | solution.py:919
  330.0 3.1 collective-permute-done.30
  337.4 1.9 dynamic_update_slice.3
  340.0 2.0 collective-permute-done.29
  (182 shorter events, 53.5 us)
Async XLA Ops:
  2.5 12.1 %collective-permute-start = (bf16[16,896]{1,0:T(8,128)(2,1)S(1)}, bf16[16,896]{1,0:T(8,128)(2,1)S(1)}, u32[]{:S(2)}, u32[]{:S(2)}) collective-permute-start(bf16[16,896]{1,0:T(8,128)(2,1)S(1)} %pad_maximum_fusion.4), channel_id=1, source_target_pairs={{0,4},{4,0},{8,12},{12,8},{16,20},{20,16},{24,28},{28,24},{1,5},{5... | collective-permute-start | bytes 86024 | tf_op jit(solution)/shard_map/ppermute | solution.py:938
  14.6 15.5 %collective-permute-start.1 = (bf16[32,896]{1,0:T(8,128)(2,1)S(1)}, bf16[32,896]{1,0:T(8,128)(2,1)S(1)}, u32[]{:S(2)}, u32[]{:S(2)}) collective-permute-start(bf16[32,896]{1,0:T(8,128)(2,1)S(1)} %pad_maximum_fusion.2.refs_0_), channel_id=1, source_target_pairs={{0,8},{4,12},{8,0},{12,4},{16,24},{20,28},{24,16},{28,20},{1,9},{5... | collective-permute-start | bytes 172040 | tf_op jit(solution)/shard_map/ppermute | solution.py:938
  16.2 13.9 %collective-permute-start.2 = (bf16[32,896]{1,0:T(8,128)(2,1)S(1)}, bf16[32,896]{1,0:T(8,128)(2,1)S(1)}, u32[]{:S(2)}, u32[]{:S(2)}) collective-permute-start(bf16[32,896]{1,0:T(8,128)(2,1)S(1)} %pad_maximum_fusion.2.refs_0_), channel_id=1, source_target_pairs={{0,16},{4,20},{8,24},{12,28},{16,0},{20,4},{24,8},{28,12},{1,17},{... | collective-permute-start | bytes 172040 | tf_op jit(solution)/shard_map/ppermute | solution.py:938
  18.8 11.3 %collective-permute-start.3 = (bf16[32,896]{1,0:T(8,128)(2,1)S(1)}, bf16[32,896]{1,0:T(8,128)(2,1)S(1)}, u32[]{:S(2)}, u32[]{:S(2)}) collective-permute-start(bf16[32,896]{1,0:T(8,128)(2,1)S(1)} %pad_maximum_fusion.2.refs_0_), channel_id=1, source_target_pairs={{0,24},{4,28},{8,16},{12,20},{16,8},{20,12},{24,0},{28,4},{1,25},{... | collective-permute-start | bytes 172040 | tf_op jit(solution)/shard_map/ppermute | solution.py:938
  141.6 8.6 %collective-permute-start.4 = (bf16[2,8,192,384]{3,2,1,0:T(8,128)(2,1)}, bf16[2,8,192,384]{3,2,1,0:T(8,128)(2,1)}, u32[]{:S(2)}, u32[]{:S(2)}) collective-permute-start(bf16[2,8,192,384]{3,2,1,0:T(8,128)(2,1)} %get-tuple-element.124), channel_id=1, source_target_pairs={{0,1},{1,0},{2,3},{3,2},{4,5},{5,4},{6,7},{7,6},{8,9},{9,8},{10,11... | collective-permute-start | bytes 7077896 | tf_op jit(solution)/shard_map/ppermute | solution.py:938
  151.4 22.0 %collective-permute-start.5 = (bf16[5,192,384]{2,1,0:T(8,128)(2,1)S(1)}, bf16[5,192,384]{2,1,0:T(8,128)(2,1)}, u32[]{:S(2)}, u32[]{:S(2)}) collective-permute-start(bf16[5,192,384]{2,1,0:T(8,128)(2,1)S(1)} %fusion.12), channel_id=1, source_target_pairs={{0,2},{1,3},{2,0},{3,1},{4,6},{5,7},{6,4},{7,5},{8,10},{9,11},{10,... | collective-permute-start | bytes 2211848 | tf_op jit(solution)/shard_map/ppermute | solution.py:938
  173.4 14.8 %collective-permute-start.7 = (bf16[2,768,1024]{2,1,0:T(8,128)(2,1)}, bf16[2,768,1024]{2,1,0:T(8,128)(2,1)}, u32[]{:S(2)}, u32[]{:S(2)}) collective-permute-start(bf16[2,768,1024]{2,1,0:T(8,128)(2,1)} %get-tuple-element.139), channel_id=1, source_target_pairs={{0,1},{1,0},{2,3},{3,2},{4,5},{5,4},{6,7},{7,6},{8,9},{9,8},{10,11... | collective-permute-start | bytes 9437192 | tf_op jit(solution)/shard_map/ppermute | solution.py:938
  175.6 12.6 %collective-permute-start.6 = (bf16[3,192,384]{2,1,0:T(8,128)(2,1)}, bf16[3,192,384]{2,1,0:T(8,128)(2,1)}, u32[]{:S(2)}, u32[]{:S(2)}) collective-permute-start(bf16[3,192,384]{2,1,0:T(8,128)(2,1)} %fusion.14), channel_id=1, source_target_pairs={{0,2},{1,3},{2,0},{3,1},{4,6},{5,7},{6,4},{7,5},{8,10},{9,11},{10,... | collective-permute-start | bytes 1327112 | tf_op jit(solution)/shard_map/ppermute | solution.py:938
  193.2 59.6 %collective-permute-start.9 = (bf16[768,512]{1,0:T(8,128)(2,1)}, bf16[768,512]{1,0:T(8,128)(2,1)}, u32[]{:S(2)}, u32[]{:S(2)}) collective-permute-start(bf16[768,512]{1,0:T(8,128)(2,1)} %fusion.6), channel_id=1, source_target_pairs={{0,2},{1,3},{2,0},{3,1},{4,6},{5,7},{6,4},{7,5},{8,10},{9,11},{10,... | collective-permute-start | bytes 2359304 | tf_op jit(solution)/shard_map/ppermute | solution.py:938
  195.1 57.7 %collective-permute-start.10 = (bf16[2,4,96,512]{3,2,1,0:T(8,128)(2,1)}, bf16[2,4,96,512]{3,2,1,0:T(8,128)(2,1)}, u32[]{:S(2)}, u32[]{:S(2)}) collective-permute-start(bf16[2,4,96,512]{3,2,1,0:T(8,128)(2,1)} %fusion.7), channel_id=1, source_target_pairs={{0,4},{4,0},{8,12},{12,8},{16,20},{20,16},{24,28},{28,24},{1,5},{5... | collective-permute-start | bytes 2359304 | tf_op jit(solution)/shard_map/ppermute | solution.py:938
  197.8 55.1 %collective-permute-start.8 = (bf16[4,192,384]{2,1,0:T(8,128)(2,1)}, bf16[4,192,384]{2,1,0:T(8,128)(2,1)}, u32[]{:S(2)}, u32[]{:S(2)}) collective-permute-start(bf16[4,192,384]{2,1,0:T(8,128)(2,1)} %dynamic-slice_bitcast_fusion.1), channel_id=1, source_target_pairs={{0,4},{4,0},{8,12},{12,8},{16,20},{20,16},{24,28},{28,24},{1,5},{5... | collective-permute-start | bytes 1769480 | tf_op jit(solution)/shard_map/ppermute | solution.py:938
  199.9 54.9 %copy-start.4 = (bf16[2,768,512]{2,1,0:T(8,128)(2,1)S(1)}, bf16[2,768,512]{2,1,0:T(8,128)(2,1)}, u32[]{:S(2)}) copy-start(bf16[2,768,512]{2,1,0:T(8,128)(2,1)} %copy-done.3) | copy-start | bytes 4718596
  253.7 11.5 %collective-permute-start.11 = (bf16[16,768]{1,0:T(8,128)(2,1)S(1)}, bf16[16,768]{1,0:T(8,128)(2,1)S(1)}, u32[]{:S(2)}, u32[]{:S(2)}) collective-permute-start(bf16[16,768]{1,0:T(8,128)(2,1)S(1)} %pad.14), channel_id=1, source_target_pairs={{0,4},{4,0},{8,12},{12,8},{16,20},{20,16},{24,28},{28,24},{1,5},{5... | collective-permute-start | bytes 73736 | tf_op jit(solution)/shard_map/ppermute | solution.py:938
  254.3 10.9 %collective-permute-start.12 = (bf16[2,768,384]{2,1,0:T(8,128)(2,1)}, bf16[2,768,384]{2,1,0:T(8,128)(2,1)S(1)}, u32[]{:S(2)}, u32[]{:S(2)}) collective-permute-start(bf16[2,768,384]{2,1,0:T(8,128)(2,1)} %get-tuple-element.159), channel_id=1, source_target_pairs={{0,1},{1,0},{2,3},{3,2},{4,5},{5,4},{6,7},{7,6},{8,9},{9,8},{10,11... | collective-permute-start | bytes 3538952 | tf_op jit(solution)/shard_map/ppermute | solution.py:938
  254.3 10.8 %collective-permute-start.13 = (bf16[2,768,256]{2,1,0:T(8,128)(2,1)}, bf16[2,768,256]{2,1,0:T(8,128)(2,1)S(1)}, u32[]{:S(2)}, u32[]{:S(2)}) collective-permute-start(bf16[2,768,256]{2,1,0:T(8,128)(2,1)} %get-tuple-element.160), channel_id=1, source_target_pairs={{0,1},{1,0},{2,3},{3,2},{4,5},{5,4},{6,7},{7,6},{8,9},{9,8},{10,11... | collective-permute-start | bytes 2359304 | tf_op jit(solution)/shard_map/ppermute | solution.py:938
  258.1 23.2 %collective-permute-start.16 = (bf16[4,96,512]{2,1,0:T(8,128)(2,1)}, bf16[4,96,512]{2,1,0:T(8,128)(2,1)}, u32[]{:S(2)}, u32[]{:S(2)}) collective-permute-start(bf16[4,96,512]{2,1,0:T(8,128)(2,1)} %dynamic-slice_bitcast_fusion.5), channel_id=1, source_target_pairs={{0,4},{4,0},{8,12},{12,8},{16,20},{20,16},{24,28},{28,24},{1,5},{5... | collective-permute-start | bytes 1179656 | tf_op jit(solution)/shard_map/ppermute | solution.py:938
  261.9 19.4 %collective-permute-start.17 = (bf16[4,96,512]{2,1,0:T(8,128)(2,1)}, bf16[4,96,512]{2,1,0:T(8,128)(2,1)}, u32[]{:S(2)}, u32[]{:S(2)}) collective-permute-start(bf16[4,96,512]{2,1,0:T(8,128)(2,1)} %dynamic-slice_bitcast_fusion.4), channel_id=1, source_target_pairs={{0,2},{1,3},{2,0},{3,1},{4,6},{5,7},{6,4},{7,5},{8,10},{9,11},{10,... | collective-permute-start | bytes 1179656 | tf_op jit(solution)/shard_map/ppermute | solution.py:938
  265.6 20.0 %collective-permute-start.18 = (bf16[768,384]{1,0:T(8,128)(2,1)S(1)}, bf16[768,384]{1,0:T(8,128)(2,1)}, u32[]{:S(2)}, u32[]{:S(2)}) collective-permute-start(bf16[768,384]{1,0:T(8,128)(2,1)S(1)} %dynamic-slice_bitcast_fusion), channel_id=1, source_target_pairs={{0,2},{1,3},{2,0},{3,1},{4,6},{5,7},{6,4},{7,5},{8,10},{9,11},{10,... | collective-permute-start | bytes 1769480 | tf_op jit(solution)/shard_map/ppermute | solution.py:938
  267.5 13.8 %collective-permute-start.19 = (bf16[2,4,96,256]{3,2,1,0:T(8,128)(2,1)}, bf16[2,4,96,256]{3,2,1,0:T(8,128)(2,1)}, u32[]{:S(2)}, u32[]{:S(2)}) collective-permute-start(bf16[2,4,96,256]{3,2,1,0:T(8,128)(2,1)} %dynamic-slice_bitcast_fusion.3), channel_id=1, source_target_pairs={{0,4},{4,0},{8,12},{12,8},{16,20},{20,16},{24,28},{28,24},{1,5},{5... | collective-permute-start | bytes 1179656 | tf_op jit(solution)/shard_map/ppermute | solution.py:938
  268.1 4.1 %collective-permute-start.14 = (bf16[32,768]{1,0:T(8,128)(2,1)S(1)}, bf16[32,768]{1,0:T(8,128)(2,1)S(1)}, u32[]{:S(2)}, u32[]{:S(2)}) collective-permute-start(bf16[32,768]{1,0:T(8,128)(2,1)S(1)} %pad_maximum_fusion.3), channel_id=1, source_target_pairs={{0,8},{4,12},{8,0},{12,4},{16,24},{20,28},{24,16},{28,20},{1,9},{5... | collective-permute-start | bytes 147464 | tf_op jit(solution)/shard_map/ppermute | solution.py:938
  272.2 9.1 %collective-permute-start.15 = (bf16[2,192,384]{2,1,0:T(8,128)(2,1)}, bf16[2,192,384]{2,1,0:T(8,128)(2,1)}, u32[]{:S(2)}, u32[]{:S(2)}) collective-permute-start(bf16[2,192,384]{2,1,0:T(8,128)(2,1)} %dynamic-slice_bitcast_fusion.7), channel_id=1, source_target_pairs={{0,8},{4,12},{8,0},{12,4},{16,24},{20,28},{24,16},{28,20},{1,9},{5... | collective-permute-start | bytes 884744 | tf_op jit(solution)/shard_map/ppermute | solution.py:938
  289.7 19.7 %collective-permute-start.21 = (bf16[192,384]{1,0:T(8,128)(2,1)}, bf16[192,384]{1,0:T(8,128)(2,1)S(1)}, u32[]{:S(2)}, u32[]{:S(2)}) collective-permute-start(bf16[192,384]{1,0:T(8,128)(2,1)} %fusion.20), channel_id=1, source_target_pairs={{0,16},{4,20},{8,24},{12,28},{16,0},{20,4},{24,8},{28,12},{1,17},{... | collective-permute-start | bytes 442376 | tf_op jit(solution)/shard_map/ppermute | solution.py:938
  293.6 16.5 %collective-permute-start.22 = (bf16[2,96,1024]{2,1,0:T(8,128)(2,1)}, bf16[2,96,1024]{2,1,0:T(8,128)(2,1)S(1)}, u32[]{:S(2)}, u32[]{:S(2)}) collective-permute-start(bf16[2,96,1024]{2,1,0:T(8,128)(2,1)} %fusion.16), channel_id=1, source_target_pairs={{0,8},{4,12},{8,0},{12,4},{16,24},{20,28},{24,16},{28,20},{1,9},{5... | collective-permute-start | bytes 1179656 | tf_op jit(solution)/shard_map/ppermute | solution.py:938
  296.1 13.4 %collective-permute-start.23 = (bf16[4,96,384]{2,1,0:T(8,128)(2,1)S(1)}, bf16[4,96,384]{2,1,0:T(8,128)(2,1)S(1)}, u32[]{:S(2)}, u32[]{:S(2)}) collective-permute-start(bf16[4,96,384]{2,1,0:T(8,128)(2,1)S(1)} %dynamic-slice_bitcast_fusion.6), channel_id=1, source_target_pairs={{0,4},{4,0},{8,12},{12,8},{16,20},{20,16},{24,28},{28,24},{1,5},{5... | collective-permute-start | bytes 884744 | tf_op jit(solution)/shard_map/ppermute | solution.py:938
  297.5 12.0 %collective-permute-start.24 = (bf16[4,96,256]{2,1,0:T(8,128)(2,1)}, bf16[4,96,256]{2,1,0:T(8,128)(2,1)}, u32[]{:S(2)}, u32[]{:S(2)}) collective-permute-start(bf16[4,96,256]{2,1,0:T(8,128)(2,1)} %dynamic-slice_bitcast_fusion.9), channel_id=1, source_target_pairs={{0,2},{1,3},{2,0},{3,1},{4,6},{5,7},{6,4},{7,5},{8,10},{9,11},{10,... | collective-permute-start | bytes 589832 | tf_op jit(solution)/shard_map/ppermute | solution.py:938
  298.7 10.7 %collective-permute-start.20 = (bf16[64,768]{1,0:T(8,128)(2,1)S(1)}, bf16[64,768]{1,0:T(8,128)(2,1)S(1)}, u32[]{:S(2)}, u32[]{:S(2)}) collective-permute-start(bf16[64,768]{1,0:T(8,128)(2,1)S(1)} %pad_maximum_fusion.1.refs_0_), channel_id=1, source_target_pairs={{0,16},{4,20},{8,24},{12,28},{16,0},{20,4},{24,8},{28,12},{1,17},{... | collective-permute-start | bytes 294920 | tf_op jit(solution)/shard_map/ppermute | solution.py:938
  311.5 16.5 %collective-permute-start.25 = (bf16[96,640]{1,0:T(8,128)(2,1)S(1)}, bf16[96,640]{1,0:T(8,128)(2,1)S(1)}, u32[]{:S(2)}, u32[]{:S(2)}) collective-permute-start(bf16[96,640]{1,0:T(8,128)(2,1)S(1)} %get-tuple-element.207), channel_id=1, source_target_pairs={{0,8},{4,12},{8,0},{12,4},{16,24},{20,28},{24,16},{28,20},{1,9},{5... | collective-permute-start | bytes 368648 | tf_op jit(solution)/shard_map/ppermute | solution.py:938
  312.3 15.7 %collective-permute-start.26 = (bf16[96,640]{1,0:T(8,128)(2,1)S(1)}, bf16[96,640]{1,0:T(8,128)(2,1)S(1)}, u32[]{:S(2)}, u32[]{:S(2)}) collective-permute-start(bf16[96,640]{1,0:T(8,128)(2,1)S(1)} %get-tuple-element.208), channel_id=1, source_target_pairs={{0,16},{4,20},{8,24},{12,28},{16,0},{20,4},{24,8},{28,12},{1,17},{... | collective-permute-start | bytes 368648 | tf_op jit(solution)/shard_map/ppermute | solution.py:938
  314.5 13.5 %collective-permute-start.27 = (bf16[96,640]{1,0:T(8,128)(2,1)S(1)}, bf16[96,640]{1,0:T(8,128)(2,1)S(1)}, u32[]{:S(2)}, u32[]{:S(2)}) collective-permute-start(bf16[96,640]{1,0:T(8,128)(2,1)S(1)} %get-tuple-element.206), channel_id=1, source_target_pairs={{0,24},{4,28},{8,16},{12,20},{16,8},{20,12},{24,0},{28,4},{1,25},{... | collective-permute-start | bytes 368648 | tf_op jit(solution)/shard_map/ppermute | solution.py:938
  316.0 17.1 %collective-permute-start.30 = (bf16[96,1024]{1,0:T(8,128)(2,1)S(1)}, bf16[96,1024]{1,0:T(8,128)(2,1)}, u32[]{:S(2)}, u32[]{:S(2)}) collective-permute-start(bf16[96,1024]{1,0:T(8,128)(2,1)S(1)} %fusion.18), channel_id=1, source_target_pairs={{0,16},{4,20},{8,24},{12,28},{16,0},{20,4},{24,8},{28,12},{1,17},{... | collective-permute-start | bytes 589832 | tf_op jit(solution)/shard_map/ppermute | solution.py:938
  329.9 6.3 %collective-permute-start.28 = (bf16[2,96,1024]{2,1,0:T(8,128)(2,1)S(1)}, bf16[2,96,1024]{2,1,0:T(8,128)(2,1)S(1)}, u32[]{:S(2)}, u32[]{:S(2)}) collective-permute-start(bf16[2,96,1024]{2,1,0:T(8,128)(2,1)S(1)} %dynamic-slice_bitcast_fusion.2), channel_id=1, source_target_pairs={{0,1},{1,0},{2,3},{3,2},{4,5},{5,4},{6,7},{7,6},{8,9},{9,8},{10,11... | collective-permute-start | bytes 1179656 | tf_op jit(solution)/shard_map/ppermute | solution.py:938
  336.4 5.7 %collective-permute-start.29 = (bf16[96,1024]{1,0:T(8,128)(2,1)S(1)}, bf16[96,1024]{1,0:T(8,128)(2,1)S(1)}, u32[]{:S(2)}, u32[]{:S(2)}) collective-permute-start(bf16[96,1024]{1,0:T(8,128)(2,1)S(1)} %dynamic-slice_bitcast_fusion.8), channel_id=1, source_target_pairs={{0,2},{1,3},{2,0},{3,1},{4,6},{5,7},{6,4},{7,5},{8,10},{9,11},{10,... | collective-permute-start | bytes 589832 | tf_op jit(solution)/shard_map/ppermute | solution.py:938
  (36 other events, 160.2 us)

commit v5 on v4

--- a/solution.py
+++ b/solution.py
@@ -1128,7 +1128,7 @@
     )
     out_sums = meet(out_sums, down)
     down.end(apart=True)
-    split = tiles * 5 // 8
+    split = tiles * 3 // 4
     down_a, down_b = Sum(down.terms), Sum(down.terms)
     sent = down_a.begin("rows", 2, 0, (1, 0, split))
     up_sums = up_grad(core, tied(second, sent), grad_up, parts, out_sums)
@@ -1139,7 +1139,7 @@
             tied(residual, *others), act, down_weight, frames_in.shape, first, number, prior
         )
 
-    pieces = (2, 2, steps - 4)
+    pieces = (2, steps - 4, 2)
     down_a.end(apart=True)
     sent = [up.sent, down_b.begin("rows", 2, 0, (1, split, tiles - split))]
     output = meet(finish_output(0, pieces[0], None, sent), down_b, up)

time: 351 us -> 352 us (level); the launches traced: 345 us -> 351 us
  Pallas kernels: 246 us -> 258 us
    pallas_call x1, Pallas kernels: 20.4 us -> 31.8 us  [up_grad(): pl.pallas_call(weight_grad_kernel, grid_spec=pltpu.PrefetchScalarGridSpec...]
    ppermute x31, waiting for transfers between devices: 14.6 us -> 11.1 us  [swap(): lax.ppermute(values, axis, [(i, i ^ distance) for i in range(lax.axis_siz...]
  transfers between devices with their start and end apart: 31 -> 31, of which waited for: 5 -> 6; matrix products, arithmetic and copies ran while one was open for 8% -> 7% of each run, Pallas kernels for 40% -> 42%
where the time goes in v5:
time: 352 us; the launch traced here: 351 us
  Pallas kernels  258 us (73%)
  starting transfers between devices  33 us (9%)
  local copies, waits for them, and re-layouts  24.6 us (7%)
  other arithmetic  23.4 us (7%)
  waiting for transfers between devices  11.1 us (3%)
    pallas_call x1, Pallas kernels, mlp(): pl.pallas_call(functools.partial(mlp_kernel, frame_len, 4), grid=(count /...  62.2 us
    pallas_call x1, Pallas kernels, attend_back(): pl.pallas_call(functools.partial(attend_back_kernel, frame_len), grid=(co...  52.7 us
    pallas_call x5, Pallas kernels, alias_call(): pl.pallas_call(body, grid=grid, in_specs=in_specs + [pl.BlockSpec(memory_...  47.5 us
    ppermute x31, starting transfers between devices, swap(): lax.ppermute(values, axis, [(i, i ^ distance) for i in range(lax.axis_siz...  33 us
    pallas_call x1, Pallas kernels, up_grad(): pl.pallas_call(weight_grad_kernel, grid_spec=pltpu.PrefetchScalarGridSpec...  31.8 us
    pallas_call x1, Pallas kernels, attend(): pl.pallas_call(functools.partial(attend_kernel, frame_len), grid=(count /...  20.9 us
    pallas_call x1, Pallas kernels, down_grad(): pl.pallas_call(down_grad_kernel, grid=(tiles // 2,), in_specs=[pl.BlockSp...  18.9 us
    ppermute x31, waiting for transfers between devices, swap(): lax.ppermute(values, axis, [(i, i ^ distance) for i in range(lax.axis_siz...  11.1 us
  transfers between devices with their start and end apart: 31, of which 6 were waited for; matrix products, arithmetic and copies ran while one was open for 7% of the time, Pallas kernels for 42%

profile of v5, /device:TPU:0, one launch (start us, length us, event | category | flops | bytes accessed | tf_op | source)
XLA Modules:
  0.0 351.1 jit_solution(11944734374819440415)
XLA Ops:
  2.5 3.0 collective-permute-start
  5.5 9.1 %project.2.refs_3_ = bf16[2800,2304]{1,0:T(8,128)(2,1)} custom-call(bf16[14,197,768]{2,1,0:T(8,128)(2,1)} %x_ref.3, f32[768]{0:T(1024)} %gain_ref.3, bf16[768,2304]{1,0:T(8,128)(2,1)} %w_ref.1), custom_call_target="tpu_custom_call" | custom-call | flops 42467328 | bytes 73728 | tf_op jit(solution)/shard_map/project/pallas_call | solution.py:100
  14.6 1.6 collective-permute-start.1
  16.2 2.6 collective-permute-start.2
  19.1 11.0 %project.3.proj_ref = bf16[2800,2304]{1,0:T(8,128)(2,1)} custom-call(bf16[14,197,768]{2,1,0:T(8,128)(2,1)} %x_ref.3, f32[768]{0:T(1024)} %gain_ref.3, bf16[768,2304]{1,0:T(8,128)(2,1)} %w_ref.1, bf16[2800,2304]{1,0:T(8,128)(2,1)} %project.2.refs_3_), custom_call_target="tpu_custom_call", output_to_operand_aliasing={{}: (3, {})} | custom-call | flops 56623104 | bytes 98304 | tf_op jit(solution)/shard_map/project/pallas_call | solution.py:100
  31.4 6.7 %message_forward.1 = (bf16[128,768]{1,0:T(8,128)(2,1)}, bf16[128,768]{1,0:T(8,128)(2,1)}, bf16[128,768]{1,0:T(8,128)(2,1)}, bf16[128,2304]{1,0:T(8,128)(2,1)}, b...) custom-call(bf16[32,896]{1,0:T(8,128)(2,1)} %copy-done.16, ...), custom_call_target="tpu_custom_call" | custom-call | flops 70000000 | bytes 90000 | tf_op jit(solution)/shard_map/message_forward/pallas_call | solution.py:751
  39.6 20.9 %attend.1 = (bf16[14,12,200,200]{3,2,1,0:T(8,128)(2,1)}, bf16[2800,768]{1,0:T(8,128)(2,1)}, f32[14,12,200]{2,1,0:T(8,128)}, bf16[2800,768]{1,0:T(8,128)(2,1)}) custom-call(bf16[14,197,768]{2,1,0:T(8,128)(2,1)} %x_ref.3, bf16[2800,2304]{1,0:T(8,128)(2,1)} %project.3.proj_ref, bf16[14,1,1536]{2,1,0:T(2,128)(2,1)} %copy.58.token_ref, bf16[768,768]{1,0:T(8,128)(2,1)} %out_w_ref.3), custom_call_target="tpu_custom_call" | custom-call | flops 250000000 | bytes 500000 | tf_op jit(solution)/shard_map/attend/pallas_call | solution.py:201
  60.5 62.2 %mlp.1 = (bf16[2800,768]{1,0:T(8,128)(2,1)}, bf16[2800,768]{1,0:T(8,128)(2,1)}, bf16[2800,3072]{1,0:T(8,128)(2,1)}, bf16[2800,3072]{1,0:T(8,128)(2,1)}, bf16[280...) custom-call(bf16[2800,768]{1,0:T(8,128)(2,1)} %get-tuple-element.173.res_ref.refs_0_, ...), custom_call_target="tpu_custom_call" | custom-call | flops 396361728 | bytes 600000 | tf_op jit(solution)/shard_map/mlp/pallas_call | solution.py:301
  122.7 18.9 %grad_down.1 = (bf16[2,8,192,384]{3,2,1,0:T(8,128)(2,1)}, bf16[2,8,192,384]{3,2,1,0:T(8,128)(2,1)}) custom-call(s32[1]{0:T(128)} %bitcast.5.core_ref, bf16[2800,768]{1,0:T(8,128)(2,1)} %get-tuple-element.122.left_ref, bf16[2800,3072]{1,0:T(8,128)(2,1)} %get-tuple-element.123.right_ref.refs_1_), custom_call_target="tpu_custom_call" | custom-call | flops 132120576 | bytes 215040 | tf_op jit(solution)/shard_map/grad_down/pallas_call | solution.py:432
  141.7 8.5 %grad_attn_out.1 = (bf16[2,768,1024]{2,1,0:T(8,128)(2,1)}, bf16[2,768,1024]{2,1,0:T(8,128)(2,1)}) custom-call(s32[1]{0:T(128)} %bitcast.5.core_ref, bf16[2800,768]{1,0:T(8,128)(2,1)} %get-tuple-element.125.mixed_ref.left_ref, bf16[2800,768]{1,0:T(8,128)(2,1)} %get-tuple-element.126.right_ref.branch_ref, f32[1,768]{1,0:T(1,128)} %get-tuple-element.127.gain_ref), custom_call_target="tpu_custom_call" | custom-call | flops 33030144 | bytes 86016 | tf_op jit(solution)/shard_map/grad_attn_out/pallas_call | solution.py:488
  151.5 1.6 collective-permute-start.5
  153.1 31.8 %grad_up.1 = (bf16[2,768,1024]{2,1,0:T(8,128)(2,1)}, bf16[2,768,1024]{2,1,0:T(8,128)(2,1)}) custom-call(s32[1]{0:T(128)} %bitcast.5.core_ref, bf16[2800,768]{1,0:T(8,128)(2,1)} %get-tuple-element.132.left_ref, bf16[2800,3072]{1,0:T(8,128)(2,1)} %get-tuple-element.133.right_ref, ...), custom_call_target="tpu_custom_call", output_to_operand_aliasing={{0}: (3, {}), {1}: (4, {})} | custom-call | flops 132120576 | bytes 215040 | tf_op jit(solution)/shard_map/grad_up/pallas_call | solution.py:385
  186.8 2.1 fusion.41
  188.8 8.3 %mlp_output.3.refs_3_ = bf16[14,197,768]{2,1,0:T(8,128)(2,1)} custom-call(bf16[2800,768]{1,0:T(8,128)(2,1)} %get-tuple-element.173.res_ref.refs_0_, bf16[2800,3072]{1,0:T(8,128)(2,1)} %get-tuple-element.123.right_ref.refs_1_, bf16[3072,768]{1,0:T(8,128)(2,1)} %refs_2_.9), custom_call_target="tpu_custom_call" | custom-call | flops 37748736 | bytes 49152 | tf_op jit(solution)/shard_map/mlp_output/pallas_call | solution.py:100
  197.1 2.0 fusion
  200.4 2.1 fusion.40
  203.8 1.5 collective-permute-start.9
  209.0 1.5 collective-permute-start.8
  211.2 52.7 %attend_back.1 = (bf16[14,197,768]{2,1,0:T(8,128)(2,1)}, f32[14,1,768]{2,1,0:T(1,128)}, bf16[14,1,768]{2,1,0:T(2,128)(2,1)}, bf16[2,768,384]{2,1,0:T(8,128)(2,1)...) custom-call(s32[1]{0:T(128)} %bitcast.5.core_ref, ...), custom_call_target="tpu_custom_call" | custom-call | flops 450000000 | bytes 500000 | tf_op jit(solution)/shard_map/attend_back/pallas_call | solution.py:621
  265.8 1.7 fusion.2
  268.5 1.6 collective-permute-start.16
  279.4 3.4 collective-permute-done.14
  284.1 10.7 %mlp_output.4.refs_3_ = bf16[14,197,768]{2,1,0:T(8,128)(2,1)} custom-call(bf16[2800,768]{1,0:T(8,128)(2,1)} %get-tuple-element.173.res_ref.refs_0_, bf16[2800,3072]{1,0:T(8,128)(2,1)} %get-tuple-element.123.right_ref.refs_1_, bf16[3072,768]{1,0:T(8,128)(2,1)} %refs_2_.9, bf16[14,197,768]{2,1,0:T(8,128)(2,1)} %mlp_output.3.refs_3_), custom_call_target="tpu_custom_call", output_to_operand_aliasing={{}: (3, {})} | custom-call | flops 56623104 | bytes 73728 | tf_op jit(solution)/shard_map/mlp_output/pallas_call | solution.py:100
  297.7 1.7 fusion.20
  299.4 3.4 collective-permute-start.21
  307.4 8.3 %mlp_output.5 = bf16[14,197,768]{2,1,0:T(8,128)(2,1)} custom-call(bf16[2800,768]{1,0:T(8,128)(2,1)} %get-tuple-element.173.res_ref.refs_0_, bf16[2800,3072]{1,0:T(8,128)(2,1)} %get-tuple-element.123.right_ref.refs_1_, bf16[3072,768]{1,0:T(8,128)(2,1)} %refs_2_.9, bf16[14,197,768]{2,1,0:T(8,128)(2,1)} %mlp_output.4.refs_3_), custom_call_target="tpu_custom_call", output_to_operand_aliasing={{}: (3, {})} | custom-call | flops 37748736 | bytes 49152 | tf_op jit(solution)/shard_map/mlp_output/pallas_call | solution.py:100
  319.2 2.8 collective-permute-start.26
  324.7 1.8 fusion.19
  326.5 8.3 %message_back.1 = (f32[16,768]{1,0:T(8,128)}, bf16[4,96,1024]{2,1,0:T(8,128)(2,1)}) custom-call(s32[1]{0:T(128)} %bitcast.44.block_ref, bf16[64,768]{1,0:T(8,128)(2,1)} %copy-done.14, bf16[64,768]{1,0:T(8,128)(2,1)} %collective-permute-done.20.refs_1_, bf16[128,768]{1,0:T(8,128)(2,1)} %get-tuple-element.185.refs_2_, ...), custom_call_target="tpu_custom_call" | custom-call | flops 80000000 | bytes 90000 | tf_op jit(solution)/shard_map/message_back/pallas_call | solution.py:919
  336.8 3.7 %collective-permute-done.30 = bf16[96,1024]{1,0:T(8,128)(2,1)S(1)} collective-permute-done((bf16[96,1024]{1,0:T(8,128)(2,1)}, bf16[96,1024]{1,0:T(8,128)(2,1)S(1)}, u32[]{:S(2)}, u32[]{:S(2)}) %collective-permute-start.30) | collective-permute-done | bytes 196640 | tf_op jit(solution)/shard_map/ppermute | solution.py:938
  343.6 1.9 dynamic_update_slice.3
  346.3 2.4 collective-permute-done.29
  (178 shorter events, 49.7 us)
Async XLA Ops:
  2.5 12.1 %collective-permute-start = (bf16[16,896]{1,0:T(8,128)(2,1)S(1)}, bf16[16,896]{1,0:T(8,128)(2,1)S(1)}, u32[]{:S(2)}, u32[]{:S(2)}) collective-permute-start(bf16[16,896]{1,0:T(8,128)(2,1)S(1)} %pad_maximum_fusion.4), channel_id=1, source_target_pairs={{0,4},{4,0},{8,12},{12,8},{16,20},{20,16},{24,28},{28,24},{1,5},{5... | collective-permute-start | bytes 86024 | tf_op jit(solution)/shard_map/ppermute | solution.py:938
  14.6 15.5 %copy-start.16 = (bf16[32,896]{1,0:T(8,128)(2,1)}, bf16[32,896]{1,0:T(8,128)(2,1)S(1)}, u32[]{:S(2)}) copy-start(bf16[32,896]{1,0:T(8,128)(2,1)S(1)} %pad_maximum_fusion.2.refs_0_) | copy-start | bytes 172036
  14.6 15.5 %collective-permute-start.1 = (bf16[32,896]{1,0:T(8,128)(2,1)S(1)}, bf16[32,896]{1,0:T(8,128)(2,1)S(1)}, u32[]{:S(2)}, u32[]{:S(2)}) collective-permute-start(bf16[32,896]{1,0:T(8,128)(2,1)S(1)} %pad_maximum_fusion.2.refs_0_), channel_id=1, source_target_pairs={{0,8},{4,12},{8,0},{12,4},{16,24},{20,28},{24,16},{28,20},{1,9},{5... | collective-permute-start | bytes 172040 | tf_op jit(solution)/shard_map/ppermute | solution.py:938
  16.2 13.9 %collective-permute-start.2 = (bf16[32,896]{1,0:T(8,128)(2,1)S(1)}, bf16[32,896]{1,0:T(8,128)(2,1)S(1)}, u32[]{:S(2)}, u32[]{:S(2)}) collective-permute-start(bf16[32,896]{1,0:T(8,128)(2,1)S(1)} %pad_maximum_fusion.2.refs_0_), channel_id=1, source_target_pairs={{0,16},{4,20},{8,24},{12,28},{16,0},{20,4},{24,8},{28,12},{1,17},{... | collective-permute-start | bytes 172040 | tf_op jit(solution)/shard_map/ppermute | solution.py:938
  18.8 11.3 %collective-permute-start.3 = (bf16[32,896]{1,0:T(8,128)(2,1)S(1)}, bf16[32,896]{1,0:T(8,128)(2,1)S(1)}, u32[]{:S(2)}, u32[]{:S(2)}) collective-permute-start(bf16[32,896]{1,0:T(8,128)(2,1)S(1)} %pad_maximum_fusion.2.refs_0_), channel_id=1, source_target_pairs={{0,24},{4,28},{8,16},{12,20},{16,8},{20,12},{24,0},{28,4},{1,25},{... | collective-permute-start | bytes 172040 | tf_op jit(solution)/shard_map/ppermute | solution.py:938
  141.7 8.5 %collective-permute-start.4 = (bf16[2,8,192,384]{3,2,1,0:T(8,128)(2,1)}, bf16[2,8,192,384]{3,2,1,0:T(8,128)(2,1)}, u32[]{:S(2)}, u32[]{:S(2)}) collective-permute-start(bf16[2,8,192,384]{3,2,1,0:T(8,128)(2,1)} %get-tuple-element.124), channel_id=1, source_target_pairs={{0,1},{1,0},{2,3},{3,2},{4,5},{5,4},{6,7},{7,6},{8,9},{9,8},{10,11... | collective-permute-start | bytes 7077896 | tf_op jit(solution)/shard_map/ppermute | solution.py:938
  151.5 33.3 %collective-permute-start.5 = (bf16[6,192,384]{2,1,0:T(8,128)(2,1)S(1)}, bf16[6,192,384]{2,1,0:T(8,128)(2,1)}, u32[]{:S(2)}, u32[]{:S(2)}) collective-permute-start(bf16[6,192,384]{2,1,0:T(8,128)(2,1)S(1)} %fusion.5), channel_id=1, source_target_pairs={{0,2},{1,3},{2,0},{3,1},{4,6},{5,7},{6,4},{7,5},{8,10},{9,11},{10,... | collective-permute-start | bytes 2654216 | tf_op jit(solution)/shard_map/ppermute | solution.py:938
  184.9 14.3 %collective-permute-start.7 = (bf16[2,768,1024]{2,1,0:T(8,128)(2,1)}, bf16[2,768,1024]{2,1,0:T(8,128)(2,1)}, u32[]{:S(2)}, u32[]{:S(2)}) collective-permute-start(bf16[2,768,1024]{2,1,0:T(8,128)(2,1)} %get-tuple-element.139), channel_id=1, source_target_pairs={{0,1},{1,0},{2,3},{3,2},{4,5},{5,4},{6,7},{7,6},{8,9},{9,8},{10,11... | collective-permute-start | bytes 9437192 | tf_op jit(solution)/shard_map/ppermute | solution.py:938
  186.1 13.1 %collective-permute-start.6 = (bf16[2,192,384]{2,1,0:T(8,128)(2,1)S(1)}, bf16[2,192,384]{2,1,0:T(8,128)(2,1)S(1)}, u32[]{:S(2)}, u32[]{:S(2)}) collective-permute-start(bf16[2,192,384]{2,1,0:T(8,128)(2,1)S(1)} %fusion.18), channel_id=1, source_target_pairs={{0,2},{1,3},{2,0},{3,1},{4,6},{5,7},{6,4},{7,5},{8,10},{9,11},{10,... | collective-permute-start | bytes 884744 | tf_op jit(solution)/shard_map/ppermute | solution.py:938
  203.8 60.1 %collective-permute-start.9 = (bf16[768,512]{1,0:T(8,128)(2,1)}, bf16[768,512]{1,0:T(8,128)(2,1)}, u32[]{:S(2)}, u32[]{:S(2)}) collective-permute-start(bf16[768,512]{1,0:T(8,128)(2,1)} %fusion.6), channel_id=1, source_target_pairs={{0,2},{1,3},{2,0},{3,1},{4,6},{5,7},{6,4},{7,5},{8,10},{9,11},{10,... | collective-permute-start | bytes 2359304 | tf_op jit(solution)/shard_map/ppermute | solution.py:938
  206.4 57.5 %collective-permute-start.10 = (bf16[2,4,96,512]{3,2,1,0:T(8,128)(2,1)}, bf16[2,4,96,512]{3,2,1,0:T(8,128)(2,1)}, u32[]{:S(2)}, u32[]{:S(2)}) collective-permute-start(bf16[2,4,96,512]{3,2,1,0:T(8,128)(2,1)} %fusion.7), channel_id=1, source_target_pairs={{0,4},{4,0},{8,12},{12,8},{16,20},{20,16},{24,28},{28,24},{1,5},{5... | collective-permute-start | bytes 2359304 | tf_op jit(solution)/shard_map/ppermute | solution.py:938
  209.0 54.8 %collective-permute-start.8 = (bf16[4,192,384]{2,1,0:T(8,128)(2,1)}, bf16[4,192,384]{2,1,0:T(8,128)(2,1)}, u32[]{:S(2)}, u32[]{:S(2)}) collective-permute-start(bf16[4,192,384]{2,1,0:T(8,128)(2,1)} %dynamic-slice_bitcast_fusion.1), channel_id=1, source_target_pairs={{0,4},{4,0},{8,12},{12,8},{16,20},{20,16},{24,28},{28,24},{1,5},{5... | collective-permute-start | bytes 1769480 | tf_op jit(solution)/shard_map/ppermute | solution.py:938
  264.7 9.5 %collective-permute-start.11 = (bf16[16,768]{1,0:T(8,128)(2,1)S(1)}, bf16[16,768]{1,0:T(8,128)(2,1)S(1)}, u32[]{:S(2)}, u32[]{:S(2)}) collective-permute-start(bf16[16,768]{1,0:T(8,128)(2,1)S(1)} %pad.14), channel_id=1, source_target_pairs={{0,4},{4,0},{8,12},{12,8},{16,20},{20,16},{24,28},{28,24},{1,5},{5... | collective-permute-start | bytes 73736 | tf_op jit(solution)/shard_map/ppermute | solution.py:938
  265.3 9.0 %collective-permute-start.12 = (bf16[2,768,384]{2,1,0:T(8,128)(2,1)}, bf16[2,768,384]{2,1,0:T(8,128)(2,1)S(1)}, u32[]{:S(2)}, u32[]{:S(2)}) collective-permute-start(bf16[2,768,384]{2,1,0:T(8,128)(2,1)} %get-tuple-element.159), channel_id=1, source_target_pairs={{0,1},{1,0},{2,3},{3,2},{4,5},{5,4},{6,7},{7,6},{8,9},{9,8},{10,11... | collective-permute-start | bytes 3538952 | tf_op jit(solution)/shard_map/ppermute | solution.py:938
  265.3 8.9 %collective-permute-start.13 = (bf16[2,768,256]{2,1,0:T(8,128)(2,1)}, bf16[2,768,256]{2,1,0:T(8,128)(2,1)S(1)}, u32[]{:S(2)}, u32[]{:S(2)}) collective-permute-start(bf16[2,768,256]{2,1,0:T(8,128)(2,1)} %get-tuple-element.160), channel_id=1, source_target_pairs={{0,1},{1,0},{2,3},{3,2},{4,5},{5,4},{6,7},{7,6},{8,9},{9,8},{10,11... | collective-permute-start | bytes 2359304 | tf_op jit(solution)/shard_map/ppermute | solution.py:938
  268.5 26.4 %collective-permute-start.16 = (bf16[4,96,512]{2,1,0:T(8,128)(2,1)S(1)}, bf16[4,96,512]{2,1,0:T(8,128)(2,1)}, u32[]{:S(2)}, u32[]{:S(2)}) collective-permute-start(bf16[4,96,512]{2,1,0:T(8,128)(2,1)S(1)} %dynamic-slice_bitcast_fusion.5), channel_id=1, source_target_pairs={{0,4},{4,0},{8,12},{12,8},{16,20},{20,16},{24,28},{28,24},{1,5},{5... | collective-permute-start | bytes 1179656 | tf_op jit(solution)/shard_map/ppermute | solution.py:938
  271.6 23.4 %collective-permute-start.17 = (bf16[4,96,512]{2,1,0:T(8,128)(2,1)S(1)}, bf16[4,96,512]{2,1,0:T(8,128)(2,1)}, u32[]{:S(2)}, u32[]{:S(2)}) collective-permute-start(bf16[4,96,512]{2,1,0:T(8,128)(2,1)S(1)} %dynamic-slice_bitcast_fusion.4), channel_id=1, source_target_pairs={{0,2},{1,3},{2,0},{3,1},{4,6},{5,7},{6,4},{7,5},{8,10},{9,11},{10,... | collective-permute-start | bytes 1179656 | tf_op jit(solution)/shard_map/ppermute | solution.py:938
  275.8 19.4 %collective-permute-start.18 = (bf16[768,384]{1,0:T(8,128)(2,1)}, bf16[768,384]{1,0:T(8,128)(2,1)}, u32[]{:S(2)}, u32[]{:S(2)}) collective-permute-start(bf16[768,384]{1,0:T(8,128)(2,1)} %dynamic-slice_bitcast_fusion), channel_id=1, source_target_pairs={{0,2},{1,3},{2,0},{3,1},{4,6},{5,7},{6,4},{7,5},{8,10},{9,11},{10,... | collective-permute-start | bytes 1769480 | tf_op jit(solution)/shard_map/ppermute | solution.py:938
  278.2 16.7 %collective-permute-start.19 = (bf16[2,4,96,256]{3,2,1,0:T(8,128)(2,1)}, bf16[2,4,96,256]{3,2,1,0:T(8,128)(2,1)}, u32[]{:S(2)}, u32[]{:S(2)}) collective-permute-start(bf16[2,4,96,256]{3,2,1,0:T(8,128)(2,1)} %dynamic-slice_bitcast_fusion.3), channel_id=1, source_target_pairs={{0,4},{4,0},{8,12},{12,8},{16,20},{20,16},{24,28},{28,24},{1,5},{5... | collective-permute-start | bytes 1179656 | tf_op jit(solution)/shard_map/ppermute | solution.py:938
  278.8 4.1 %collective-permute-start.14 = (bf16[32,768]{1,0:T(8,128)(2,1)S(1)}, bf16[32,768]{1,0:T(8,128)(2,1)S(1)}, u32[]{:S(2)}, u32[]{:S(2)}) collective-permute-start(bf16[32,768]{1,0:T(8,128)(2,1)S(1)} %pad_maximum_fusion.3), channel_id=1, source_target_pairs={{0,8},{4,12},{8,0},{12,4},{16,24},{20,28},{24,16},{28,20},{1,9},{5... | collective-permute-start | bytes 147464 | tf_op jit(solution)/shard_map/ppermute | solution.py:938
  283.5 11.4 %collective-permute-start.15 = (bf16[2,192,384]{2,1,0:T(8,128)(2,1)}, bf16[2,192,384]{2,1,0:T(8,128)(2,1)}, u32[]{:S(2)}, u32[]{:S(2)}) collective-permute-start(bf16[2,192,384]{2,1,0:T(8,128)(2,1)} %dynamic-slice_bitcast_fusion.7), channel_id=1, source_target_pairs={{0,8},{4,12},{8,0},{12,4},{16,24},{20,28},{24,16},{28,20},{1,9},{5... | collective-permute-start | bytes 884744 | tf_op jit(solution)/shard_map/ppermute | solution.py:938
  299.4 16.4 %collective-permute-start.21 = (bf16[192,384]{1,0:T(8,128)(2,1)}, bf16[192,384]{1,0:T(8,128)(2,1)}, u32[]{:S(2)}, u32[]{:S(2)}) collective-permute-start(bf16[192,384]{1,0:T(8,128)(2,1)} %fusion.20), channel_id=1, source_target_pairs={{0,16},{4,20},{8,24},{12,28},{16,0},{20,4},{24,8},{28,12},{1,17},{... | collective-permute-start | bytes 442376 | tf_op jit(solution)/shard_map/ppermute | solution.py:938
  304.2 12.9 %collective-permute-start.22 = (bf16[2,96,1024]{2,1,0:T(8,128)(2,1)S(1)}, bf16[2,96,1024]{2,1,0:T(8,128)(2,1)S(1)}, u32[]{:S(2)}, u32[]{:S(2)}) collective-permute-start(bf16[2,96,1024]{2,1,0:T(8,128)(2,1)S(1)} %fusion.15), channel_id=1, source_target_pairs={{0,8},{4,12},{8,0},{12,4},{16,24},{20,28},{24,16},{28,20},{1,9},{5... | collective-permute-start | bytes 1179656 | tf_op jit(solution)/shard_map/ppermute | solution.py:938
  305.0 10.7 %collective-permute-start.23 = (bf16[4,96,384]{2,1,0:T(8,128)(2,1)S(1)}, bf16[4,96,384]{2,1,0:T(8,128)(2,1)S(1)}, u32[]{:S(2)}, u32[]{:S(2)}) collective-permute-start(bf16[4,96,384]{2,1,0:T(8,128)(2,1)S(1)} %dynamic-slice_bitcast_fusion.6), channel_id=1, source_target_pairs={{0,4},{4,0},{8,12},{12,8},{16,20},{20,16},{24,28},{28,24},{1,5},{5... | collective-permute-start | bytes 884744 | tf_op jit(solution)/shard_map/ppermute | solution.py:938
  305.9 9.9 %collective-permute-start.24 = (bf16[4,96,256]{2,1,0:T(8,128)(2,1)S(1)}, bf16[4,96,256]{2,1,0:T(8,128)(2,1)}, u32[]{:S(2)}, u32[]{:S(2)}) collective-permute-start(bf16[4,96,256]{2,1,0:T(8,128)(2,1)S(1)} %dynamic-slice_bitcast_fusion.9), channel_id=1, source_target_pairs={{0,2},{1,3},{2,0},{3,1},{4,6},{5,7},{6,4},{7,5},{8,10},{9,11},{10,... | collective-permute-start | bytes 589832 | tf_op jit(solution)/shard_map/ppermute | solution.py:938
  306.5 9.2 %collective-permute-start.20 = (bf16[64,768]{1,0:T(8,128)(2,1)S(1)}, bf16[64,768]{1,0:T(8,128)(2,1)}, u32[]{:S(2)}, u32[]{:S(2)}) collective-permute-start(bf16[64,768]{1,0:T(8,128)(2,1)S(1)} %pad_maximum_fusion.1.refs_0_), channel_id=1, source_target_pairs={{0,16},{4,20},{8,24},{12,28},{16,0},{20,4},{24,8},{28,12},{1,17},{... | collective-permute-start | bytes 294920 | tf_op jit(solution)/shard_map/ppermute | solution.py:938
  318.9 15.9 %collective-permute-start.25 = (bf16[96,640]{1,0:T(8,128)(2,1)S(1)}, bf16[96,640]{1,0:T(8,128)(2,1)S(1)}, u32[]{:S(2)}, u32[]{:S(2)}) collective-permute-start(bf16[96,640]{1,0:T(8,128)(2,1)S(1)} %get-tuple-element.207), channel_id=1, source_target_pairs={{0,8},{4,12},{8,0},{12,4},{16,24},{20,28},{24,16},{28,20},{1,9},{5... | collective-permute-start | bytes 368648 | tf_op jit(solution)/shard_map/ppermute | solution.py:938
  319.2 15.7 %collective-permute-start.26 = (bf16[96,640]{1,0:T(8,128)(2,1)S(1)}, bf16[96,640]{1,0:T(8,128)(2,1)S(1)}, u32[]{:S(2)}, u32[]{:S(2)}) collective-permute-start(bf16[96,640]{1,0:T(8,128)(2,1)S(1)} %get-tuple-element.208), channel_id=1, source_target_pairs={{0,16},{4,20},{8,24},{12,28},{16,0},{20,4},{24,8},{28,12},{1,17},{... | collective-permute-start | bytes 368648 | tf_op jit(solution)/shard_map/ppermute | solution.py:938
  322.0 12.9 %collective-permute-start.27 = (bf16[96,640]{1,0:T(8,128)(2,1)S(1)}, bf16[96,640]{1,0:T(8,128)(2,1)S(1)}, u32[]{:S(2)}, u32[]{:S(2)}) collective-permute-start(bf16[96,640]{1,0:T(8,128)(2,1)S(1)} %get-tuple-element.206), channel_id=1, source_target_pairs={{0,24},{4,28},{8,16},{12,20},{16,8},{20,12},{24,0},{28,4},{1,25},{... | collective-permute-start | bytes 368648 | tf_op jit(solution)/shard_map/ppermute | solution.py:938
  323.4 17.1 %collective-permute-start.30 = (bf16[96,1024]{1,0:T(8,128)(2,1)}, bf16[96,1024]{1,0:T(8,128)(2,1)S(1)}, u32[]{:S(2)}, u32[]{:S(2)}) collective-permute-start(bf16[96,1024]{1,0:T(8,128)(2,1)} %fusion.17), channel_id=1, source_target_pairs={{0,16},{4,20},{8,24},{12,28},{16,0},{20,4},{24,8},{28,12},{1,17},{... | collective-permute-start | bytes 589832 | tf_op jit(solution)/shard_map/ppermute | solution.py:938
  336.7 6.0 %collective-permute-start.28 = (bf16[2,96,1024]{2,1,0:T(8,128)(2,1)S(1)}, bf16[2,96,1024]{2,1,0:T(8,128)(2,1)S(1)}, u32[]{:S(2)}, u32[]{:S(2)}) collective-permute-start(bf16[2,96,1024]{2,1,0:T(8,128)(2,1)S(1)} %dynamic-slice_bitcast_fusion.2), channel_id=1, source_target_pairs={{0,1},{1,0},{2,3},{3,2},{4,5},{5,4},{6,7},{7,6},{8,9},{9,8},{10,11... | collective-permute-start | bytes 1179656 | tf_op jit(solution)/shard_map/ppermute | solution.py:938
  342.9 5.8 %collective-permute-start.29 = (bf16[96,1024]{1,0:T(8,128)(2,1)S(1)}, bf16[96,1024]{1,0:T(8,128)(2,1)S(1)}, u32[]{:S(2)}, u32[]{:S(2)}) collective-permute-start(bf16[96,1024]{1,0:T(8,128)(2,1)S(1)} %dynamic-slice_bitcast_fusion.8), channel_id=1, source_target_pairs={{0,2},{1,3},{2,0},{3,1},{4,6},{5,7},{6,4},{7,5},{8,10},{9,11},{10,... | collective-permute-start | bytes 589832 | tf_op jit(solution)/shard_map/ppermute | solution.py:938
  (34 other events, 123.9 us)

commit v6 on v5

--- a/solution.py
+++ b/solution.py
@@ -1173,9 +1173,10 @@
     qkv_a, qkv_b = (Sum.of_cores(qkv_sums[i], qkv_sums[2 + i]) for i in range(2))
     for one in (down, up_a, up_b):
         one.end()
-    gather.got = tied(gather.got, up_a.terms, up_b.terms, down.terms)
     gather.end()
     gather.begin(direct=False)
+    for one in (down, up_a, up_b):
+        one.terms = tied(one.terms, gather.got)
     sent = [gather.values, down.step_frames(), up_a.begin_frames(), up_b.begin("rows", 2, 0)]
     sent = meet(sent, qkv_a, qkv_b)
     qkv_a.end()

time: 352 us -> 354 us (level)
  waiting for transfers between devices: 11.1 us -> 15.1 us
    ppermute x31, waiting for transfers between devices: 11.1 us -> 15.1 us  [swap(): lax.ppermute(values, axis, [(i, i ^ distance) for i in range(lax.axis_siz...]
where the time goes in v6:
time: 354 us; the launch traced here: 353 us
  Pallas kernels  258 us (73%)
  starting transfers between devices  31.7 us (9%)
  other arithmetic  23.7 us (7%)
  local copies, waits for them, and re-layouts  23.4 us (7%)
  waiting for transfers between devices  15.1 us (4%)
    pallas_call x1, Pallas kernels, mlp(): pl.pallas_call(functools.partial(mlp_kernel, frame_len, 4), grid=(count /...  62.2 us
    pallas_call x1, Pallas kernels, attend_back(): pl.pallas_call(functools.partial(attend_back_kernel, frame_len), grid=(co...  52.7 us
    pallas_call x5, Pallas kernels, alias_call(): pl.pallas_call(body, grid=grid, in_specs=in_specs + [pl.BlockSpec(memory_...  47.5 us
    pallas_call x1, Pallas kernels, up_grad(): pl.pallas_call(weight_grad_kernel, grid_spec=pltpu.PrefetchScalarGridSpec...  31.8 us
    ppermute x31, starting transfers between devices, swap(): lax.ppermute(values, axis, [(i, i ^ distance) for i in range(lax.axis_siz...  31.7 us
    pallas_call x1, Pallas kernels, attend(): pl.pallas_call(functools.partial(attend_kernel, frame_len), grid=(count /...  20.9 us
    pallas_call x1, Pallas kernels, down_grad(): pl.pallas_call(down_grad_kernel, grid=(tiles // 2,), in_specs=[pl.BlockSp...  18.9 us
    ppermute x31, waiting for transfers between devices, swap(): lax.ppermute(values, axis, [(i, i ^ distance) for i in range(lax.axis_siz...  15.1 us
  transfers between devices with their start and end apart: 31, of which 6 were waited for; matrix products, arithmetic and copies ran while one was open for 7% of the time, Pallas kernels for 42%

profile of v6, /device:TPU:0, one launch (start us, length us, event | category | flops | bytes accessed | tf_op | source)
XLA Modules:
  0.0 353.0 jit_solution(4264641108850921793)
XLA Ops:
  2.5 3.0 collective-permute-start
  5.5 9.1 %project.2.refs_3_ = bf16[2800,2304]{1,0:T(8,128)(2,1)} custom-call(bf16[14,197,768]{2,1,0:T(8,128)(2,1)} %x_ref.3, f32[768]{0:T(1024)} %gain_ref.3, bf16[768,2304]{1,0:T(8,128)(2,1)} %w_ref.1), custom_call_target="tpu_custom_call" | custom-call | flops 42467328 | bytes 73728 | tf_op jit(solution)/shard_map/project/pallas_call | solution.py:100
  14.6 1.6 collective-permute-start.1
  16.2 2.6 collective-permute-start.2
  19.1 11.0 %project.3.proj_ref = bf16[2800,2304]{1,0:T(8,128)(2,1)} custom-call(bf16[14,197,768]{2,1,0:T(8,128)(2,1)} %x_ref.3, f32[768]{0:T(1024)} %gain_ref.3, bf16[768,2304]{1,0:T(8,128)(2,1)} %w_ref.1, bf16[2800,2304]{1,0:T(8,128)(2,1)} %project.2.refs_3_), custom_call_target="tpu_custom_call", output_to_operand_aliasing={{}: (3, {})} | custom-call | flops 56623104 | bytes 98304 | tf_op jit(solution)/shard_map/project/pallas_call | solution.py:100
  31.4 6.7 %message_forward.1 = (bf16[128,768]{1,0:T(8,128)(2,1)}, bf16[128,768]{1,0:T(8,128)(2,1)}, bf16[128,768]{1,0:T(8,128)(2,1)}, bf16[128,2304]{1,0:T(8,128)(2,1)}, b...) custom-call(bf16[32,896]{1,0:T(8,128)(2,1)} %copy-done.16, ...), custom_call_target="tpu_custom_call" | custom-call | flops 70000000 | bytes 90000 | tf_op jit(solution)/shard_map/message_forward/pallas_call | solution.py:751
  39.6 20.9 %attend.1 = (bf16[14,12,200,200]{3,2,1,0:T(8,128)(2,1)}, bf16[2800,768]{1,0:T(8,128)(2,1)}, f32[14,12,200]{2,1,0:T(8,128)}, bf16[2800,768]{1,0:T(8,128)(2,1)}) custom-call(bf16[14,197,768]{2,1,0:T(8,128)(2,1)} %x_ref.3, bf16[2800,2304]{1,0:T(8,128)(2,1)} %project.3.proj_ref, bf16[14,1,1536]{2,1,0:T(2,128)(2,1)} %copy.58.token_ref, bf16[768,768]{1,0:T(8,128)(2,1)} %out_w_ref.3), custom_call_target="tpu_custom_call" | custom-call | flops 250000000 | bytes 500000 | tf_op jit(solution)/shard_map/attend/pallas_call | solution.py:201
  60.5 62.2 %mlp.1 = (bf16[2800,768]{1,0:T(8,128)(2,1)}, bf16[2800,768]{1,0:T(8,128)(2,1)}, bf16[2800,3072]{1,0:T(8,128)(2,1)}, bf16[2800,3072]{1,0:T(8,128)(2,1)}, bf16[280...) custom-call(bf16[2800,768]{1,0:T(8,128)(2,1)} %get-tuple-element.177.res_ref.refs_0_, ...), custom_call_target="tpu_custom_call" | custom-call | flops 396361728 | bytes 600000 | tf_op jit(solution)/shard_map/mlp/pallas_call | solution.py:301
  122.7 18.9 %grad_down.1 = (bf16[2,8,192,384]{3,2,1,0:T(8,128)(2,1)}, bf16[2,8,192,384]{3,2,1,0:T(8,128)(2,1)}) custom-call(s32[1]{0:T(128)} %bitcast.5.core_ref, bf16[2800,768]{1,0:T(8,128)(2,1)} %get-tuple-element.124.left_ref, bf16[2800,3072]{1,0:T(8,128)(2,1)} %get-tuple-element.125.right_ref.refs_1_), custom_call_target="tpu_custom_call" | custom-call | flops 132120576 | bytes 215040 | tf_op jit(solution)/shard_map/grad_down/pallas_call | solution.py:432
  141.7 8.5 %grad_attn_out.1 = (bf16[2,768,1024]{2,1,0:T(8,128)(2,1)}, bf16[2,768,1024]{2,1,0:T(8,128)(2,1)}) custom-call(s32[1]{0:T(128)} %bitcast.5.core_ref, bf16[2800,768]{1,0:T(8,128)(2,1)} %get-tuple-element.127.mixed_ref.left_ref, bf16[2800,768]{1,0:T(8,128)(2,1)} %get-tuple-element.128.right_ref.branch_ref, f32[1,768]{1,0:T(1,128)} %get-tuple-element.129.gain_ref), custom_call_target="tpu_custom_call" | custom-call | flops 33030144 | bytes 86016 | tf_op jit(solution)/shard_map/grad_attn_out/pallas_call | solution.py:488
  151.5 1.6 collective-permute-start.5
  153.1 31.8 %grad_up.1 = (bf16[2,768,1024]{2,1,0:T(8,128)(2,1)}, bf16[2,768,1024]{2,1,0:T(8,128)(2,1)}) custom-call(s32[1]{0:T(128)} %bitcast.5.core_ref, bf16[2800,768]{1,0:T(8,128)(2,1)} %get-tuple-element.134.left_ref, bf16[2800,3072]{1,0:T(8,128)(2,1)} %get-tuple-element.135.right_ref, ...), custom_call_target="tpu_custom_call", output_to_operand_aliasing={{0}: (3, {}), {1}: (4, {})} | custom-call | flops 132120576 | bytes 215040 | tf_op jit(solution)/shard_map/grad_up/pallas_call | solution.py:385
  186.8 2.1 fusion.41
  188.8 8.3 %mlp_output.3.refs_3_ = bf16[14,197,768]{2,1,0:T(8,128)(2,1)} custom-call(bf16[2800,768]{1,0:T(8,128)(2,1)} %get-tuple-element.177.res_ref.refs_0_, bf16[2800,3072]{1,0:T(8,128)(2,1)} %get-tuple-element.125.right_ref.refs_1_, bf16[3072,768]{1,0:T(8,128)(2,1)} %refs_2_.9), custom_call_target="tpu_custom_call" | custom-call | flops 37748736 | bytes 49152 | tf_op jit(solution)/shard_map/mlp_output/pallas_call | solution.py:100
  197.1 2.0 fusion
  200.4 2.1 fusion.40
  211.2 52.7 %attend_back.1 = (bf16[14,197,768]{2,1,0:T(8,128)(2,1)}, f32[14,1,768]{2,1,0:T(1,128)}, bf16[14,1,768]{2,1,0:T(2,128)(2,1)}, bf16[2,768,384]{2,1,0:T(8,128)(2,1)...) custom-call(s32[1]{0:T(128)} %bitcast.5.core_ref, ...), custom_call_target="tpu_custom_call" | custom-call | flops 450000000 | bytes 500000 | tf_op jit(solution)/shard_map/attend_back/pallas_call | solution.py:621
  265.8 1.7 fusion.2
  267.5 1.8 fusion.1
  271.9 2.2 collective-permute-done.12
  282.0 10.7 %mlp_output.4.refs_3_ = bf16[14,197,768]{2,1,0:T(8,128)(2,1)} custom-call(bf16[2800,768]{1,0:T(8,128)(2,1)} %get-tuple-element.177.res_ref.refs_0_, bf16[2800,3072]{1,0:T(8,128)(2,1)} %get-tuple-element.125.right_ref.refs_1_, bf16[3072,768]{1,0:T(8,128)(2,1)} %refs_2_.9, bf16[14,197,768]{2,1,0:T(8,128)(2,1)} %mlp_output.3.refs_3_), custom_call_target="tpu_custom_call", output_to_operand_aliasing={{}: (3, {})} | custom-call | flops 56623104 | bytes 73728 | tf_op jit(solution)/shard_map/mlp_output/pallas_call | solution.py:100
  292.8 5.3 %collective-permute-done.18 = bf16[768,384]{1,0:T(8,128)(2,1)} collective-permute-done((bf16[768,384]{1,0:T(8,128)(2,1)}, bf16[768,384]{1,0:T(8,128)(2,1)}, u32[]{:S(2)}, u32[]{:S(2)}) %collective-permute-start.18) | collective-permute-done | bytes 589856 | tf_op jit(solution)/shard_map/ppermute | solution.py:938
  300.6 1.7 fusion.20
  302.3 2.4 collective-permute-start.21
  306.2 1.8 collective-permute-start.22
  309.4 8.3 %mlp_output.5 = bf16[14,197,768]{2,1,0:T(8,128)(2,1)} custom-call(bf16[2800,768]{1,0:T(8,128)(2,1)} %get-tuple-element.177.res_ref.refs_0_, bf16[2800,3072]{1,0:T(8,128)(2,1)} %get-tuple-element.125.right_ref.refs_1_, bf16[3072,768]{1,0:T(8,128)(2,1)} %refs_2_.9, bf16[14,197,768]{2,1,0:T(8,128)(2,1)} %mlp_output.4.refs_3_), custom_call_target="tpu_custom_call", output_to_operand_aliasing={{}: (3, {})} | custom-call | flops 37748736 | bytes 49152 | tf_op jit(solution)/shard_map/mlp_output/pallas_call | solution.py:100
  321.0 2.8 collective-permute-start.26
  326.5 1.8 fusion.19
  328.3 8.4 %message_back.1 = (f32[16,768]{1,0:T(8,128)}, bf16[4,96,1024]{2,1,0:T(8,128)(2,1)}) custom-call(s32[1]{0:T(128)} %bitcast.44.block_ref, bf16[64,768]{1,0:T(8,128)(2,1)} %copy-done.14, bf16[64,768]{1,0:T(8,128)(2,1)} %collective-permute-done.20.refs_1_, bf16[128,768]{1,0:T(8,128)(2,1)} %get-tuple-element.189.refs_2_, ...), custom_call_target="tpu_custom_call" | custom-call | flops 80000000 | bytes 90000 | tf_op jit(solution)/shard_map/message_back/pallas_call | solution.py:919
  338.7 3.7 %collective-permute-done.30 = bf16[96,1024]{1,0:T(8,128)(2,1)S(1)} collective-permute-done((bf16[96,1024]{1,0:T(8,128)(2,1)}, bf16[96,1024]{1,0:T(8,128)(2,1)S(1)}, u32[]{:S(2)}, u32[]{:S(2)}) %collective-permute-start.30) | collective-permute-done | bytes 196640 | tf_op jit(solution)/shard_map/ppermute | solution.py:938
  345.4 1.9 dynamic_update_slice.3
  348.0 2.5 collective-permute-done.29
  (178 shorter events, 49.2 us)
Async XLA Ops:
  2.5 12.1 %collective-permute-start = (bf16[16,896]{1,0:T(8,128)(2,1)S(1)}, bf16[16,896]{1,0:T(8,128)(2,1)S(1)}, u32[]{:S(2)}, u32[]{:S(2)}) collective-permute-start(bf16[16,896]{1,0:T(8,128)(2,1)S(1)} %pad_maximum_fusion.4), channel_id=1, source_target_pairs={{0,4},{4,0},{8,12},{12,8},{16,20},{20,16},{24,28},{28,24},{1,5},{5... | collective-permute-start | bytes 86024 | tf_op jit(solution)/shard_map/ppermute | solution.py:938
  14.6 15.5 %copy-start.16 = (bf16[32,896]{1,0:T(8,128)(2,1)}, bf16[32,896]{1,0:T(8,128)(2,1)S(1)}, u32[]{:S(2)}) copy-start(bf16[32,896]{1,0:T(8,128)(2,1)S(1)} %pad_maximum_fusion.2.refs_0_) | copy-start | bytes 172036
  14.6 15.5 %collective-permute-start.1 = (bf16[32,896]{1,0:T(8,128)(2,1)S(1)}, bf16[32,896]{1,0:T(8,128)(2,1)S(1)}, u32[]{:S(2)}, u32[]{:S(2)}) collective-permute-start(bf16[32,896]{1,0:T(8,128)(2,1)S(1)} %pad_maximum_fusion.2.refs_0_), channel_id=1, source_target_pairs={{0,8},{4,12},{8,0},{12,4},{16,24},{20,28},{24,16},{28,20},{1,9},{5... | collective-permute-start | bytes 172040 | tf_op jit(solution)/shard_map/ppermute | solution.py:938
  16.2 13.9 %collective-permute-start.2 = (bf16[32,896]{1,0:T(8,128)(2,1)S(1)}, bf16[32,896]{1,0:T(8,128)(2,1)S(1)}, u32[]{:S(2)}, u32[]{:S(2)}) collective-permute-start(bf16[32,896]{1,0:T(8,128)(2,1)S(1)} %pad_maximum_fusion.2.refs_0_), channel_id=1, source_target_pairs={{0,16},{4,20},{8,24},{12,28},{16,0},{20,4},{24,8},{28,12},{1,17},{... | collective-permute-start | bytes 172040 | tf_op jit(solution)/shard_map/ppermute | solution.py:938
  18.8 11.3 %collective-permute-start.3 = (bf16[32,896]{1,0:T(8,128)(2,1)S(1)}, bf16[32,896]{1,0:T(8,128)(2,1)S(1)}, u32[]{:S(2)}, u32[]{:S(2)}) collective-permute-start(bf16[32,896]{1,0:T(8,128)(2,1)S(1)} %pad_maximum_fusion.2.refs_0_), channel_id=1, source_target_pairs={{0,24},{4,28},{8,16},{12,20},{16,8},{20,12},{24,0},{28,4},{1,25},{... | collective-permute-start | bytes 172040 | tf_op jit(solution)/shard_map/ppermute | solution.py:938
  141.7 8.5 %collective-permute-start.4 = (bf16[2,8,192,384]{3,2,1,0:T(8,128)(2,1)}, bf16[2,8,192,384]{3,2,1,0:T(8,128)(2,1)}, u32[]{:S(2)}, u32[]{:S(2)}) collective-permute-start(bf16[2,8,192,384]{3,2,1,0:T(8,128)(2,1)} %get-tuple-element.126), channel_id=1, source_target_pairs={{0,1},{1,0},{2,3},{3,2},{4,5},{5,4},{6,7},{7,6},{8,9},{9,8},{10,11... | collective-permute-start | bytes 7077896 | tf_op jit(solution)/shard_map/ppermute | solution.py:938
  151.5 33.3 %collective-permute-start.5 = (bf16[6,192,384]{2,1,0:T(8,128)(2,1)S(1)}, bf16[6,192,384]{2,1,0:T(8,128)(2,1)}, u32[]{:S(2)}, u32[]{:S(2)}) collective-permute-start(bf16[6,192,384]{2,1,0:T(8,128)(2,1)S(1)} %fusion.5), channel_id=1, source_target_pairs={{0,2},{1,3},{2,0},{3,1},{4,6},{5,7},{6,4},{7,5},{8,10},{9,11},{10,... | collective-permute-start | bytes 2654216 | tf_op jit(solution)/shard_map/ppermute | solution.py:938
  184.9 14.3 %collective-permute-start.7 = (bf16[2,768,1024]{2,1,0:T(8,128)(2,1)}, bf16[2,768,1024]{2,1,0:T(8,128)(2,1)}, u32[]{:S(2)}, u32[]{:S(2)}) collective-permute-start(bf16[2,768,1024]{2,1,0:T(8,128)(2,1)} %get-tuple-element.141), channel_id=1, source_target_pairs={{0,1},{1,0},{2,3},{3,2},{4,5},{5,4},{6,7},{7,6},{8,9},{9,8},{10,11... | collective-permute-start | bytes 9437192 | tf_op jit(solution)/shard_map/ppermute | solution.py:938
  186.1 13.1 %collective-permute-start.6 = (bf16[2,192,384]{2,1,0:T(8,128)(2,1)S(1)}, bf16[2,192,384]{2,1,0:T(8,128)(2,1)S(1)}, u32[]{:S(2)}, u32[]{:S(2)}) collective-permute-start(bf16[2,192,384]{2,1,0:T(8,128)(2,1)S(1)} %fusion.18), channel_id=1, source_target_pairs={{0,2},{1,3},{2,0},{3,1},{4,6},{5,7},{6,4},{7,5},{8,10},{9,11},{10,... | collective-permute-start | bytes 884744 | tf_op jit(solution)/shard_map/ppermute | solution.py:938
  203.8 60.1 %collective-permute-start.9 = (bf16[768,512]{1,0:T(8,128)(2,1)}, bf16[768,512]{1,0:T(8,128)(2,1)}, u32[]{:S(2)}, u32[]{:S(2)}) collective-permute-start(bf16[768,512]{1,0:T(8,128)(2,1)} %fusion.6), channel_id=1, source_target_pairs={{0,2},{1,3},{2,0},{3,1},{4,6},{5,7},{6,4},{7,5},{8,10},{9,11},{10,... | collective-permute-start | bytes 2359304 | tf_op jit(solution)/shard_map/ppermute | solution.py:938
  206.4 57.5 %collective-permute-start.10 = (bf16[2,4,96,512]{3,2,1,0:T(8,128)(2,1)}, bf16[2,4,96,512]{3,2,1,0:T(8,128)(2,1)}, u32[]{:S(2)}, u32[]{:S(2)}) collective-permute-start(bf16[2,4,96,512]{3,2,1,0:T(8,128)(2,1)} %fusion.7), channel_id=1, source_target_pairs={{0,4},{4,0},{8,12},{12,8},{16,20},{20,16},{24,28},{28,24},{1,5},{5... | collective-permute-start | bytes 2359304 | tf_op jit(solution)/shard_map/ppermute | solution.py:938
  209.0 54.8 %collective-permute-start.8 = (bf16[4,192,384]{2,1,0:T(8,128)(2,1)}, bf16[4,192,384]{2,1,0:T(8,128)(2,1)}, u32[]{:S(2)}, u32[]{:S(2)}) collective-permute-start(bf16[4,192,384]{2,1,0:T(8,128)(2,1)} %dynamic-slice_bitcast_fusion.1), channel_id=1, source_target_pairs={{0,4},{4,0},{8,12},{12,8},{16,20},{20,16},{24,28},{28,24},{1,5},{5... | collective-permute-start | bytes 1769480 | tf_op jit(solution)/shard_map/ppermute | solution.py:938
  264.7 4.6 %collective-permute-start.11 = (bf16[16,768]{1,0:T(8,128)(2,1)S(1)}, bf16[16,768]{1,0:T(8,128)(2,1)S(1)}, u32[]{:S(2)}, u32[]{:S(2)}) collective-permute-start(bf16[16,768]{1,0:T(8,128)(2,1)S(1)} %pad.14), channel_id=1, source_target_pairs={{0,4},{4,0},{8,12},{12,8},{16,20},{20,16},{24,28},{28,24},{1,5},{5... | collective-permute-start | bytes 73736 | tf_op jit(solution)/shard_map/ppermute | solution.py:938
  265.3 11.7 %collective-permute-start.13 = (bf16[2,768,384]{2,1,0:T(8,128)(2,1)}, bf16[2,768,384]{2,1,0:T(8,128)(2,1)S(1)}, u32[]{:S(2)}, u32[]{:S(2)}) collective-permute-start(bf16[2,768,384]{2,1,0:T(8,128)(2,1)} %get-tuple-element.163), channel_id=1, source_target_pairs={{0,1},{1,0},{2,3},{3,2},{4,5},{5,4},{6,7},{7,6},{8,9},{9,8},{10,11... | collective-permute-start | bytes 3538952 | tf_op jit(solution)/shard_map/ppermute | solution.py:938
  265.3 11.7 %collective-permute-start.14 = (bf16[2,768,256]{2,1,0:T(8,128)(2,1)}, bf16[2,768,256]{2,1,0:T(8,128)(2,1)S(1)}, u32[]{:S(2)}, u32[]{:S(2)}) collective-permute-start(bf16[2,768,256]{2,1,0:T(8,128)(2,1)} %get-tuple-element.164), channel_id=1, source_target_pairs={{0,1},{1,0},{2,3},{3,2},{4,5},{5,4},{6,7},{7,6},{8,9},{9,8},{10,11... | collective-permute-start | bytes 2359304 | tf_op jit(solution)/shard_map/ppermute | solution.py:938
  270.0 4.1 %collective-permute-start.12 = (bf16[32,768]{1,0:T(8,128)(2,1)S(1)}, bf16[32,768]{1,0:T(8,128)(2,1)S(1)}, u32[]{:S(2)}, u32[]{:S(2)}) collective-permute-start(bf16[32,768]{1,0:T(8,128)(2,1)S(1)} %pad_maximum_fusion.3), channel_id=1, source_target_pairs={{0,8},{4,12},{8,0},{12,4},{16,24},{20,28},{24,16},{28,20},{1,9},{5... | collective-permute-start | bytes 147464 | tf_op jit(solution)/shard_map/ppermute | solution.py:938
  274.1 18.7 %collective-permute-start.16 = (bf16[4,96,512]{2,1,0:T(8,128)(2,1)S(1)}, bf16[4,96,512]{2,1,0:T(8,128)(2,1)}, u32[]{:S(2)}, u32[]{:S(2)}) collective-permute-start(bf16[4,96,512]{2,1,0:T(8,128)(2,1)S(1)} %dynamic-slice_bitcast_fusion.5), channel_id=1, source_target_pairs={{0,4},{4,0},{8,12},{12,8},{16,20},{20,16},{24,28},{28,24},{1,5},{5... | collective-permute-start | bytes 1179656 | tf_op jit(solution)/shard_map/ppermute | solution.py:938
  275.7 17.1 %collective-permute-start.17 = (bf16[4,96,512]{2,1,0:T(8,128)(2,1)S(1)}, bf16[4,96,512]{2,1,0:T(8,128)(2,1)}, u32[]{:S(2)}, u32[]{:S(2)}) collective-permute-start(bf16[4,96,512]{2,1,0:T(8,128)(2,1)S(1)} %dynamic-slice_bitcast_fusion.4), channel_id=1, source_target_pairs={{0,2},{1,3},{2,0},{3,1},{4,6},{5,7},{6,4},{7,5},{8,10},{9,11},{10,... | collective-permute-start | bytes 1179656 | tf_op jit(solution)/shard_map/ppermute | solution.py:938
  278.3 19.8 %collective-permute-start.18 = (bf16[768,384]{1,0:T(8,128)(2,1)}, bf16[768,384]{1,0:T(8,128)(2,1)}, u32[]{:S(2)}, u32[]{:S(2)}) collective-permute-start(bf16[768,384]{1,0:T(8,128)(2,1)} %dynamic-slice_bitcast_fusion), channel_id=1, source_target_pairs={{0,2},{1,3},{2,0},{3,1},{4,6},{5,7},{6,4},{7,5},{8,10},{9,11},{10,... | collective-permute-start | bytes 1769480 | tf_op jit(solution)/shard_map/ppermute | solution.py:938
  280.8 12.0 %collective-permute-start.19 = (bf16[2,4,96,256]{3,2,1,0:T(8,128)(2,1)}, bf16[2,4,96,256]{3,2,1,0:T(8,128)(2,1)}, u32[]{:S(2)}, u32[]{:S(2)}) collective-permute-start(bf16[2,4,96,256]{3,2,1,0:T(8,128)(2,1)} %dynamic-slice_bitcast_fusion.3), channel_id=1, source_target_pairs={{0,4},{4,0},{8,12},{12,8},{16,20},{20,16},{24,28},{28,24},{1,5},{5... | collective-permute-start | bytes 1179656 | tf_op jit(solution)/shard_map/ppermute | solution.py:938
  281.3 11.4 %collective-permute-start.15 = (bf16[2,192,384]{2,1,0:T(8,128)(2,1)}, bf16[2,192,384]{2,1,0:T(8,128)(2,1)}, u32[]{:S(2)}, u32[]{:S(2)}) collective-permute-start(bf16[2,192,384]{2,1,0:T(8,128)(2,1)} %dynamic-slice_bitcast_fusion.7), channel_id=1, source_target_pairs={{0,8},{4,12},{8,0},{12,4},{16,24},{20,28},{24,16},{28,20},{1,9},{5... | collective-permute-start | bytes 884744 | tf_op jit(solution)/shard_map/ppermute | solution.py:938
  302.3 15.4 %collective-permute-start.21 = (bf16[192,384]{1,0:T(8,128)(2,1)}, bf16[192,384]{1,0:T(8,128)(2,1)}, u32[]{:S(2)}, u32[]{:S(2)}) collective-permute-start(bf16[192,384]{1,0:T(8,128)(2,1)} %fusion.20), channel_id=1, source_target_pairs={{0,16},{4,20},{8,24},{12,28},{16,0},{20,4},{24,8},{28,12},{1,17},{... | collective-permute-start | bytes 442376 | tf_op jit(solution)/shard_map/ppermute | solution.py:938
  306.2 12.8 %collective-permute-start.22 = (bf16[2,96,1024]{2,1,0:T(8,128)(2,1)S(1)}, bf16[2,96,1024]{2,1,0:T(8,128)(2,1)S(1)}, u32[]{:S(2)}, u32[]{:S(2)}) collective-permute-start(bf16[2,96,1024]{2,1,0:T(8,128)(2,1)S(1)} %fusion.15), channel_id=1, source_target_pairs={{0,8},{4,12},{8,0},{12,4},{16,24},{20,28},{24,16},{28,20},{1,9},{5... | collective-permute-start | bytes 1179656 | tf_op jit(solution)/shard_map/ppermute | solution.py:938
  308.0 9.8 %collective-permute-start.23 = (bf16[4,96,384]{2,1,0:T(8,128)(2,1)S(1)}, bf16[4,96,384]{2,1,0:T(8,128)(2,1)S(1)}, u32[]{:S(2)}, u32[]{:S(2)}) collective-permute-start(bf16[4,96,384]{2,1,0:T(8,128)(2,1)S(1)} %dynamic-slice_bitcast_fusion.6), channel_id=1, source_target_pairs={{0,4},{4,0},{8,12},{12,8},{16,20},{20,16},{24,28},{28,24},{1,5},{5... | collective-permute-start | bytes 884744 | tf_op jit(solution)/shard_map/ppermute | solution.py:938
  308.6 9.2 %collective-permute-start.24 = (bf16[4,96,256]{2,1,0:T(8,128)(2,1)S(1)}, bf16[4,96,256]{2,1,0:T(8,128)(2,1)}, u32[]{:S(2)}, u32[]{:S(2)}) collective-permute-start(bf16[4,96,256]{2,1,0:T(8,128)(2,1)S(1)} %dynamic-slice_bitcast_fusion.9), channel_id=1, source_target_pairs={{0,2},{1,3},{2,0},{3,1},{4,6},{5,7},{6,4},{7,5},{8,10},{9,11},{10,... | collective-permute-start | bytes 589832 | tf_op jit(solution)/shard_map/ppermute | solution.py:938
  309.3 8.5 %collective-permute-start.20 = (bf16[64,768]{1,0:T(8,128)(2,1)S(1)}, bf16[64,768]{1,0:T(8,128)(2,1)}, u32[]{:S(2)}, u32[]{:S(2)}) collective-permute-start(bf16[64,768]{1,0:T(8,128)(2,1)S(1)} %pad_maximum_fusion.1.refs_0_), channel_id=1, source_target_pairs={{0,16},{4,20},{8,24},{12,28},{16,0},{20,4},{24,8},{28,12},{1,17},{... | collective-permute-start | bytes 294920 | tf_op jit(solution)/shard_map/ppermute | solution.py:938
  320.9 15.8 %collective-permute-start.25 = (bf16[96,640]{1,0:T(8,128)(2,1)S(1)}, bf16[96,640]{1,0:T(8,128)(2,1)S(1)}, u32[]{:S(2)}, u32[]{:S(2)}) collective-permute-start(bf16[96,640]{1,0:T(8,128)(2,1)S(1)} %get-tuple-element.211), channel_id=1, source_target_pairs={{0,8},{4,12},{8,0},{12,4},{16,24},{20,28},{24,16},{28,20},{1,9},{5... | collective-permute-start | bytes 368648 | tf_op jit(solution)/shard_map/ppermute | solution.py:938
  321.0 15.8 %collective-permute-start.26 = (bf16[96,640]{1,0:T(8,128)(2,1)S(1)}, bf16[96,640]{1,0:T(8,128)(2,1)S(1)}, u32[]{:S(2)}, u32[]{:S(2)}) collective-permute-start(bf16[96,640]{1,0:T(8,128)(2,1)S(1)} %get-tuple-element.212), channel_id=1, source_target_pairs={{0,16},{4,20},{8,24},{12,28},{16,0},{20,4},{24,8},{28,12},{1,17},{... | collective-permute-start | bytes 368648 | tf_op jit(solution)/shard_map/ppermute | solution.py:938
  323.8 13.0 %collective-permute-start.27 = (bf16[96,640]{1,0:T(8,128)(2,1)S(1)}, bf16[96,640]{1,0:T(8,128)(2,1)S(1)}, u32[]{:S(2)}, u32[]{:S(2)}) collective-permute-start(bf16[96,640]{1,0:T(8,128)(2,1)S(1)} %get-tuple-element.210), channel_id=1, source_target_pairs={{0,24},{4,28},{8,16},{12,20},{16,8},{20,12},{24,0},{28,4},{1,25},{... | collective-permute-start | bytes 368648 | tf_op jit(solution)/shard_map/ppermute | solution.py:938
  325.3 17.1 %collective-permute-start.30 = (bf16[96,1024]{1,0:T(8,128)(2,1)}, bf16[96,1024]{1,0:T(8,128)(2,1)S(1)}, u32[]{:S(2)}, u32[]{:S(2)}) collective-permute-start(bf16[96,1024]{1,0:T(8,128)(2,1)} %fusion.17), channel_id=1, source_target_pairs={{0,16},{4,20},{8,24},{12,28},{16,0},{20,4},{24,8},{28,12},{1,17},{... | collective-permute-start | bytes 589832 | tf_op jit(solution)/shard_map/ppermute | solution.py:938
  338.6 6.0 %collective-permute-start.28 = (bf16[2,96,1024]{2,1,0:T(8,128)(2,1)S(1)}, bf16[2,96,1024]{2,1,0:T(8,128)(2,1)S(1)}, u32[]{:S(2)}, u32[]{:S(2)}) collective-permute-start(bf16[2,96,1024]{2,1,0:T(8,128)(2,1)S(1)} %dynamic-slice_bitcast_fusion.2), channel_id=1, source_target_pairs={{0,1},{1,0},{2,3},{3,2},{4,5},{5,4},{6,7},{7,6},{8,9},{9,8},{10,11... | collective-permute-start | bytes 1179656 | tf_op jit(solution)/shard_map/ppermute | solution.py:938
  344.8 5.8 %collective-permute-start.29 = (bf16[96,1024]{1,0:T(8,128)(2,1)S(1)}, bf16[96,1024]{1,0:T(8,128)(2,1)S(1)}, u32[]{:S(2)}, u32[]{:S(2)}) collective-permute-start(bf16[96,1024]{1,0:T(8,128)(2,1)S(1)} %dynamic-slice_bitcast_fusion.8), channel_id=1, source_target_pairs={{0,2},{1,3},{2,0},{3,1},{4,6},{5,7},{6,4},{7,5},{8,10},{9,11},{10,... | collective-permute-start | bytes 589832 | tf_op jit(solution)/shard_map/ppermute | solution.py:938
  (34 other events, 137.2 us)
